TPU v7x, 32 devices: a whole 2x2x4 slice. The times are simulated.
32 devices in a mesh: group: 4 (over z), member: 8 (over y, x, core).
Axes of the slice: x: 2, y: 2, z: 4, core: 2. Of those that a mesh axis runs over, the one named last changes fastest.
Arguments:
- source: bfloat16 [32768, 256], P(('group', 'member')), may hold values from -6 to 6
- target: bfloat16 [8192, 256], P(('group', 'member')), may hold values from -6 to 6
- pair_source: int32 [32, 32], P(('group', 'member')), may hold values from 0 to 3, as said below
- pair_target: int32 [32, 32], P(('group', 'member')), may hold values from 0 to 15, as said below
- pair_count: int32 [32], P(('group', 'member')), may hold values from 4 to 32, as said below
Outputs:
- log_source: float32 [32768], P(('group', 'member'))
- log_target: float32 [8192], P(('group', 'member'))
Inputs may be any that keep to these rules, and one draw needn't show every extreme that they name: `pair_source`: each entry is the device's own source tile, 0 to 3; slots 0 to 3 name each of them once, and no (source tile, window tile) pair stands twice on one device. `pair_target`: window index of the pair's target tile; on every device slot 0 names the device's own target tile (index equal to its member index). `pair_count`: at least 4; in every group one device has exactly 32.
All inputs are finite; a program needn't handle non-finite values.
Results may differ from a plain program's by a relative error of at most 0.0031.
Values may be sent and summed in bfloat16 or wider, within the bound.
No kernel may reach another device: no remote copies, remote signals or barrier semaphores. Data moves between devices by JAX's collectives and lax.ppermute only.
A program may use at most 128 MiB of HBM per device.

v0:
```python
import functools
import math

import jax
import jax.numpy as jnp
from jax import lax
from jax.experimental import pallas as pl
from jax.experimental.pallas import tpu as pltpu
from jax.sharding import PartitionSpec as P


ITERS = 2
REGULARIZER = 0.05
EPSILON = 1e-06
CORES = 2
LANES = 128
MIB = 2**20


BOTH = ("group", "member")
VM = pl.BlockSpec(memory_space=pltpu.VMEM)
SM = pl.BlockSpec(memory_space=pltpu.SMEM)
HB = pl.BlockSpec(memory_space=pltpu.HBM)
F32 = jnp.float32
BF16 = jnp.bfloat16
FACTOR = math.log2(math.e) / REGULARIZER


def odd(bits):
    return bin(bits).count("1") % 2


def odd_traced(value, width):
    result = jnp.int32(0)
    for b in range(width):
        result = result ^ (value >> b)
    return result & 1


def hop(x, up, bits):
    groups, members = lax.axis_size("group"), lax.axis_size("member")
    turn = odd(bits) ^ ((up & 1) if groups % 2 == 0 else 0)
    mask = CORES * bits + turn
    return lax.ppermute(
        x,
        BOTH,
        [
            (g * members + m, (g - up) % groups * members + (m ^ mask))
            for g in range(groups)
            for m in range(members)
        ],
    )


def partner(x):
    size = lax.axis_size("member")
    return lax.ppermute(x, "member", [(i, i ^ 1) for i in range(size)])


def spread_tiles(start, chips):
    half = start.shape[0] // 2
    tiles = {0: [start]}

    def part(k, which):
        blocks = tiles[k]
        return blocks[which] if len(blocks) == 2 else blocks[0][which * half : (which + 1) * half]

    for k in sorted(range(1, chips), key=lambda k: (bin(k).count("1"), k)):
        low, high = k & -k, 1 << (k.bit_length() - 1)
        if low == high:
            tiles[k] = [hop(start, 0, k)]
        else:
            upper = hop(part(k ^ high, 0), 0, high)
            tiles[k] = [upper, hop(part(k ^ low, 1), 0, low)]
    return [tiles[k] for k in range(chips)]


def unit(values):
    floats = values.astype(F32)
    return (floats / jnp.sqrt(jnp.sum(floats * floats, axis=1, keepdims=True) + EPSILON)).astype(
        BF16
    )


def rows_out(acc, out):
    tiles, cells, lanes = acc.shape
    lane = lax.broadcasted_iota(jnp.int32, (cells, lanes), 1)
    table = jnp.zeros((cells, lanes), F32)
    for s in range(tiles):
        table = jnp.where(lane == s, jnp.sum(acc[s], axis=1, keepdims=True), table)
    out[...] = jnp.transpose(table)[:tiles]


def add_halves(acc, s, values):
    total = values[:, :LANES]
    for j in range(1, values.shape[1] // LANES):
        total = total + values[:, j * LANES : (j + 1) * LANES]
    acc[s] += total


def prepare_kernel(
    chips, slots, even, own, target, other, mine, theirs, units, home, first, second, raw, tile, done
):
    cells = units.shape[1]
    tiles = own.shape[0] // cells
    fetch = pltpu.make_async_copy(own, raw, done.at[0])
    fetch_home = pltpu.make_async_copy(target, tile, done.at[1])
    fetch.start()
    fetch_home.start()
    members = CORES * chips
    width = members.bit_length()
    member = lax.axis_index("member")
    chip = member // CORES
    kind = odd_traced(member, width)
    counts = (jnp.int32(0), jnp.int32(0))
    for half, info in enumerate((mine, theirs)):

        def slot(k, counts, half=half, info=info):
            early, late = counts
            label = info[0, slots + k]
            w = label // CORES
            beyond = (label >= members).astype(jnp.int32)
            place = lax.rem(label, members)
            here = (odd_traced(place, width) ^ (beyond & even)) == kind
            is_late = jnp.logical_and(beyond == 1, place // CORES != chip)
            s = half * tiles + info[0, k]
            to_early = jnp.logical_and(here, jnp.logical_not(is_late))
            to_late = jnp.logical_and(here, is_late)

            @pl.when(to_early)
            def _():
                first[1 + 2 * early] = s
                first[2 + 2 * early] = w

            @pl.when(to_late)
            def _():
                second[1 + 2 * late] = s
                second[2 + 2 * late] = w

            return early + to_early.astype(jnp.int32), late + to_late.astype(jnp.int32)

        counts = lax.fori_loop(0, info[0, 2 * slots], slot, counts)
    first[0], second[0] = counts
    for s in range(tiles):
        units[tiles + s] = unit(other[s * cells : (s + 1) * cells])
    fetch.wait()
    for s in range(tiles):
        units[s] = unit(raw[s * cells : (s + 1) * cells])
    fetch_home.wait()
    home[...] = unit(tile[...])


def place(window, at, blocks):
    row = 0
    for block in blocks:
        rows = block.shape[0]
        window[at, row : row + rows] = unit(block[...])
        row += rows


def build_pairs(units, window, table, factors, acc, where):
    def pair(n, carry):
        s, w = table[1 + 2 * n], table[2 + 2 * n]
        logits = lax.dot_general(
            units[s], window[where(w)], (((1,), (1,)), ((), ())), preferred_element_type=F32
        )
        values = jnp.exp2(logits * FACTOR)
        factors[n] = values.astype(BF16)
        add_halves(acc, s, values)
        return carry

    lax.fori_loop(0, table[0], pair, 0)


def first_kernel(chips, shape, units, table, home, *refs):
    count = sum(shape)
    tiles = refs[:count]
    factors, acc, window = refs[count:]
    chip = lax.axis_index("member") // CORES
    window[chip] = home[...]
    at = 0
    for k, blocks in enumerate(shape):
        slot = chip ^ (k + 1) if k + 1 < chips else chips
        place(window, slot, tiles[at : at + blocks])
        at += blocks
    acc[...] = jnp.zeros_like(acc)
    build_pairs(units, window, table, factors, acc, lambda w: jnp.minimum(w, chips))


def second_kernel(chips, shape, units, table, before, *refs):
    count = sum(shape)
    tiles = refs[:count]
    factors, rows, acc, window = refs[count:]
    chip = lax.axis_index("member") // CORES
    at = 0
    for k, blocks in enumerate(shape):
        place(window, chip ^ (k + 1), tiles[at : at + blocks])
        at += blocks
    acc[...] = before[...]
    build_pairs(units, window, table, factors, acc, lambda w: w - chips)
    rows_out(acc, rows)


def row_kernel(first, second, lists_first, lists_second, columns, before, after, rows, scale, acc):
    chips = before.shape[0]
    tiles = acc.shape[0] // CORES
    scale[:chips] = float(tiles) / (columns[:chips] + before[...])
    scale[chips:] = float(tiles) / (columns[chips:] + after[...])
    acc[...] = jnp.zeros_like(acc)
    for factors, table in ((first, lists_first), (second, lists_second)):

        def pair(n, carry, factors=factors, table=table):
            s, w = table[1 + 2 * n], table[2 + 2 * n]
            add_halves(acc, s, factors[n].astype(F32) * scale[pl.ds(w, 1), :])
            return carry

        lax.fori_loop(0, table[0], pair, 0)
    rows_out(acc, rows)


def column_kernel(last, first, second, lists_first, lists_second, rows, arrived, columns, *rest):
    if last:
        logs, spread, acc = rest
    else:
        spread, acc = rest
    tiles = rows.shape[0] // CORES
    cells = first.shape[1]
    total = rows[...] + jnp.concatenate([arrived[tiles:], arrived[:tiles]], 0)
    scale = 1.0 / total
    if last:
        logs[...] = jnp.log(scale[:tiles] * float(cells))
    flipped = jnp.transpose(scale)
    for s in range(CORES * tiles):
        spread[s] = jnp.broadcast_to(flipped[:, s : s + 1], (cells, LANES))
    acc[...] = jnp.zeros_like(acc)
    for factors, table in ((first, lists_first), (second, lists_second)):

        def pair(n, carry, factors=factors, table=table):
            s, w = table[1 + 2 * n], table[2 + 2 * n]
            values = factors[n].astype(F32)
            for j in range(cells // LANES):
                part = values[:, j * LANES : (j + 1) * LANES] * spread[s]
                acc[w, :, j * LANES : (j + 1) * LANES] += jnp.sum(
                    part.reshape(cells // 8, 8, LANES), axis=0
                )
            return carry

        lax.fori_loop(0, table[0], pair, 0)
    columns[...] = jnp.sum(acc[...], axis=1)


def step(source, target, pair_source, pair_target, pair_count):
    groups, members = lax.axis_size("group"), lax.axis_size("member")
    chips = members // CORES
    cells, width = target.shape
    tiles = source.shape[0] // cells
    both = CORES * tiles
    slots = pair_source.shape[1]
    even = 1 if groups % 2 == 0 else 0
    most_first = min(CORES * slots, both * (chips + 1))
    most_second = min(CORES * slots, both * (chips - 1))

    beyond = hop(target, 1, 0)
    own_tiles = spread_tiles(target, chips)
    next_tiles = spread_tiles(beyond, chips)
    info = jnp.concatenate([pair_source, pair_target, pair_count[:, None]], 1)
    partner_source = partner(source)
    partner_info = partner(info)

    def shaped(*dims, kind=F32):
        return jax.ShapeDtypeStruct(dims, kind)

    def limit(size):
        return pltpu.CompilerParams(vmem_limit_bytes=int(size))

    def cost(pairs):
        return pl.CostEstimate(
            flops=2 * pairs * cells * cells * width,
            transcendentals=pairs * cells * cells,
            bytes_accessed=pairs * cells * cells * 2,
        )

    tile = cells * width * 2
    lanes_acc = (both, cells, LANES)
    prepare = pl.pallas_call(
        functools.partial(prepare_kernel, chips, slots, even),
        out_shape=(
            shaped(both, cells, width, kind=BF16),
            shaped(cells, width, kind=BF16),
            shaped(1 + 2 * most_first, kind=jnp.int32),
            shaped(1 + 2 * most_second, kind=jnp.int32),
        ),
        in_specs=[HB, HB, VM, SM, SM],
        out_specs=(VM, VM, SM, SM),
        scratch_shapes=[
            pltpu.VMEM(source.shape, BF16),
            pltpu.VMEM(target.shape, BF16),
            pltpu.SemaphoreType.DMA((2,)),
        ],
        compiler_params=limit(4 * MIB),
        cost_estimate=cost(both),
        name="prepare",
    )
    units, home, lists_first, lists_second = prepare(
        source, target, partner_source, info, partner_info
    )

    early = own_tiles[1:] + [next_tiles[0]]
    late = next_tiles[1:]
    first_call = pl.pallas_call(
        functools.partial(first_kernel, chips, [len(t) for t in early]),
        out_shape=(shaped(most_first, cells, cells, kind=BF16), shaped(*lanes_acc)),
        in_specs=[VM, SM, VM] + [VM] * sum(len(t) for t in early),
        out_specs=(VM, VM),
        scratch_shapes=[pltpu.VMEM((chips + 1, cells, width), BF16)],
        compiler_params=limit((most_first + 2 * chips + 2 + both) * tile + 5 * MIB),
        cost_estimate=cost(most_first),
        name="first",
    )
    first, acc = first_call(units, lists_first, home, *[b for t in early for b in t])
    second, rows = pl.pallas_call(
        functools.partial(second_kernel, chips, [len(t) for t in late]),
        out_shape=(shaped(most_second, cells, cells, kind=BF16), shaped(both, cells)),
        in_specs=[VM, SM, VM] + [VM] * sum(len(t) for t in late),
        out_specs=(VM, VM),
        scratch_shapes=[pltpu.VMEM(lanes_acc, F32), pltpu.VMEM((chips, cells, width), BF16)],
        compiler_params=limit((most_second + 2 * chips + both) * tile + 5 * MIB),
        cost_estimate=cost(most_second),
        name="second",
    )(units, lists_second, acc, *[b for t in late for b in t])
    held = (first, second, lists_first, lists_second)
    held_limit = limit((most_first + most_second) * tile + 4 * MIB)

    for sweep in range(ITERS):
        last = sweep + 1 == ITERS
        if sweep > 0:
            rows = pl.pallas_call(
                row_kernel,
                out_shape=shaped(both, cells),
                in_specs=[VM, VM, SM, SM, VM, VM, VM],
                out_specs=VM,
                scratch_shapes=[pltpu.VMEM((2 * chips, cells), F32), pltpu.VMEM(lanes_acc, F32)],
                compiler_params=held_limit,
                name="rows",
            )(*held, columns, before, after)
        found = pl.pallas_call(
            functools.partial(column_kernel, last),
            out_shape=(shaped(2 * chips, cells),) + ((shaped(tiles, cells),) if last else ()),
            in_specs=[VM, VM, SM, SM, VM, VM],
            out_specs=(VM,) + ((VM,) if last else ()),
            scratch_shapes=[
                pltpu.VMEM(lanes_acc, F32),
                pltpu.VMEM((2 * chips, 8, cells), F32),
            ],
            compiler_params=held_limit,
            name="columns",
        )(*held, rows, partner(rows))
        columns = found[0]
        bits = [1 << b for b in range(chips.bit_length() - 1)]
        if not last:
            for bit in bits:
                columns = columns + hop(columns, 0, bit)
            before = hop(columns[chips:], -1, 0)
            after = hop(columns[:chips], 1, 0)
        else:
            chip = lax.axis_index("member") // CORES
            for bit in bits[:-1]:
                columns = columns + hop(columns, 0, bit)
            far = bits[-1]

            def row(index):
                return lax.dynamic_slice_in_dim(columns, index, 1, 0)

            own = row(chip)
            own = own + hop(row(chip ^ far), 0, far)
            own = own + hop(row(chips + chip), -1, 0)
            own = own + hop(row(chips + (chip ^ far)), -1, far)
    return (
        found[1].reshape(tiles * cells),
        jnp.log(float(tiles) / own).reshape(cells),
    )


def solution(mesh):
    placed = (
        P(BOTH, None),
        P(BOTH, None),
        P(BOTH, None),
        P(BOTH, None),
        P(BOTH),
    )
    return jax.shard_map(
        step,
        mesh=mesh,
        in_specs=placed,
        out_specs=(P(BOTH), P(BOTH)),
        check_vma=False,
    )
```

profile of v0, /device:TPU:0, one launch (start us, length us, event | category | flops | bytes accessed | tf_op | source)
XLA Modules:
  0.0 59.5 jit_solution(17275939964881327637)
XLA Ops:
  1.2 4.7 %collective-permute-start.6 = (bf16[256,256]{1,0:T(8,128)(2,1)}, bf16[256,256]{1,0:T(8,128)(2,1)S(1)}, u32[]{:S(2)}, u32[]{:S(2)}) collective-permute-start(bf16[256,256]{1,0:T(8,128)(2,1)} %target.1), channel_id=1, source_target_pairs={{0,25},{1,24},{2,27},{3,26},{4,29},{5,28},{6,31},{7,30},{8,1},{9,0... | collective-permute-start | bytes 393224 | tf_op jit(solution)/shard_map/ppermute | solution.py:44
  5.9 1.2 %collective-permute-start.2 = (bf16[256,256]{1,0:T(8,128)(2,1)}, bf16[256,256]{1,0:T(8,128)(2,1)S(1)}, u32[]{:S(2)}, u32[]{:S(2)}) collective-permute-start(bf16[256,256]{1,0:T(8,128)(2,1)} %target.1), channel_id=1, source_target_pairs={{0,3},{1,2},{2,1},{3,0},{4,7},{5,6},{6,5},{7,4},{8,11},{9,10},{10,... | collective-permute-start | bytes 393224 | tf_op jit(solution)/shard_map/ppermute | solution.py:44
  7.1 1.6 %collective-permute-start.3 = (bf16[256,256]{1,0:T(8,128)(2,1)}, bf16[256,256]{1,0:T(8,128)(2,1)S(1)}, u32[]{:S(2)}, u32[]{:S(2)}) collective-permute-start(bf16[256,256]{1,0:T(8,128)(2,1)} %target.1), channel_id=1, source_target_pairs={{0,5},{1,4},{2,7},{3,6},{4,1},{5,0},{6,3},{7,2},{8,13},{9,12},{10,... | collective-permute-start | bytes 393224 | tf_op jit(solution)/shard_map/ppermute | solution.py:44
  8.6 0.9 %collective-permute-done.6.refs_4_ = bf16[256,256]{1,0:T(8,128)(2,1)S(1)} collective-permute-done((bf16[256,256]{1,0:T(8,128)(2,1)}, bf16[256,256]{1,0:T(8,128)(2,1)S(1)}, u32[]{:S(2)}, u32[]{:S(2)}) %collective-permute-start.6) | collective-permute-done | bytes 131104 | tf_op jit(solution)/shard_map/ppermute | solution.py:44
  9.5 0.6 collective-permute-start.7
  10.1 2.1 %collective-permute-start.8 = (bf16[256,256]{1,0:T(8,128)(2,1)S(1)}, bf16[256,256]{1,0:T(8,128)(2,1)S(1)}, u32[]{:S(2)}, u32[]{:S(2)}) collective-permute-start(bf16[256,256]{1,0:T(8,128)(2,1)S(1)} %collective-permute-done.6.refs_4_), channel_id=1, source_target_pairs={{0,5},{1,4},{2,7},{3,6},{4,1},{5,0},{6,3},{7,2},{8,13},{9,12},{10,... | collective-permute-start | bytes 393224 | tf_op jit(solution)/shard_map/ppermute | solution.py:44
  13.2 1.3 %collective-permute-start.5 = (bf16[128,256]{1,0:T(8,128)(2,1)S(1)}, bf16[128,256]{1,0:T(8,128)(2,1)S(1)}, u32[]{:S(2)}, u32[]{:S(2)}) collective-permute-start(bf16[128,256]{1,0:T(8,128)(2,1)S(1)} %slice.25), channel_id=1, source_target_pairs={{0,3},{1,2},{2,1},{3,0},{4,7},{5,6},{6,5},{7,4},{8,11},{9,10},{10,... | collective-permute-start | bytes 196616 | tf_op jit(solution)/shard_map/ppermute | solution.py:44
  14.5 0.7 %pad_add_fusion.mine = s32[1,65]{1,0:T(1,128)S(1)} fusion(s32[1,1]{1,0:T(1,128)} %bitcast.4, s32[1,32]{1,0:T(1,128)} %param.8, s32[1,32]{1,0:T(1,128)} %param.7), kind=kLoop, calls=%fused_computation.4 | loop fusion | flops 130 | bytes 520 | tf_op jit(solution)/shard_map/concatenate | solution.py:266
  15.6 2.0 %collective-permute-start.9 = (bf16[128,256]{1,0:T(8,128)(2,1)S(1)}, bf16[128,256]{1,0:T(8,128)(2,1)S(1)}, u32[]{:S(2)}, u32[]{:S(2)}) collective-permute-start(bf16[128,256]{1,0:T(8,128)(2,1)S(1)} %slice.26), channel_id=1, source_target_pairs={{0,5},{1,4},{2,7},{3,6},{4,1},{5,0},{6,3},{7,2},{8,13},{9,12},{10,... | collective-permute-start | bytes 196616 | tf_op jit(solution)/shard_map/ppermute | solution.py:44
  17.8 1.0 %copy-done = bf16[1024,256]{1,0:T(8,128)(2,1)S(1)} copy-done((bf16[1024,256]{1,0:T(8,128)(2,1)S(1)}, bf16[1024,256]{1,0:T(8,128)(2,1)}, u32[]{:S(2)}) %copy-start) | copy-done | bytes 524312
  18.9 0.9 %copy-done.1 = bf16[256,256]{1,0:T(8,128)(2,1)S(1)} copy-done((bf16[256,256]{1,0:T(8,128)(2,1)S(1)}, bf16[256,256]{1,0:T(8,128)(2,1)}, u32[]{:S(2)}) %copy-start.1) | copy-done | bytes 131096
  19.8 2.7 %prepare.1 = (bf16[8,256,256]{2,1,0:T(8,128)(2,1)S(1)}, bf16[256,256]{1,0:T(8,128)(2,1)S(1)}, s32[81]{0:T(128)S(1)}, s32[49]{0:T(128)S(1)}) custom-call(bf16[1024,256]{1,0:T(8,128)(2,1)S(1)} %copy-done, bf16[256,256]{1,0:T(8,128)(2,1)S(1)} %copy-done.1, bf16[1024,256]{1,0:T(8,128)(2,1)S(1)} %collective-permute-done.other, s32[1,65]{1,0:T(1,128)S(1)} %pad_add_fusion.mine, ...), custom_call_target="tpu_custom_call" | custom-call | flops 268435456 | bytes 1048576 | tf_op jit(solution)/shard_map/prepare/pallas_call | solution.py:304
  22.5 3.5 %first.1 = (bf16[40,256,256]{2,1,0:T(8,128)(2,1)S(1)}, f32[8,256,128]{2,1,0:T(8,128)S(1)}) custom-call(bf16[8,256,256]{2,1,0:T(8,128)(2,1)S(1)} %get-tuple-element.12.units, s32[81]{0:T(128)S(1)} %get-tuple-element.13.table.lists_first, bf16[256,256]{1,0:T(8,128)(2,1)S(1)} %get-tuple-element.14.home, bf16[256,256]{1,0:T(8,128)(2,1)S(1)} %collective-permute-done.2.refs_0_, ...), custom_call_target="tpu_custom_call" | custom-call | flops 1342177280 | bytes 5242880 | tf_op jit(solution)/shard_map/first/pallas_call | solution.py:320
  26.0 1.7 %second.1 = (bf16[24,256,256]{2,1,0:T(8,128)(2,1)S(1)}, f32[8,256]{1,0:T(8,128)S(1)}) custom-call(bf16[8,256,256]{2,1,0:T(8,128)(2,1)S(1)} %get-tuple-element.12.units, s32[49]{0:T(128)S(1)} %get-tuple-element.16.table.lists_second, f32[8,256,128]{2,1,0:T(8,128)S(1)} %get-tuple-element.17.before, bf16[256,256]{1,0:T(8,128)(2,1)S(1)} %collective-permute-done.7.refs_0_, ...), custom_call_target="tpu_custom_call" | custom-call | flops 805306368 | bytes 3145728 | tf_op jit(solution)/shard_map/second/pallas_call | solution.py:321
  27.7 1.5 %collective-permute-start.11 = (f32[8,256]{1,0:T(8,128)S(1)}, f32[8,256]{1,0:T(8,128)S(1)}, u32[]{:S(2)}, u32[]{:S(2)}) collective-permute-start(f32[8,256]{1,0:T(8,128)S(1)} %get-tuple-element.19.rows), channel_id=1, source_target_pairs={{0,1},{1,0},{2,3},{3,2},{4,5},{5,4},{6,7},{7,6},{8,9},{9,8},{10,11... | collective-permute-start | bytes 24584 | tf_op jit(solution)/shard_map/ppermute | solution.py:57
  29.2 0.8 %collective-permute-done.11.arrived = f32[8,256]{1,0:T(8,128)S(1)} collective-permute-done((f32[8,256]{1,0:T(8,128)S(1)}, f32[8,256]{1,0:T(8,128)S(1)}, u32[]{:S(2)}, u32[]{:S(2)}) %collective-permute-start.11) | collective-permute-done | bytes 8224 | tf_op jit(solution)/shard_map/ppermute | solution.py:57
  30.0 1.7 %columns.2 = f32[8,256]{1,0:T(8,128)S(1)} custom-call(bf16[40,256,256]{2,1,0:T(8,128)(2,1)S(1)} %get-tuple-element.15.first, bf16[24,256,256]{2,1,0:T(8,128)(2,1)S(1)} %get-tuple-element.18.second, s32[81]{0:T(128)S(1)} %get-tuple-element.13.table.lists_first, s32[49]{0:T(128)S(1)} %get-tuple-element.16.table.lists_second, ...), custom_call_target="tpu_custom_call" | custom-call | tf_op jit(solution)/shard_map/columns/pallas_call | solution.py:346
  31.8 3.1 %collective-permute-done.12 = f32[8,256]{1,0:T(8,128)S(1)} collective-permute-done((f32[8,256]{1,0:T(8,128)S(1)}, f32[8,256]{1,0:T(8,128)S(1)}, u32[]{:S(2)}, u32[]{:S(2)}) %collective-permute-start.12) | collective-permute-done | bytes 8224 | tf_op jit(solution)/shard_map/ppermute | solution.py:44
  34.9 3.5 %collective-permute-start.13 = (f32[8,256]{1,0:T(8,128)S(1)}, f32[8,256]{1,0:T(8,128)S(1)}, u32[]{:S(2)}, u32[]{:S(2)}) collective-permute-start(f32[8,256]{1,0:T(8,128)S(1)} %add.41), channel_id=1, source_target_pairs={{0,5},{1,4},{2,7},{3,6},{4,1},{5,0},{6,3},{7,2},{8,13},{9,12},{10,... | collective-permute-start | bytes 24584 | tf_op jit(solution)/shard_map/ppermute | solution.py:44
  38.3 1.4 %collective-permute-done.13 = f32[8,256]{1,0:T(8,128)S(1)} collective-permute-done((f32[8,256]{1,0:T(8,128)S(1)}, f32[8,256]{1,0:T(8,128)S(1)}, u32[]{:S(2)}, u32[]{:S(2)}) %collective-permute-start.13) | collective-permute-done | bytes 8224 | tf_op jit(solution)/shard_map/ppermute | solution.py:44
  39.7 3.5 %collective-permute-start.15 = (f32[4,256]{1,0:T(4,128)S(1)}, f32[4,256]{1,0:T(4,128)S(1)}, u32[]{:S(2)}, u32[]{:S(2)}) collective-permute-start(f32[4,256]{1,0:T(4,128)S(1)} %get-tuple-element.25), channel_id=1, source_target_pairs={{0,25},{1,24},{2,27},{3,26},{4,29},{5,28},{6,31},{7,30},{8,1},{9,0... | collective-permute-start | bytes 12296 | tf_op jit(solution)/shard_map/ppermute | solution.py:44
  43.3 1.3 %collective-permute-done.14.before = f32[4,256]{1,0:T(4,128)S(1)} collective-permute-done((f32[4,256]{1,0:T(4,128)S(1)}, f32[4,256]{1,0:T(4,128)S(1)}, u32[]{:S(2)}, u32[]{:S(2)}) %collective-permute-start.14) | collective-permute-done | bytes 4128 | tf_op jit(solution)/shard_map/ppermute | solution.py:44
  44.6 1.4 %rows.1 = f32[8,256]{1,0:T(8,128)S(1)} custom-call(bf16[40,256,256]{2,1,0:T(8,128)(2,1)S(1)} %get-tuple-element.15.first, bf16[24,256,256]{2,1,0:T(8,128)(2,1)S(1)} %get-tuple-element.18.second, s32[81]{0:T(128)S(1)} %get-tuple-element.13.table.lists_first, s32[49]{0:T(128)S(1)} %get-tuple-element.16.table.lists_second, f32[8,256]{1,0:T(8,128)S(1)} %add.42.columns, ...), custom_call_target="tpu_custom_call" | custom-call | tf_op jit(solution)/shard_map/rows/pallas_call | solution.py:337
  46.2 1.0 %collective-permute-done.16.arrived = f32[8,256]{1,0:T(8,128)S(1)} collective-permute-done((f32[8,256]{1,0:T(8,128)S(1)}, f32[8,256]{1,0:T(8,128)S(1)}, u32[]{:S(2)}, u32[]{:S(2)}) %collective-permute-start.16) | collective-permute-done | bytes 8224 | tf_op jit(solution)/shard_map/ppermute | solution.py:57
  47.2 1.7 %columns.3 = (f32[8,256]{1,0:T(8,128)S(1)}, f32[4,256]{1,0:T(4,128)S(1)}) custom-call(bf16[40,256,256]{2,1,0:T(8,128)(2,1)S(1)} %get-tuple-element.15.first, bf16[24,256,256]{2,1,0:T(8,128)(2,1)S(1)} %get-tuple-element.18.second, s32[81]{0:T(128)S(1)} %get-tuple-element.13.table.lists_first, s32[49]{0:T(128)S(1)} %get-tuple-element.16.table.lists_second, ...), custom_call_target="tpu_custom_call" | custom-call | tf_op jit(solution)/shard_map/columns/pallas_call | solution.py:346
  49.0 3.0 %collective-permute-done.17 = f32[8,256]{1,0:T(8,128)S(1)} collective-permute-done((f32[8,256]{1,0:T(8,128)S(1)}, f32[8,256]{1,0:T(8,128)S(1)}, u32[]{:S(2)}, u32[]{:S(2)}) %collective-permute-start.17) | collective-permute-done | bytes 8224 | tf_op jit(solution)/shard_map/ppermute | solution.py:44
  52.1 1.5 %collective-permute-start.20 = (f32[1,256]{1,0:T(1,128)S(1)}, f32[1,256]{1,0:T(1,128)S(1)}, u32[]{:S(2)}, u32[]{:S(2)}) collective-permute-start(f32[1,256]{1,0:T(1,128)S(1)} %get-tuple-element.23), channel_id=1, source_target_pairs={{0,12},{1,13},{2,14},{3,15},{4,8},{5,9},{6,10},{7,11},{8,20},{9,21... | collective-permute-start | bytes 3080 | tf_op jit(solution)/shard_map/ppermute | solution.py:44
  53.5 0.7 %collective-permute-start.19 = (f32[1,256]{1,0:T(1,128)S(1)}, f32[1,256]{1,0:T(1,128)S(1)}, u32[]{:S(2)}, u32[]{:S(2)}) collective-permute-start(f32[1,256]{1,0:T(1,128)S(1)} %get-tuple-element.24), channel_id=1, source_target_pairs={{0,9},{1,8},{2,11},{3,10},{4,13},{5,12},{6,15},{7,14},{8,17},{9,16... | collective-permute-start | bytes 3080 | tf_op jit(solution)/shard_map/ppermute | solution.py:44
  54.3 0.9 %collective-permute-start.18 = (f32[1,256]{1,0:T(1,128)S(1)}, f32[1,256]{1,0:T(1,128)S(1)}, u32[]{:S(2)}, u32[]{:S(2)}) collective-permute-start(f32[1,256]{1,0:T(1,128)S(1)} %get-tuple-element.22), channel_id=1, source_target_pairs={{0,5},{1,4},{2,7},{3,6},{4,1},{5,0},{6,3},{7,2},{8,13},{9,12},{10,... | collective-permute-start | bytes 3080 | tf_op jit(solution)/shard_map/ppermute | solution.py:44
  55.2 0.6 %copy.7 = f32[1,2,4,128]{3,1,2,0:T(2,128)} copy(f32[1,2,4,128]{3,2,1,0:T(4,128)S(1)} %bitcast.5) | data formatting | bytes 8192
  55.8 2.6 %collective-permute-done.20 = f32[1,256]{1,0:T(1,128)S(1)} collective-permute-done((f32[1,256]{1,0:T(1,128)S(1)}, f32[1,256]{1,0:T(1,128)S(1)}, u32[]{:S(2)}, u32[]{:S(2)}) %collective-permute-start.20) | collective-permute-done | bytes 1056 | tf_op jit(solution)/shard_map/ppermute | solution.py:44
  58.9 0.6 divide_log_fusion
  (32 shorter events, 2.5 us)
Async XLA Ops:
  0.6 17.2 %collective-permute-start = (bf16[1024,256]{1,0:T(8,128)(2,1)}, bf16[1024,256]{1,0:T(8,128)(2,1)S(1)}, u32[]{:S(2)}, u32[]{:S(2)}) collective-permute-start(bf16[1024,256]{1,0:T(8,128)(2,1)} %own.1), channel_id=1, source_target_pairs={{0,1},{1,0},{2,3},{3,2},{4,5},{5,4},{6,7},{7,6},{8,9},{9,8},{10,11... | collective-permute-start | bytes 1572872 | tf_op jit(solution)/shard_map/ppermute | solution.py:57
  1.2 8.3 %collective-permute-start.6 = (bf16[256,256]{1,0:T(8,128)(2,1)}, bf16[256,256]{1,0:T(8,128)(2,1)S(1)}, u32[]{:S(2)}, u32[]{:S(2)}) collective-permute-start(bf16[256,256]{1,0:T(8,128)(2,1)} %target.1), channel_id=1, source_target_pairs={{0,25},{1,24},{2,27},{3,26},{4,29},{5,28},{6,31},{7,30},{8,1},{9,0... | collective-permute-start | bytes 393224 | tf_op jit(solution)/shard_map/ppermute | solution.py:44
  5.9 7.0 %collective-permute-start.2 = (bf16[256,256]{1,0:T(8,128)(2,1)}, bf16[256,256]{1,0:T(8,128)(2,1)S(1)}, u32[]{:S(2)}, u32[]{:S(2)}) collective-permute-start(bf16[256,256]{1,0:T(8,128)(2,1)} %target.1), channel_id=1, source_target_pairs={{0,3},{1,2},{2,1},{3,0},{4,7},{5,6},{6,5},{7,4},{8,11},{9,10},{10,... | collective-permute-start | bytes 393224 | tf_op jit(solution)/shard_map/ppermute | solution.py:44
  7.1 6.1 %collective-permute-start.3 = (bf16[256,256]{1,0:T(8,128)(2,1)}, bf16[256,256]{1,0:T(8,128)(2,1)S(1)}, u32[]{:S(2)}, u32[]{:S(2)}) collective-permute-start(bf16[256,256]{1,0:T(8,128)(2,1)} %target.1), channel_id=1, source_target_pairs={{0,5},{1,4},{2,7},{3,6},{4,1},{5,0},{6,3},{7,2},{8,13},{9,12},{10,... | collective-permute-start | bytes 393224 | tf_op jit(solution)/shard_map/ppermute | solution.py:44
  9.5 5.8 %collective-permute-start.7 = (bf16[256,256]{1,0:T(8,128)(2,1)S(1)}, bf16[256,256]{1,0:T(8,128)(2,1)S(1)}, u32[]{:S(2)}, u32[]{:S(2)}) collective-permute-start(bf16[256,256]{1,0:T(8,128)(2,1)S(1)} %collective-permute-done.6.refs_4_), channel_id=1, source_target_pairs={{0,3},{1,2},{2,1},{3,0},{4,7},{5,6},{6,5},{7,4},{8,11},{9,10},{10,... | collective-permute-start | bytes 393224 | tf_op jit(solution)/shard_map/ppermute | solution.py:44
  10.1 5.5 %collective-permute-start.8 = (bf16[256,256]{1,0:T(8,128)(2,1)S(1)}, bf16[256,256]{1,0:T(8,128)(2,1)S(1)}, u32[]{:S(2)}, u32[]{:S(2)}) collective-permute-start(bf16[256,256]{1,0:T(8,128)(2,1)S(1)} %collective-permute-done.6.refs_4_), channel_id=1, source_target_pairs={{0,5},{1,4},{2,7},{3,6},{4,1},{5,0},{6,3},{7,2},{8,13},{9,12},{10,... | collective-permute-start | bytes 393224 | tf_op jit(solution)/shard_map/ppermute | solution.py:44
  12.9 9.6 %collective-permute-start.4 = (bf16[128,256]{1,0:T(8,128)(2,1)S(1)}, bf16[128,256]{1,0:T(8,128)(2,1)S(1)}, u32[]{:S(2)}, u32[]{:S(2)}) collective-permute-start(bf16[128,256]{1,0:T(8,128)(2,1)S(1)} %slice.24), channel_id=1, source_target_pairs={{0,5},{1,4},{2,7},{3,6},{4,1},{5,0},{6,3},{7,2},{8,13},{9,12},{10,... | collective-permute-start | bytes 196616 | tf_op jit(solution)/shard_map/ppermute | solution.py:44
  13.2 9.3 %collective-permute-start.5 = (bf16[128,256]{1,0:T(8,128)(2,1)S(1)}, bf16[128,256]{1,0:T(8,128)(2,1)S(1)}, u32[]{:S(2)}, u32[]{:S(2)}) collective-permute-start(bf16[128,256]{1,0:T(8,128)(2,1)S(1)} %slice.25), channel_id=1, source_target_pairs={{0,3},{1,2},{2,1},{3,0},{4,7},{5,6},{6,5},{7,4},{8,11},{9,10},{10,... | collective-permute-start | bytes 196616 | tf_op jit(solution)/shard_map/ppermute | solution.py:44
  15.2 2.3 %collective-permute-start.1 = (s32[1,65]{1,0:T(1,128)S(1)}, s32[1,65]{1,0:T(1,128)S(1)}, u32[]{:S(2)}, u32[]{:S(2)}) collective-permute-start(s32[1,65]{1,0:T(1,128)S(1)} %pad_add_fusion.mine), channel_id=1, source_target_pairs={{0,1},{1,0},{2,3},{3,2},{4,5},{5,4},{6,7},{7,6},{8,9},{9,8},{10,11... | collective-permute-start | bytes 788 | tf_op jit(solution)/shard_map/ppermute | solution.py:57
  15.6 10.4 %collective-permute-start.9 = (bf16[128,256]{1,0:T(8,128)(2,1)S(1)}, bf16[128,256]{1,0:T(8,128)(2,1)S(1)}, u32[]{:S(2)}, u32[]{:S(2)}) collective-permute-start(bf16[128,256]{1,0:T(8,128)(2,1)S(1)} %slice.26), channel_id=1, source_target_pairs={{0,5},{1,4},{2,7},{3,6},{4,1},{5,0},{6,3},{7,2},{8,13},{9,12},{10,... | collective-permute-start | bytes 196616 | tf_op jit(solution)/shard_map/ppermute | solution.py:44
  17.6 8.5 %collective-permute-start.10 = (bf16[128,256]{1,0:T(8,128)(2,1)S(1)}, bf16[128,256]{1,0:T(8,128)(2,1)S(1)}, u32[]{:S(2)}, u32[]{:S(2)}) collective-permute-start(bf16[128,256]{1,0:T(8,128)(2,1)S(1)} %slice.27), channel_id=1, source_target_pairs={{0,3},{1,2},{2,1},{3,0},{4,7},{5,6},{6,5},{7,4},{8,11},{9,10},{10,... | collective-permute-start | bytes 196616 | tf_op jit(solution)/shard_map/ppermute | solution.py:44
  17.8 1.0 %copy-start = (bf16[1024,256]{1,0:T(8,128)(2,1)S(1)}, bf16[1024,256]{1,0:T(8,128)(2,1)}, u32[]{:S(2)}) copy-start(bf16[1024,256]{1,0:T(8,128)(2,1)} %own.1) | copy-start | bytes 1572868
  18.9 0.9 %copy-start.1 = (bf16[256,256]{1,0:T(8,128)(2,1)S(1)}, bf16[256,256]{1,0:T(8,128)(2,1)}, u32[]{:S(2)}) copy-start(bf16[256,256]{1,0:T(8,128)(2,1)} %target.1) | copy-start | bytes 393220
  27.7 2.3 %collective-permute-start.11 = (f32[8,256]{1,0:T(8,128)S(1)}, f32[8,256]{1,0:T(8,128)S(1)}, u32[]{:S(2)}, u32[]{:S(2)}) collective-permute-start(f32[8,256]{1,0:T(8,128)S(1)} %get-tuple-element.19.rows), channel_id=1, source_target_pairs={{0,1},{1,0},{2,3},{3,2},{4,5},{5,4},{6,7},{7,6},{8,9},{9,8},{10,11... | collective-permute-start | bytes 24584 | tf_op jit(solution)/shard_map/ppermute | solution.py:57
  31.7 3.1 %collective-permute-start.12 = (f32[8,256]{1,0:T(8,128)S(1)}, f32[8,256]{1,0:T(8,128)S(1)}, u32[]{:S(2)}, u32[]{:S(2)}) collective-permute-start(f32[8,256]{1,0:T(8,128)S(1)} %columns.2), channel_id=1, source_target_pairs={{0,3},{1,2},{2,1},{3,0},{4,7},{5,6},{6,5},{7,4},{8,11},{9,10},{10,... | collective-permute-start | bytes 24584 | tf_op jit(solution)/shard_map/ppermute | solution.py:44
  34.9 4.8 %collective-permute-start.13 = (f32[8,256]{1,0:T(8,128)S(1)}, f32[8,256]{1,0:T(8,128)S(1)}, u32[]{:S(2)}, u32[]{:S(2)}) collective-permute-start(f32[8,256]{1,0:T(8,128)S(1)} %add.41), channel_id=1, source_target_pairs={{0,5},{1,4},{2,7},{3,6},{4,1},{5,0},{6,3},{7,2},{8,13},{9,12},{10,... | collective-permute-start | bytes 24584 | tf_op jit(solution)/shard_map/ppermute | solution.py:44
  39.7 4.8 %collective-permute-start.14 = (f32[4,256]{1,0:T(4,128)S(1)}, f32[4,256]{1,0:T(4,128)S(1)}, u32[]{:S(2)}, u32[]{:S(2)}) collective-permute-start(f32[4,256]{1,0:T(4,128)S(1)} %get-tuple-element.26), channel_id=1, source_target_pairs={{0,9},{1,8},{2,11},{3,10},{4,13},{5,12},{6,15},{7,14},{8,17},{9,16... | collective-permute-start | bytes 12296 | tf_op jit(solution)/shard_map/ppermute | solution.py:44
  39.7 4.9 %collective-permute-start.15 = (f32[4,256]{1,0:T(4,128)S(1)}, f32[4,256]{1,0:T(4,128)S(1)}, u32[]{:S(2)}, u32[]{:S(2)}) collective-permute-start(f32[4,256]{1,0:T(4,128)S(1)} %get-tuple-element.25), channel_id=1, source_target_pairs={{0,25},{1,24},{2,27},{3,26},{4,29},{5,28},{6,31},{7,30},{8,1},{9,0... | collective-permute-start | bytes 12296 | tf_op jit(solution)/shard_map/ppermute | solution.py:44
  46.0 1.2 %collective-permute-start.16 = (f32[8,256]{1,0:T(8,128)S(1)}, f32[8,256]{1,0:T(8,128)S(1)}, u32[]{:S(2)}, u32[]{:S(2)}) collective-permute-start(f32[8,256]{1,0:T(8,128)S(1)} %rows.1), channel_id=1, source_target_pairs={{0,1},{1,0},{2,3},{3,2},{4,5},{5,4},{6,7},{7,6},{8,9},{9,8},{10,11... | collective-permute-start | bytes 24584 | tf_op jit(solution)/shard_map/ppermute | solution.py:57
  48.9 3.1 %collective-permute-start.17 = (f32[8,256]{1,0:T(8,128)S(1)}, f32[8,256]{1,0:T(8,128)S(1)}, u32[]{:S(2)}, u32[]{:S(2)}) collective-permute-start(f32[8,256]{1,0:T(8,128)S(1)} %get-tuple-element.21), channel_id=1, source_target_pairs={{0,3},{1,2},{2,1},{3,0},{4,7},{5,6},{6,5},{7,4},{8,11},{9,10},{10,... | collective-permute-start | bytes 24584 | tf_op jit(solution)/shard_map/ppermute | solution.py:44
  52.1 6.3 %collective-permute-start.20 = (f32[1,256]{1,0:T(1,128)S(1)}, f32[1,256]{1,0:T(1,128)S(1)}, u32[]{:S(2)}, u32[]{:S(2)}) collective-permute-start(f32[1,256]{1,0:T(1,128)S(1)} %get-tuple-element.23), channel_id=1, source_target_pairs={{0,12},{1,13},{2,14},{3,15},{4,8},{5,9},{6,10},{7,11},{8,20},{9,21... | collective-permute-start | bytes 3080 | tf_op jit(solution)/shard_map/ppermute | solution.py:44
  53.5 5.3 %collective-permute-start.19 = (f32[1,256]{1,0:T(1,128)S(1)}, f32[1,256]{1,0:T(1,128)S(1)}, u32[]{:S(2)}, u32[]{:S(2)}) collective-permute-start(f32[1,256]{1,0:T(1,128)S(1)} %get-tuple-element.24), channel_id=1, source_target_pairs={{0,9},{1,8},{2,11},{3,10},{4,13},{5,12},{6,15},{7,14},{8,17},{9,16... | collective-permute-start | bytes 3080 | tf_op jit(solution)/shard_map/ppermute | solution.py:44
  54.3 4.6 %collective-permute-start.18 = (f32[1,256]{1,0:T(1,128)S(1)}, f32[1,256]{1,0:T(1,128)S(1)}, u32[]{:S(2)}, u32[]{:S(2)}) collective-permute-start(f32[1,256]{1,0:T(1,128)S(1)} %get-tuple-element.22), channel_id=1, source_target_pairs={{0,5},{1,4},{2,7},{3,6},{4,1},{5,0},{6,3},{7,2},{8,13},{9,12},{10,... | collective-permute-start | bytes 3080 | tf_op jit(solution)/shard_map/ppermute | solution.py:44
where the time goes:
time: 59.7 us; the launch traced here: 59.5 us
  starting transfers between devices  26.7 us (45%)
  waiting for transfers between devices  14.8 us (25%)
  Pallas kernels  12.6 us (21%)
  local copies, waits for them, and re-layouts  2.58 us (4%)
  between operations  1.43 us (2%)
  other arithmetic  1.34 us (2%)
    ppermute x17, starting transfers between devices, hop(): lax.ppermute(x, BOTH, [(g * members + m, (g - up) % groups * members + (m...  24.2 us
    ppermute x17, waiting for transfers between devices, hop(): lax.ppermute(x, BOTH, [(g * members + m, (g - up) % groups * members + (m...  13 us
    pallas_call x1, Pallas kernels, step(): first_call(units, lists_first, home, *[b for t in early for b in t])  3.5 us
    pallas_call x2, Pallas kernels, step(): pl.pallas_call(functools.partial(column_kernel, last), out_shape=(shaped(...  3.36 us
    pallas_call x1, Pallas kernels, step(): prepare(source, target, partner_source, info, partner_info)  2.69 us
    unnamed x5, local copies, waits for them, and re-layouts  2.54 us
    ppermute x4, starting transfers between devices, partner(): return lax.ppermute(x, 'member', [(i, i ^ 1) for i in range(size)])  2.43 us
    ppermute x4, waiting for transfers between devices, partner(): return lax.ppermute(x, 'member', [(i, i ^ 1) for i in range(size)])  1.84 us
  transfers between devices with their start and end apart: 21, of which 10 were waited for; matrix products, arithmetic and copies ran while one was open for 2% of the time, Pallas kernels for 10%

commit v1 on v0

--- a/solution.py
+++ b/solution.py
@@ -15,6 +15,7 @@
 CORES = 2
 LANES = 128
 MIB = 2**20
+GROUP = 4
 
 
 BOTH = ("group", "member")
@@ -35,6 +36,10 @@
     for b in range(width):
         result = result ^ (value >> b)
     return result & 1
+
+
+def up_to_group(count):
+    return -(-count // GROUP) * GROUP
 
 
 def hop(x, up, bits):
@@ -58,21 +63,10 @@
 
 
 def spread_tiles(start, chips):
-    half = start.shape[0] // 2
-    tiles = {0: [start]}
-
-    def part(k, which):
-        blocks = tiles[k]
-        return blocks[which] if len(blocks) == 2 else blocks[0][which * half : (which + 1) * half]
-
-    for k in sorted(range(1, chips), key=lambda k: (bin(k).count("1"), k)):
-        low, high = k & -k, 1 << (k.bit_length() - 1)
-        if low == high:
-            tiles[k] = [hop(start, 0, k)]
-        else:
-            upper = hop(part(k ^ high, 0), 0, high)
-            tiles[k] = [upper, hop(part(k ^ low, 1), 0, low)]
-    return [tiles[k] for k in range(chips)]
+    tiles = [start]
+    for k in range(1, chips):
+        tiles.append(hop(start, 0, k))
+    return tiles
 
 
 def unit(values):
@@ -83,7 +77,8 @@
 
 
 def rows_out(acc, out):
-    tiles, cells, lanes = acc.shape
+    tiles = out.shape[0]
+    cells, lanes = acc.shape[1:]
     lane = lax.broadcasted_iota(jnp.int32, (cells, lanes), 1)
     table = jnp.zeros((cells, lanes), F32)
     for s in range(tiles):
@@ -150,52 +145,45 @@
     home[...] = unit(tile[...])
 
 
-def place(window, at, blocks):
-    row = 0
-    for block in blocks:
-        rows = block.shape[0]
-        window[at, row : row + rows] = unit(block[...])
-        row += rows
-
-
 def build_pairs(units, window, table, factors, acc, where):
-    def pair(n, carry):
-        s, w = table[1 + 2 * n], table[2 + 2 * n]
-        logits = lax.dot_general(
-            units[s], window[where(w)], (((1,), (1,)), ((), ())), preferred_element_type=F32
-        )
-        values = jnp.exp2(logits * FACTOR)
-        factors[n] = values.astype(BF16)
-        add_halves(acc, s, values)
+    spare = acc.shape[0] - 1
+    found = table[0]
+
+    def step(m, carry):
+        for i in range(GROUP):
+            n = m * GROUP + i
+            real = n < found
+            at = jnp.where(real, n, 0)
+            s, w = table[1 + 2 * at], table[2 + 2 * at]
+            logits = lax.dot_general(
+                units[s], window[where(w)], (((1,), (1,)), ((), ())), preferred_element_type=F32
+            )
+            values = jnp.exp2(logits * FACTOR)
+            factors[n] = values.astype(BF16)
+            add_halves(acc, jnp.where(real, s, spare), values)
         return carry
 
-    lax.fori_loop(0, table[0], pair, 0)
-
-
-def first_kernel(chips, shape, units, table, home, *refs):
-    count = sum(shape)
-    tiles = refs[:count]
-    factors, acc, window = refs[count:]
+    lax.fori_loop(0, (found + GROUP - 1) // GROUP, step, 0)
+
+
+def first_kernel(chips, units, table, home, *refs):
+    tiles = refs[:chips]
+    factors, acc, window = refs[chips:]
     chip = lax.axis_index("member") // CORES
     window[chip] = home[...]
-    at = 0
-    for k, blocks in enumerate(shape):
-        slot = chip ^ (k + 1) if k + 1 < chips else chips
-        place(window, slot, tiles[at : at + blocks])
-        at += blocks
+    for k in range(1, chips):
+        window[chip ^ k] = unit(tiles[k - 1][...])
+    window[chips] = unit(tiles[chips - 1][...])
     acc[...] = jnp.zeros_like(acc)
     build_pairs(units, window, table, factors, acc, lambda w: jnp.minimum(w, chips))
 
 
-def second_kernel(chips, shape, units, table, before, *refs):
-    count = sum(shape)
-    tiles = refs[:count]
-    factors, rows, acc, window = refs[count:]
+def second_kernel(chips, units, table, before, *refs):
+    tiles = refs[: chips - 1]
+    factors, rows, acc, window = refs[chips - 1 :]
     chip = lax.axis_index("member") // CORES
-    at = 0
-    for k, blocks in enumerate(shape):
-        place(window, chip ^ (k + 1), tiles[at : at + blocks])
-        at += blocks
+    for k in range(1, chips):
+        window[chip ^ k] = unit(tiles[k - 1][...])
     acc[...] = before[...]
     build_pairs(units, window, table, factors, acc, lambda w: w - chips)
     rows_out(acc, rows)
@@ -257,8 +245,8 @@
     both = CORES * tiles
     slots = pair_source.shape[1]
     even = 1 if groups % 2 == 0 else 0
-    most_first = min(CORES * slots, both * (chips + 1))
-    most_second = min(CORES * slots, both * (chips - 1))
+    most_first = up_to_group(min(CORES * slots, both * (chips + 1)))
+    most_second = up_to_group(min(CORES * slots, both * (chips - 1)))
 
     beyond = hop(target, 1, 0)
     own_tiles = spread_tiles(target, chips)
@@ -308,26 +296,29 @@
     early = own_tiles[1:] + [next_tiles[0]]
     late = next_tiles[1:]
     first_call = pl.pallas_call(
-        functools.partial(first_kernel, chips, [len(t) for t in early]),
-        out_shape=(shaped(most_first, cells, cells, kind=BF16), shaped(*lanes_acc)),
-        in_specs=[VM, SM, VM] + [VM] * sum(len(t) for t in early),
+        functools.partial(first_kernel, chips),
+        out_shape=(shaped(most_first, cells, cells, kind=BF16), shaped(both + 1, cells, LANES)),
+        in_specs=[VM, SM, VM] + [VM] * len(early),
         out_specs=(VM, VM),
         scratch_shapes=[pltpu.VMEM((chips + 1, cells, width), BF16)],
         compiler_params=limit((most_first + 2 * chips + 2 + both) * tile + 5 * MIB),
         cost_estimate=cost(most_first),
         name="first",
     )
-    first, acc = first_call(units, lists_first, home, *[b for t in early for b in t])
+    first, acc = first_call(units, lists_first, home, *early)
     second, rows = pl.pallas_call(
-        functools.partial(second_kernel, chips, [len(t) for t in late]),
+        functools.partial(second_kernel, chips),
         out_shape=(shaped(most_second, cells, cells, kind=BF16), shaped(both, cells)),
-        in_specs=[VM, SM, VM] + [VM] * sum(len(t) for t in late),
+        in_specs=[VM, SM, VM] + [VM] * len(late),
         out_specs=(VM, VM),
-        scratch_shapes=[pltpu.VMEM(lanes_acc, F32), pltpu.VMEM((chips, cells, width), BF16)],
+        scratch_shapes=[
+            pltpu.VMEM((both + 1, cells, LANES), F32),
+            pltpu.VMEM((chips, cells, width), BF16),
+        ],
         compiler_params=limit((most_second + 2 * chips + both) * tile + 5 * MIB),
         cost_estimate=cost(most_second),
         name="second",
-    )(units, lists_second, acc, *[b for t in late for b in t])
+    )(units, lists_second, acc, *late)
     held = (first, second, lists_first, lists_second)
     held_limit = limit((most_first + most_second) * tile + 4 * MIB)
 

time: 59.7 us -> 54.5 us (0.913)
  starting transfers between devices: 26.7 us -> 22.6 us
  Pallas kernels: 12.6 us -> 11 us
  waiting for transfers between devices: 14.8 us -> 15.4 us
    ppermute x17 -> x15, starting transfers between devices: 24.2 us -> 20.8 us  [hop(): lax.ppermute(x, BOTH, [(g * members + m, (g - up) % groups * members + (m...]
    pallas_call x2, Pallas kernels: 5.16 us -> 3.58 us  [the longest x1 2.02 us: step(): first, acc = first_call(units, lists_first, home, *early)]
    ppermute x4, starting transfers between devices: 2.43 us -> 1.71 us  [partner(): return lax.ppermute(x, 'member', [(i, i ^ 1) for i in range(size)])]
    ppermute x17 -> x15, waiting for transfers between devices: 13 us -> 13.5 us  [hop(): lax.ppermute(x, BOTH, [(g * members + m, (g - up) % groups * members + (m...]
  transfers between devices with their start and end apart: 21 -> 19, of which waited for: 10 -> 9; matrix products, arithmetic and copies ran while one was open for 2% -> 2% of each run, Pallas kernels for 10% -> 9%
where the time goes in v1:
time: 54.5 us; the launch traced here: 54.3 us
  starting transfers between devices  22.6 us (41%)
  waiting for transfers between devices  15.4 us (28%)
  Pallas kernels  11 us (20%)
  local copies, waits for them, and re-layouts  2.56 us (5%)
  between operations  1.4 us (3%)
  other arithmetic  1.34 us (2%)
    ppermute x15, starting transfers between devices, hop(): lax.ppermute(x, BOTH, [(g * members + m, (g - up) % groups * members + (m...  20.8 us
    ppermute x15, waiting for transfers between devices, hop(): lax.ppermute(x, BOTH, [(g * members + m, (g - up) % groups * members + (m...  13.5 us
    pallas_call x2, Pallas kernels, step(): pl.pallas_call(functools.partial(column_kernel, last), out_shape=(shaped(...  3.36 us
    pallas_call x1, Pallas kernels, step(): prepare(source, target, partner_source, info, partner_info)  2.69 us
    unnamed x5, local copies, waits for them, and re-layouts  2.54 us
    pallas_call x1, Pallas kernels, step(): first, acc = first_call(units, lists_first, home, *early)  2.02 us
    ppermute x4, waiting for transfers between devices, partner(): return lax.ppermute(x, 'member', [(i, i ^ 1) for i in range(size)])  1.85 us
    ppermute x4, starting transfers between devices, partner(): return lax.ppermute(x, 'member', [(i, i ^ 1) for i in range(size)])  1.71 us
  transfers between devices with their start and end apart: 19, of which 9 were waited for; matrix products, arithmetic and copies ran while one was open for 2% of the time, Pallas kernels for 9%

profile of v1, /device:TPU:0, one launch (start us, length us, event | category | flops | bytes accessed | tf_op | source)
XLA Modules:
  0.0 54.3 jit_solution(16142798930670370612)
XLA Ops:
  0.6 0.6 %collective-permute-start = (bf16[1024,256]{1,0:T(8,128)(2,1)}, bf16[1024,256]{1,0:T(8,128)(2,1)S(1)}, u32[]{:S(2)}, u32[]{:S(2)}) collective-permute-start(bf16[1024,256]{1,0:T(8,128)(2,1)} %own.1), channel_id=1, source_target_pairs={{0,1},{1,0},{2,3},{3,2},{4,5},{5,4},{6,7},{7,6},{8,9},{9,8},{10,11... | collective-permute-start | bytes 1572872 | tf_op jit(solution)/shard_map/ppermute | solution.py:62
  1.2 2.6 %collective-permute-start.2 = (bf16[256,256]{1,0:T(8,128)(2,1)}, bf16[256,256]{1,0:T(8,128)(2,1)S(1)}, u32[]{:S(2)}, u32[]{:S(2)}) collective-permute-start(bf16[256,256]{1,0:T(8,128)(2,1)} %target.1), channel_id=1, source_target_pairs={{0,3},{1,2},{2,1},{3,0},{4,7},{5,6},{6,5},{7,4},{8,11},{9,10},{10,... | collective-permute-start | bytes 393224 | tf_op jit(solution)/shard_map/ppermute | solution.py:49
  3.8 3.3 %collective-permute-start.5 = (bf16[256,256]{1,0:T(8,128)(2,1)}, bf16[256,256]{1,0:T(8,128)(2,1)S(1)}, u32[]{:S(2)}, u32[]{:S(2)}) collective-permute-start(bf16[256,256]{1,0:T(8,128)(2,1)} %target.1), channel_id=1, source_target_pairs={{0,25},{1,24},{2,27},{3,26},{4,29},{5,28},{6,31},{7,30},{8,1},{9,0... | collective-permute-start | bytes 393224 | tf_op jit(solution)/shard_map/ppermute | solution.py:49
  7.7 0.7 %pad_add_fusion.mine = s32[1,65]{1,0:T(1,128)S(1)} fusion(s32[1,1]{1,0:T(1,128)} %bitcast.4, s32[1,32]{1,0:T(1,128)} %param.8, s32[1,32]{1,0:T(1,128)} %param.7), kind=kLoop, calls=%fused_computation.4 | loop fusion | flops 130 | bytes 520 | tf_op jit(solution)/shard_map/concatenate | solution.py:254
  8.9 1.2 %collective-permute-start.3 = (bf16[256,256]{1,0:T(8,128)(2,1)}, bf16[256,256]{1,0:T(8,128)(2,1)S(1)}, u32[]{:S(2)}, u32[]{:S(2)}) collective-permute-start(bf16[256,256]{1,0:T(8,128)(2,1)} %target.1), channel_id=1, source_target_pairs={{0,5},{1,4},{2,7},{3,6},{4,1},{5,0},{6,3},{7,2},{8,13},{9,12},{10,... | collective-permute-start | bytes 393224 | tf_op jit(solution)/shard_map/ppermute | solution.py:49
  10.1 1.1 %collective-permute-start.4 = (bf16[256,256]{1,0:T(8,128)(2,1)}, bf16[256,256]{1,0:T(8,128)(2,1)S(1)}, u32[]{:S(2)}, u32[]{:S(2)}) collective-permute-start(bf16[256,256]{1,0:T(8,128)(2,1)} %target.1), channel_id=1, source_target_pairs={{0,6},{1,7},{2,4},{3,5},{4,2},{5,3},{6,0},{7,1},{8,14},{9,15},{10,... | collective-permute-start | bytes 393224 | tf_op jit(solution)/shard_map/ppermute | solution.py:49
  11.2 1.2 %collective-permute-start.6 = (bf16[256,256]{1,0:T(8,128)(2,1)S(1)}, bf16[256,256]{1,0:T(8,128)(2,1)S(1)}, u32[]{:S(2)}, u32[]{:S(2)}) collective-permute-start(bf16[256,256]{1,0:T(8,128)(2,1)S(1)} %collective-permute-done.5.refs_3_), channel_id=1, source_target_pairs={{0,3},{1,2},{2,1},{3,0},{4,7},{5,6},{6,5},{7,4},{8,11},{9,10},{10,... | collective-permute-start | bytes 393224 | tf_op jit(solution)/shard_map/ppermute | solution.py:49
  12.4 0.9 %collective-permute-start.7 = (bf16[256,256]{1,0:T(8,128)(2,1)S(1)}, bf16[256,256]{1,0:T(8,128)(2,1)S(1)}, u32[]{:S(2)}, u32[]{:S(2)}) collective-permute-start(bf16[256,256]{1,0:T(8,128)(2,1)S(1)} %collective-permute-done.5.refs_3_), channel_id=1, source_target_pairs={{0,5},{1,4},{2,7},{3,6},{4,1},{5,0},{6,3},{7,2},{8,13},{9,12},{10,... | collective-permute-start | bytes 393224 | tf_op jit(solution)/shard_map/ppermute | solution.py:49
  13.3 1.1 %collective-permute-start.8 = (bf16[256,256]{1,0:T(8,128)(2,1)S(1)}, bf16[256,256]{1,0:T(8,128)(2,1)S(1)}, u32[]{:S(2)}, u32[]{:S(2)}) collective-permute-start(bf16[256,256]{1,0:T(8,128)(2,1)S(1)} %collective-permute-done.5.refs_3_), channel_id=1, source_target_pairs={{0,6},{1,7},{2,4},{3,5},{4,2},{5,3},{6,0},{7,1},{8,14},{9,15},{10,... | collective-permute-start | bytes 393224 | tf_op jit(solution)/shard_map/ppermute | solution.py:49
  14.4 1.0 %copy-done = bf16[1024,256]{1,0:T(8,128)(2,1)S(1)} copy-done((bf16[1024,256]{1,0:T(8,128)(2,1)S(1)}, bf16[1024,256]{1,0:T(8,128)(2,1)}, u32[]{:S(2)}) %copy-start) | copy-done | bytes 524312
  15.5 0.9 %copy-done.1 = bf16[256,256]{1,0:T(8,128)(2,1)S(1)} copy-done((bf16[256,256]{1,0:T(8,128)(2,1)S(1)}, bf16[256,256]{1,0:T(8,128)(2,1)}, u32[]{:S(2)}) %copy-start.1) | copy-done | bytes 131096
  16.4 2.7 %prepare.1 = (bf16[8,256,256]{2,1,0:T(8,128)(2,1)S(1)}, bf16[256,256]{1,0:T(8,128)(2,1)S(1)}, s32[81]{0:T(128)S(1)}, s32[49]{0:T(128)S(1)}) custom-call(bf16[1024,256]{1,0:T(8,128)(2,1)S(1)} %copy-done, bf16[256,256]{1,0:T(8,128)(2,1)S(1)} %copy-done.1, bf16[1024,256]{1,0:T(8,128)(2,1)S(1)} %collective-permute-done.other, s32[1,65]{1,0:T(1,128)S(1)} %pad_add_fusion.mine, ...), custom_call_target="tpu_custom_call" | custom-call | flops 268435456 | bytes 1048576 | tf_op jit(solution)/shard_map/prepare/pallas_call | solution.py:292
  19.1 2.0 %first.1 = (bf16[40,256,256]{2,1,0:T(8,128)(2,1)S(1)}, f32[9,256,128]{2,1,0:T(8,128)S(1)}) custom-call(bf16[8,256,256]{2,1,0:T(8,128)(2,1)S(1)} %get-tuple-element.12.units, s32[81]{0:T(128)S(1)} %get-tuple-element.13.table.lists_first, bf16[256,256]{1,0:T(8,128)(2,1)S(1)} %get-tuple-element.14.home, bf16[256,256]{1,0:T(8,128)(2,1)S(1)} %collective-permute-done.2.refs_0_, ...), custom_call_target="tpu_custom_call" | custom-call | flops 1342177280 | bytes 5242880 | tf_op jit(solution)/shard_map/first/pallas_call | solution.py:308
  21.1 1.9 %collective-permute-done.7.refs_1_ = bf16[256,256]{1,0:T(8,128)(2,1)S(1)} collective-permute-done((bf16[256,256]{1,0:T(8,128)(2,1)S(1)}, bf16[256,256]{1,0:T(8,128)(2,1)S(1)}, u32[]{:S(2)}, u32[]{:S(2)}) %collective-permute-start.7) | collective-permute-done | bytes 131104 | tf_op jit(solution)/shard_map/ppermute | solution.py:49
  23.1 1.6 %second.1 = (bf16[24,256,256]{2,1,0:T(8,128)(2,1)S(1)}, f32[8,256]{1,0:T(8,128)S(1)}) custom-call(bf16[8,256,256]{2,1,0:T(8,128)(2,1)S(1)} %get-tuple-element.12.units, s32[49]{0:T(128)S(1)} %get-tuple-element.16.table.lists_second, f32[9,256,128]{2,1,0:T(8,128)S(1)} %get-tuple-element.17.before, bf16[256,256]{1,0:T(8,128)(2,1)S(1)} %collective-permute-done.6.refs_0_, ...), custom_call_target="tpu_custom_call" | custom-call | flops 805306368 | bytes 3145728 | tf_op jit(solution)/shard_map/second/pallas_call | solution.py:309
  24.6 0.5 collective-permute-start.9
  25.2 0.8 %collective-permute-done.9.arrived = f32[8,256]{1,0:T(8,128)S(1)} collective-permute-done((f32[8,256]{1,0:T(8,128)S(1)}, f32[8,256]{1,0:T(8,128)S(1)}, u32[]{:S(2)}, u32[]{:S(2)}) %collective-permute-start.9) | collective-permute-done | bytes 8224 | tf_op jit(solution)/shard_map/ppermute | solution.py:62
  26.0 1.7 %columns.2 = f32[8,256]{1,0:T(8,128)S(1)} custom-call(bf16[40,256,256]{2,1,0:T(8,128)(2,1)S(1)} %get-tuple-element.15.first, bf16[24,256,256]{2,1,0:T(8,128)(2,1)S(1)} %get-tuple-element.18.second, s32[81]{0:T(128)S(1)} %get-tuple-element.13.table.lists_first, s32[49]{0:T(128)S(1)} %get-tuple-element.16.table.lists_second, ...), custom_call_target="tpu_custom_call" | custom-call | tf_op jit(solution)/shard_map/columns/pallas_call | solution.py:337
  28.2 2.6 %collective-permute-done.10 = f32[8,256]{1,0:T(8,128)S(1)} collective-permute-done((f32[8,256]{1,0:T(8,128)S(1)}, f32[8,256]{1,0:T(8,128)S(1)}, u32[]{:S(2)}, u32[]{:S(2)}) %collective-permute-start.10) | collective-permute-done | bytes 8224 | tf_op jit(solution)/shard_map/ppermute | solution.py:49
  30.8 2.3 %collective-permute-start.11 = (f32[8,256]{1,0:T(8,128)S(1)}, f32[8,256]{1,0:T(8,128)S(1)}, u32[]{:S(2)}, u32[]{:S(2)}) collective-permute-start(f32[8,256]{1,0:T(8,128)S(1)} %add.41), channel_id=1, source_target_pairs={{0,5},{1,4},{2,7},{3,6},{4,1},{5,0},{6,3},{7,2},{8,13},{9,12},{10,... | collective-permute-start | bytes 24584 | tf_op jit(solution)/shard_map/ppermute | solution.py:49
  33.2 1.4 %collective-permute-done.11 = f32[8,256]{1,0:T(8,128)S(1)} collective-permute-done((f32[8,256]{1,0:T(8,128)S(1)}, f32[8,256]{1,0:T(8,128)S(1)}, u32[]{:S(2)}, u32[]{:S(2)}) %collective-permute-start.11) | collective-permute-done | bytes 8224 | tf_op jit(solution)/shard_map/ppermute | solution.py:49
  34.5 3.5 %collective-permute-start.13 = (f32[4,256]{1,0:T(4,128)S(1)}, f32[4,256]{1,0:T(4,128)S(1)}, u32[]{:S(2)}, u32[]{:S(2)}) collective-permute-start(f32[4,256]{1,0:T(4,128)S(1)} %get-tuple-element.25), channel_id=1, source_target_pairs={{0,25},{1,24},{2,27},{3,26},{4,29},{5,28},{6,31},{7,30},{8,1},{9,0... | collective-permute-start | bytes 12296 | tf_op jit(solution)/shard_map/ppermute | solution.py:49
  38.1 1.3 %collective-permute-done.12.before = f32[4,256]{1,0:T(4,128)S(1)} collective-permute-done((f32[4,256]{1,0:T(4,128)S(1)}, f32[4,256]{1,0:T(4,128)S(1)}, u32[]{:S(2)}, u32[]{:S(2)}) %collective-permute-start.12) | collective-permute-done | bytes 4128 | tf_op jit(solution)/shard_map/ppermute | solution.py:49
  39.4 1.4 %rows.1 = f32[8,256]{1,0:T(8,128)S(1)} custom-call(bf16[40,256,256]{2,1,0:T(8,128)(2,1)S(1)} %get-tuple-element.15.first, bf16[24,256,256]{2,1,0:T(8,128)(2,1)S(1)} %get-tuple-element.18.second, s32[81]{0:T(128)S(1)} %get-tuple-element.13.table.lists_first, s32[49]{0:T(128)S(1)} %get-tuple-element.16.table.lists_second, f32[8,256]{1,0:T(8,128)S(1)} %add.42.columns, ...), custom_call_target="tpu_custom_call" | custom-call | tf_op jit(solution)/shard_map/rows/pallas_call | solution.py:328
  41.0 1.0 %collective-permute-done.14.arrived = f32[8,256]{1,0:T(8,128)S(1)} collective-permute-done((f32[8,256]{1,0:T(8,128)S(1)}, f32[8,256]{1,0:T(8,128)S(1)}, u32[]{:S(2)}, u32[]{:S(2)}) %collective-permute-start.14) | collective-permute-done | bytes 8224 | tf_op jit(solution)/shard_map/ppermute | solution.py:62
  42.0 1.7 %columns.3 = (f32[8,256]{1,0:T(8,128)S(1)}, f32[4,256]{1,0:T(4,128)S(1)}) custom-call(bf16[40,256,256]{2,1,0:T(8,128)(2,1)S(1)} %get-tuple-element.15.first, bf16[24,256,256]{2,1,0:T(8,128)(2,1)S(1)} %get-tuple-element.18.second, s32[81]{0:T(128)S(1)} %get-tuple-element.13.table.lists_first, s32[49]{0:T(128)S(1)} %get-tuple-element.16.table.lists_second, ...), custom_call_target="tpu_custom_call" | custom-call | tf_op jit(solution)/shard_map/columns/pallas_call | solution.py:337
  43.8 3.0 %collective-permute-done.15 = f32[8,256]{1,0:T(8,128)S(1)} collective-permute-done((f32[8,256]{1,0:T(8,128)S(1)}, f32[8,256]{1,0:T(8,128)S(1)}, u32[]{:S(2)}, u32[]{:S(2)}) %collective-permute-start.15) | collective-permute-done | bytes 8224 | tf_op jit(solution)/shard_map/ppermute | solution.py:49
  46.9 2.0 %collective-permute-start.17 = (f32[1,256]{1,0:T(1,128)S(1)}, f32[1,256]{1,0:T(1,128)S(1)}, u32[]{:S(2)}, u32[]{:S(2)}) collective-permute-start(f32[1,256]{1,0:T(1,128)S(1)} %get-tuple-element.24), channel_id=1, source_target_pairs={{0,9},{1,8},{2,11},{3,10},{4,13},{5,12},{6,15},{7,14},{8,17},{9,16... | collective-permute-start | bytes 3080 | tf_op jit(solution)/shard_map/ppermute | solution.py:49
  48.9 1.0 %collective-permute-start.16 = (f32[1,256]{1,0:T(1,128)S(1)}, f32[1,256]{1,0:T(1,128)S(1)}, u32[]{:S(2)}, u32[]{:S(2)}) collective-permute-start(f32[1,256]{1,0:T(1,128)S(1)} %get-tuple-element.22), channel_id=1, source_target_pairs={{0,5},{1,4},{2,7},{3,6},{4,1},{5,0},{6,3},{7,2},{8,13},{9,12},{10,... | collective-permute-start | bytes 3080 | tf_op jit(solution)/shard_map/ppermute | solution.py:49
  49.9 0.6 %copy.7 = f32[1,2,4,128]{3,1,2,0:T(2,128)} copy(f32[1,2,4,128]{3,2,1,0:T(4,128)S(1)} %bitcast.5) | data formatting | bytes 8192
  50.5 2.7 %collective-permute-done.18 = f32[1,256]{1,0:T(1,128)S(1)} collective-permute-done((f32[1,256]{1,0:T(1,128)S(1)}, f32[1,256]{1,0:T(1,128)S(1)}, u32[]{:S(2)}, u32[]{:S(2)}) %collective-permute-start.18) | collective-permute-done | bytes 1056 | tf_op jit(solution)/shard_map/ppermute | solution.py:49
  53.7 0.6 %divide_log_fusion = f32[1,256]{1,0:T(1,128)} fusion(f32[1,256]{1,0:T(1,128)S(1)} %collective-permute-done.18, f32[1,256]{1,0:T(1,128)S(1)} %collective-permute-done.17, f32[1,256]{1,0:T(1,128)S(1)} %collective-permute-done.16, f32[8,256]{1,0:T(8,128)S(1)} %add.43, s32[]{:T(128)S(6)} %select_n.18), kind=kLoop, calls=%fused_computation | loop fusion | flops 1024 | bytes 5124 | tf_op jit(solution)/shard_map/log | solution.py:371
  (24 shorter events, 1.9 us)
Async XLA Ops:
  0.6 12.7 %collective-permute-start = (bf16[1024,256]{1,0:T(8,128)(2,1)}, bf16[1024,256]{1,0:T(8,128)(2,1)S(1)}, u32[]{:S(2)}, u32[]{:S(2)}) collective-permute-start(bf16[1024,256]{1,0:T(8,128)(2,1)} %own.1), channel_id=1, source_target_pairs={{0,1},{1,0},{2,3},{3,2},{4,5},{5,4},{6,7},{7,6},{8,9},{9,8},{10,11... | collective-permute-start | bytes 1572872 | tf_op jit(solution)/shard_map/ppermute | solution.py:62
  1.2 11.2 %collective-permute-start.2 = (bf16[256,256]{1,0:T(8,128)(2,1)}, bf16[256,256]{1,0:T(8,128)(2,1)S(1)}, u32[]{:S(2)}, u32[]{:S(2)}) collective-permute-start(bf16[256,256]{1,0:T(8,128)(2,1)} %target.1), channel_id=1, source_target_pairs={{0,3},{1,2},{2,1},{3,0},{4,7},{5,6},{6,5},{7,4},{8,11},{9,10},{10,... | collective-permute-start | bytes 393224 | tf_op jit(solution)/shard_map/ppermute | solution.py:49
  3.8 7.4 %collective-permute-start.5 = (bf16[256,256]{1,0:T(8,128)(2,1)}, bf16[256,256]{1,0:T(8,128)(2,1)S(1)}, u32[]{:S(2)}, u32[]{:S(2)}) collective-permute-start(bf16[256,256]{1,0:T(8,128)(2,1)} %target.1), channel_id=1, source_target_pairs={{0,25},{1,24},{2,27},{3,26},{4,29},{5,28},{6,31},{7,30},{8,1},{9,0... | collective-permute-start | bytes 393224 | tf_op jit(solution)/shard_map/ppermute | solution.py:49
  8.5 1.6 %collective-permute-start.1 = (s32[1,65]{1,0:T(1,128)S(1)}, s32[1,65]{1,0:T(1,128)S(1)}, u32[]{:S(2)}, u32[]{:S(2)}) collective-permute-start(s32[1,65]{1,0:T(1,128)S(1)} %pad_add_fusion.mine), channel_id=1, source_target_pairs={{0,1},{1,0},{2,3},{3,2},{4,5},{5,4},{6,7},{7,6},{8,9},{9,8},{10,11... | collective-permute-start | bytes 788 | tf_op jit(solution)/shard_map/ppermute | solution.py:62
  8.9 10.2 %collective-permute-start.3 = (bf16[256,256]{1,0:T(8,128)(2,1)}, bf16[256,256]{1,0:T(8,128)(2,1)S(1)}, u32[]{:S(2)}, u32[]{:S(2)}) collective-permute-start(bf16[256,256]{1,0:T(8,128)(2,1)} %target.1), channel_id=1, source_target_pairs={{0,5},{1,4},{2,7},{3,6},{4,1},{5,0},{6,3},{7,2},{8,13},{9,12},{10,... | collective-permute-start | bytes 393224 | tf_op jit(solution)/shard_map/ppermute | solution.py:49
  10.1 9.0 %collective-permute-start.4 = (bf16[256,256]{1,0:T(8,128)(2,1)}, bf16[256,256]{1,0:T(8,128)(2,1)S(1)}, u32[]{:S(2)}, u32[]{:S(2)}) collective-permute-start(bf16[256,256]{1,0:T(8,128)(2,1)} %target.1), channel_id=1, source_target_pairs={{0,6},{1,7},{2,4},{3,5},{4,2},{5,3},{6,0},{7,1},{8,14},{9,15},{10,... | collective-permute-start | bytes 393224 | tf_op jit(solution)/shard_map/ppermute | solution.py:49
  11.2 9.9 %collective-permute-start.6 = (bf16[256,256]{1,0:T(8,128)(2,1)S(1)}, bf16[256,256]{1,0:T(8,128)(2,1)S(1)}, u32[]{:S(2)}, u32[]{:S(2)}) collective-permute-start(bf16[256,256]{1,0:T(8,128)(2,1)S(1)} %collective-permute-done.5.refs_3_), channel_id=1, source_target_pairs={{0,3},{1,2},{2,1},{3,0},{4,7},{5,6},{6,5},{7,4},{8,11},{9,10},{10,... | collective-permute-start | bytes 393224 | tf_op jit(solution)/shard_map/ppermute | solution.py:49
  12.4 10.7 %collective-permute-start.7 = (bf16[256,256]{1,0:T(8,128)(2,1)S(1)}, bf16[256,256]{1,0:T(8,128)(2,1)S(1)}, u32[]{:S(2)}, u32[]{:S(2)}) collective-permute-start(bf16[256,256]{1,0:T(8,128)(2,1)S(1)} %collective-permute-done.5.refs_3_), channel_id=1, source_target_pairs={{0,5},{1,4},{2,7},{3,6},{4,1},{5,0},{6,3},{7,2},{8,13},{9,12},{10,... | collective-permute-start | bytes 393224 | tf_op jit(solution)/shard_map/ppermute | solution.py:49
  13.3 9.7 %collective-permute-start.8 = (bf16[256,256]{1,0:T(8,128)(2,1)S(1)}, bf16[256,256]{1,0:T(8,128)(2,1)S(1)}, u32[]{:S(2)}, u32[]{:S(2)}) collective-permute-start(bf16[256,256]{1,0:T(8,128)(2,1)S(1)} %collective-permute-done.5.refs_3_), channel_id=1, source_target_pairs={{0,6},{1,7},{2,4},{3,5},{4,2},{5,3},{6,0},{7,1},{8,14},{9,15},{10,... | collective-permute-start | bytes 393224 | tf_op jit(solution)/shard_map/ppermute | solution.py:49
  14.4 1.0 %copy-start = (bf16[1024,256]{1,0:T(8,128)(2,1)S(1)}, bf16[1024,256]{1,0:T(8,128)(2,1)}, u32[]{:S(2)}) copy-start(bf16[1024,256]{1,0:T(8,128)(2,1)} %own.1) | copy-start | bytes 1572868
  15.5 0.9 %copy-start.1 = (bf16[256,256]{1,0:T(8,128)(2,1)S(1)}, bf16[256,256]{1,0:T(8,128)(2,1)}, u32[]{:S(2)}) copy-start(bf16[256,256]{1,0:T(8,128)(2,1)} %target.1) | copy-start | bytes 393220
  24.6 1.4 %collective-permute-start.9 = (f32[8,256]{1,0:T(8,128)S(1)}, f32[8,256]{1,0:T(8,128)S(1)}, u32[]{:S(2)}, u32[]{:S(2)}) collective-permute-start(f32[8,256]{1,0:T(8,128)S(1)} %get-tuple-element.19.rows), channel_id=1, source_target_pairs={{0,1},{1,0},{2,3},{3,2},{4,5},{5,4},{6,7},{7,6},{8,9},{9,8},{10,11... | collective-permute-start | bytes 24584 | tf_op jit(solution)/shard_map/ppermute | solution.py:62
  27.7 3.1 %collective-permute-start.10 = (f32[8,256]{1,0:T(8,128)S(1)}, f32[8,256]{1,0:T(8,128)S(1)}, u32[]{:S(2)}, u32[]{:S(2)}) collective-permute-start(f32[8,256]{1,0:T(8,128)S(1)} %columns.2), channel_id=1, source_target_pairs={{0,3},{1,2},{2,1},{3,0},{4,7},{5,6},{6,5},{7,4},{8,11},{9,10},{10,... | collective-permute-start | bytes 24584 | tf_op jit(solution)/shard_map/ppermute | solution.py:49
  30.8 3.7 %collective-permute-start.11 = (f32[8,256]{1,0:T(8,128)S(1)}, f32[8,256]{1,0:T(8,128)S(1)}, u32[]{:S(2)}, u32[]{:S(2)}) collective-permute-start(f32[8,256]{1,0:T(8,128)S(1)} %add.41), channel_id=1, source_target_pairs={{0,5},{1,4},{2,7},{3,6},{4,1},{5,0},{6,3},{7,2},{8,13},{9,12},{10,... | collective-permute-start | bytes 24584 | tf_op jit(solution)/shard_map/ppermute | solution.py:49
  34.5 4.8 %collective-permute-start.12 = (f32[4,256]{1,0:T(4,128)S(1)}, f32[4,256]{1,0:T(4,128)S(1)}, u32[]{:S(2)}, u32[]{:S(2)}) collective-permute-start(f32[4,256]{1,0:T(4,128)S(1)} %get-tuple-element.26), channel_id=1, source_target_pairs={{0,9},{1,8},{2,11},{3,10},{4,13},{5,12},{6,15},{7,14},{8,17},{9,16... | collective-permute-start | bytes 12296 | tf_op jit(solution)/shard_map/ppermute | solution.py:49
  34.5 4.9 %collective-permute-start.13 = (f32[4,256]{1,0:T(4,128)S(1)}, f32[4,256]{1,0:T(4,128)S(1)}, u32[]{:S(2)}, u32[]{:S(2)}) collective-permute-start(f32[4,256]{1,0:T(4,128)S(1)} %get-tuple-element.25), channel_id=1, source_target_pairs={{0,25},{1,24},{2,27},{3,26},{4,29},{5,28},{6,31},{7,30},{8,1},{9,0... | collective-permute-start | bytes 12296 | tf_op jit(solution)/shard_map/ppermute | solution.py:49
  40.8 1.2 %collective-permute-start.14 = (f32[8,256]{1,0:T(8,128)S(1)}, f32[8,256]{1,0:T(8,128)S(1)}, u32[]{:S(2)}, u32[]{:S(2)}) collective-permute-start(f32[8,256]{1,0:T(8,128)S(1)} %rows.1), channel_id=1, source_target_pairs={{0,1},{1,0},{2,3},{3,2},{4,5},{5,4},{6,7},{7,6},{8,9},{9,8},{10,11... | collective-permute-start | bytes 24584 | tf_op jit(solution)/shard_map/ppermute | solution.py:62
  43.7 3.1 %collective-permute-start.15 = (f32[8,256]{1,0:T(8,128)S(1)}, f32[8,256]{1,0:T(8,128)S(1)}, u32[]{:S(2)}, u32[]{:S(2)}) collective-permute-start(f32[8,256]{1,0:T(8,128)S(1)} %get-tuple-element.21), channel_id=1, source_target_pairs={{0,3},{1,2},{2,1},{3,0},{4,7},{5,6},{6,5},{7,4},{8,11},{9,10},{10,... | collective-permute-start | bytes 24584 | tf_op jit(solution)/shard_map/ppermute | solution.py:49
  46.9 6.3 %collective-permute-start.18 = (f32[1,256]{1,0:T(1,128)S(1)}, f32[1,256]{1,0:T(1,128)S(1)}, u32[]{:S(2)}, u32[]{:S(2)}) collective-permute-start(f32[1,256]{1,0:T(1,128)S(1)} %get-tuple-element.23), channel_id=1, source_target_pairs={{0,12},{1,13},{2,14},{3,15},{4,8},{5,9},{6,10},{7,11},{8,20},{9,21... | collective-permute-start | bytes 3080 | tf_op jit(solution)/shard_map/ppermute | solution.py:49
  46.9 6.8 %collective-permute-start.17 = (f32[1,256]{1,0:T(1,128)S(1)}, f32[1,256]{1,0:T(1,128)S(1)}, u32[]{:S(2)}, u32[]{:S(2)}) collective-permute-start(f32[1,256]{1,0:T(1,128)S(1)} %get-tuple-element.24), channel_id=1, source_target_pairs={{0,9},{1,8},{2,11},{3,10},{4,13},{5,12},{6,15},{7,14},{8,17},{9,16... | collective-permute-start | bytes 3080 | tf_op jit(solution)/shard_map/ppermute | solution.py:49
  48.9 4.8 %collective-permute-start.16 = (f32[1,256]{1,0:T(1,128)S(1)}, f32[1,256]{1,0:T(1,128)S(1)}, u32[]{:S(2)}, u32[]{:S(2)}) collective-permute-start(f32[1,256]{1,0:T(1,128)S(1)} %get-tuple-element.22), channel_id=1, source_target_pairs={{0,5},{1,4},{2,7},{3,6},{4,1},{5,0},{6,3},{7,2},{8,13},{9,12},{10,... | collective-permute-start | bytes 3080 | tf_op jit(solution)/shard_map/ppermute | solution.py:49

commit v2 on v1

--- a/solution.py
+++ b/solution.py
@@ -16,12 +16,12 @@
 LANES = 128
 MIB = 2**20
 GROUP = 4
+FIELD = 256
 
 
 BOTH = ("group", "member")
 VM = pl.BlockSpec(memory_space=pltpu.VMEM)
 SM = pl.BlockSpec(memory_space=pltpu.SMEM)
-HB = pl.BlockSpec(memory_space=pltpu.HBM)
 F32 = jnp.float32
 BF16 = jnp.bfloat16
 FACTOR = math.log2(math.e) / REGULARIZER
@@ -31,11 +31,28 @@
     return bin(bits).count("1") % 2
 
 
-def odd_traced(value, width):
-    result = jnp.int32(0)
-    for b in range(width):
+def odd_traced(value, size):
+    result = value
+    for b in range(1, size.bit_length()):
         result = result ^ (value >> b)
     return result & 1
+
+
+def coded(pair_source, pair_target, pair_count, members, even):
+    chip = lax.axis_index("member") // CORES
+    beyond = (pair_target >= members).astype(jnp.int32)
+    place = pair_target - beyond * members
+    kind = odd_traced(place, members) ^ (beyond & even)
+    late = beyond * (place // CORES != chip).astype(jnp.int32)
+    slots = pair_source.shape[1]
+    listed = (jnp.arange(slots, dtype=jnp.int32)[None] < pair_count[:, None]).astype(jnp.int32)
+    entry = pair_source + (pair_target // CORES) * FIELD
+    code = kind + 2 * late + 4 * listed + 8 * entry
+    return jnp.concatenate([code, pair_count[:, None]], 1)
+
+
+def entry_of(code):
+    return code & (FIELD - 1), code // FIELD
 
 
 def up_to_group(count):
@@ -71,9 +88,8 @@
 
 def unit(values):
     floats = values.astype(F32)
-    return (floats / jnp.sqrt(jnp.sum(floats * floats, axis=1, keepdims=True) + EPSILON)).astype(
-        BF16
-    )
+    length = jnp.sqrt(jnp.sum(floats * floats, axis=1, keepdims=True) + EPSILON)
+    return (floats * (1.0 / length)).astype(BF16)
 
 
 def rows_out(acc, out):
@@ -93,56 +109,34 @@
     acc[s] += total
 
 
-def prepare_kernel(
-    chips, slots, even, own, target, other, mine, theirs, units, home, first, second, raw, tile, done
-):
+def prepare_kernel(own, target, other, mine, theirs, units, home, first, second):
     cells = units.shape[1]
     tiles = own.shape[0] // cells
-    fetch = pltpu.make_async_copy(own, raw, done.at[0])
-    fetch_home = pltpu.make_async_copy(target, tile, done.at[1])
-    fetch.start()
-    fetch_home.start()
-    members = CORES * chips
-    width = members.bit_length()
-    member = lax.axis_index("member")
-    chip = member // CORES
-    kind = odd_traced(member, width)
+    slots = mine.shape[1] - 1
+    kind = odd_traced(lax.axis_index("member"), lax.axis_size("member"))
     counts = (jnp.int32(0), jnp.int32(0))
     for half, info in enumerate((mine, theirs)):
 
-        def slot(k, counts, half=half, info=info):
+        def step(m, counts, half=half, info=info):
             early, late = counts
-            label = info[0, slots + k]
-            w = label // CORES
-            beyond = (label >= members).astype(jnp.int32)
-            place = lax.rem(label, members)
-            here = (odd_traced(place, width) ^ (beyond & even)) == kind
-            is_late = jnp.logical_and(beyond == 1, place // CORES != chip)
-            s = half * tiles + info[0, k]
-            to_early = jnp.logical_and(here, jnp.logical_not(is_late))
-            to_late = jnp.logical_and(here, is_late)
-
-            @pl.when(to_early)
-            def _():
-                first[1 + 2 * early] = s
-                first[2 + 2 * early] = w
-
-            @pl.when(to_late)
-            def _():
-                second[1 + 2 * late] = s
-                second[2 + 2 * late] = w
-
-            return early + to_early.astype(jnp.int32), late + to_late.astype(jnp.int32)
-
-        counts = lax.fori_loop(0, info[0, 2 * slots], slot, counts)
+            for i in range(math.gcd(slots, GROUP)):
+                code = info[0, m * math.gcd(slots, GROUP) + i]
+                hit = ((code & 5) == (4 | kind)).astype(jnp.int32)
+                is_late = (code >> 1) & 1
+                entry = (code >> 3) + half * tiles
+                first[1 + early] = entry
+                second[1 + late] = entry
+                late_hit = hit & is_late
+                early, late = early + hit - late_hit, late + late_hit
+            return early, late
+
+        group = math.gcd(slots, GROUP)
+        counts = lax.fori_loop(0, (info[0, slots] + group - 1) // group, step, counts)
     first[0], second[0] = counts
     for s in range(tiles):
+        units[s] = unit(own[s * cells : (s + 1) * cells])
         units[tiles + s] = unit(other[s * cells : (s + 1) * cells])
-    fetch.wait()
-    for s in range(tiles):
-        units[s] = unit(raw[s * cells : (s + 1) * cells])
-    fetch_home.wait()
-    home[...] = unit(tile[...])
+    home[...] = unit(target[...])
 
 
 def build_pairs(units, window, table, factors, acc, where):
@@ -154,7 +148,7 @@
             n = m * GROUP + i
             real = n < found
             at = jnp.where(real, n, 0)
-            s, w = table[1 + 2 * at], table[2 + 2 * at]
+            s, w = entry_of(table[1 + at])
             logits = lax.dot_general(
                 units[s], window[where(w)], (((1,), (1,)), ((), ())), preferred_element_type=F32
             )
@@ -198,7 +192,7 @@
     for factors, table in ((first, lists_first), (second, lists_second)):
 
         def pair(n, carry, factors=factors, table=table):
-            s, w = table[1 + 2 * n], table[2 + 2 * n]
+            s, w = entry_of(table[1 + n])
             add_halves(acc, s, factors[n].astype(F32) * scale[pl.ds(w, 1), :])
             return carry
 
@@ -217,24 +211,29 @@
     scale = 1.0 / total
     if last:
         logs[...] = jnp.log(scale[:tiles] * float(cells))
-    flipped = jnp.transpose(scale)
     for s in range(CORES * tiles):
-        spread[s] = jnp.broadcast_to(flipped[:, s : s + 1], (cells, LANES))
+        spread[s] = jnp.transpose(jnp.broadcast_to(scale[s : s + 1], (LANES, cells)))
     acc[...] = jnp.zeros_like(acc)
+    spare = acc.shape[0] - 1
     for factors, table in ((first, lists_first), (second, lists_second)):
-
-        def pair(n, carry, factors=factors, table=table):
-            s, w = table[1 + 2 * n], table[2 + 2 * n]
-            values = factors[n].astype(F32)
-            for j in range(cells // LANES):
-                part = values[:, j * LANES : (j + 1) * LANES] * spread[s]
-                acc[w, :, j * LANES : (j + 1) * LANES] += jnp.sum(
-                    part.reshape(cells // 8, 8, LANES), axis=0
-                )
+        found = table[0]
+
+        def step(m, carry, factors=factors, table=table, found=found):
+            for i in range(GROUP):
+                n = m * GROUP + i
+                real = n < found
+                s, w = entry_of(table[1 + jnp.where(real, n, 0)])
+                w = jnp.where(real, w, spare)
+                values = factors[n].astype(F32)
+                for j in range(cells // LANES):
+                    part = values[:, j * LANES : (j + 1) * LANES] * spread[s]
+                    acc[w, :, j * LANES : (j + 1) * LANES] += jnp.sum(
+                        part.reshape(cells // 8, 8, LANES), axis=0
+                    )
             return carry
 
-        lax.fori_loop(0, table[0], pair, 0)
-    columns[...] = jnp.sum(acc[...], axis=1)
+        lax.fori_loop(0, (found + GROUP - 1) // GROUP, step, 0)
+    columns[...] = jnp.sum(acc[:spare], axis=1)
 
 
 def step(source, target, pair_source, pair_target, pair_count):
@@ -251,8 +250,11 @@
     beyond = hop(target, 1, 0)
     own_tiles = spread_tiles(target, chips)
     next_tiles = spread_tiles(beyond, chips)
-    info = jnp.concatenate([pair_source, pair_target, pair_count[:, None]], 1)
+    info = coded(pair_source, pair_target, pair_count, members, even)
     partner_source = partner(source)
+    stay = [(i, i) for i in range(members)]
+    own_source = lax.ppermute(source, "member", stay)
+    own_target = lax.ppermute(target, "member", stay)
     partner_info = partner(info)
 
     def shaped(*dims, kind=F32):
@@ -271,26 +273,21 @@
     tile = cells * width * 2
     lanes_acc = (both, cells, LANES)
     prepare = pl.pallas_call(
-        functools.partial(prepare_kernel, chips, slots, even),
+        prepare_kernel,
         out_shape=(
             shaped(both, cells, width, kind=BF16),
             shaped(cells, width, kind=BF16),
-            shaped(1 + 2 * most_first, kind=jnp.int32),
-            shaped(1 + 2 * most_second, kind=jnp.int32),
+            shaped(2 + most_first, kind=jnp.int32),
+            shaped(2 + most_second, kind=jnp.int32),
         ),
-        in_specs=[HB, HB, VM, SM, SM],
+        in_specs=[VM, VM, VM, SM, SM],
         out_specs=(VM, VM, SM, SM),
-        scratch_shapes=[
-            pltpu.VMEM(source.shape, BF16),
-            pltpu.VMEM(target.shape, BF16),
-            pltpu.SemaphoreType.DMA((2,)),
-        ],
         compiler_params=limit(4 * MIB),
         cost_estimate=cost(both),
         name="prepare",
     )
     units, home, lists_first, lists_second = prepare(
-        source, target, partner_source, info, partner_info
+        own_source, own_target, partner_source, info, partner_info
     )
 
     early = own_tiles[1:] + [next_tiles[0]]
@@ -341,7 +338,7 @@
             out_specs=(VM,) + ((VM,) if last else ()),
             scratch_shapes=[
                 pltpu.VMEM(lanes_acc, F32),
-                pltpu.VMEM((2 * chips, 8, cells), F32),
+                pltpu.VMEM((2 * chips + 1, 8, cells), F32),
             ],
             compiler_params=held_limit,
             name="columns",

time: 54.5 us -> 56.6 us (1.039)
  waiting for transfers between devices: 15.4 us -> 19.8 us
  local copies, waits for them, and re-layouts: 2.56 us -> 0.61 us
  Pallas kernels: 11 us -> 9.52 us
  starting transfers between devices: 22.6 us -> 23.7 us
    ppermute x15, waiting for transfers between devices: 13.5 us -> 16.8 us  [hop(): lax.ppermute(x, BOTH, [(g * members + m, (g - up) % groups * members + (m...]
    ppermute x0 -> x2, starting transfers between devices: none -> 1.95 us  [the longest x1 1.04 us: step(): own_source = lax.ppermute(source, 'member', stay)]
    unnamed x5 -> x1, local copies, waits for them, and re-layouts: 2.54 us -> 0.59 us
    pallas_call x1, Pallas kernels: 2.69 us -> 1.55 us  [step(): prepare(own_source, own_target, partner_source, info, partner_info)]
    ppermute x4, waiting for transfers between devices: 1.85 us -> 2.98 us  [partner(): return lax.ppermute(x, 'member', [(i, i ^ 1) for i in range(size)])]
    add x0 -> x1, other arithmetic: none -> 0.69 us  [coded(): code = kind + 2 * late + 4 * listed + 8 * entry]
    concatenate x1, other arithmetic: 0.75 us -> 0.08 us  [coded(): return jnp.concatenate([code, pair_count[:, None]], 1)]
  transfers between devices with their start and end apart: 19 -> 21, of which waited for: 9 -> 12; matrix products, arithmetic and copies ran while one was open for 2% -> 2% of each run, Pallas kernels for 9% -> 6%
where the time goes in v2:
time: 56.6 us; the launch traced here: 56.4 us
  starting transfers between devices  23.7 us (42%)
  waiting for transfers between devices  19.8 us (35%)
  Pallas kernels  9.52 us (17%)
  between operations  1.4 us (2%)
  other arithmetic  1.36 us (2%)
  local copies, waits for them, and re-layouts  0.61 us (1%)
    ppermute x15, starting transfers between devices, hop(): lax.ppermute(x, BOTH, [(g * members + m, (g - up) % groups * members + (m...  20.3 us
    ppermute x15, waiting for transfers between devices, hop(): lax.ppermute(x, BOTH, [(g * members + m, (g - up) % groups * members + (m...  16.8 us
    ppermute x4, waiting for transfers between devices, partner(): return lax.ppermute(x, 'member', [(i, i ^ 1) for i in range(size)])  2.98 us
    pallas_call x2, Pallas kernels, step(): pl.pallas_call(functools.partial(column_kernel, last), out_shape=(shaped(...  2.88 us
    pallas_call x1, Pallas kernels, step(): first, acc = first_call(units, lists_first, home, *early)  2.03 us
    pallas_call x1, Pallas kernels, step(): pl.pallas_call(functools.partial(second_kernel, chips), out_shape=(shaped...  1.57 us
    pallas_call x1, Pallas kernels, step(): prepare(own_source, own_target, partner_source, info, partner_info)  1.55 us
    pallas_call x1, Pallas kernels, step(): pl.pallas_call(row_kernel, out_shape=shaped(both, cells), in_specs=[VM, V...  1.49 us
  transfers between devices with their start and end apart: 21, of which 12 were waited for; matrix products, arithmetic and copies ran while one was open for 2% of the time, Pallas kernels for 6%

profile of v2, /device:TPU:0, one launch (start us, length us, event | category | flops | bytes accessed | tf_op | source)
XLA Modules:
  0.0 56.4 jit_solution(11355542584610032526)
XLA Ops:
  0.6 1.0 %collective-permute-start = (bf16[1024,256]{1,0:T(8,128)(2,1)}, bf16[1024,256]{1,0:T(8,128)(2,1)S(1)}, u32[]{:S(2)}, u32[]{:S(2)}) collective-permute-start(bf16[1024,256]{1,0:T(8,128)(2,1)} %param.5), channel_id=1, source_target_pairs={{0,0},{1,1},{2,2},{3,3},{4,4},{5,5},{6,6},{7,7},{8,8},{9,9},{10,10... | collective-permute-start | bytes 1572872 | tf_op jit(solution)/shard_map/ppermute | solution.py:256
  2.2 0.9 %collective-permute-start.1 = (bf16[256,256]{1,0:T(8,128)(2,1)}, bf16[256,256]{1,0:T(8,128)(2,1)S(1)}, u32[]{:S(2)}, u32[]{:S(2)}) collective-permute-start(bf16[256,256]{1,0:T(8,128)(2,1)} %param.6), channel_id=1, source_target_pairs={{0,0},{1,1},{2,2},{3,3},{4,4},{5,5},{6,6},{7,7},{8,8},{9,9},{10,10... | collective-permute-start | bytes 393224 | tf_op jit(solution)/shard_map/ppermute | solution.py:257
  3.1 2.6 %collective-permute-start.4 = (bf16[256,256]{1,0:T(8,128)(2,1)}, bf16[256,256]{1,0:T(8,128)(2,1)S(1)}, u32[]{:S(2)}, u32[]{:S(2)}) collective-permute-start(bf16[256,256]{1,0:T(8,128)(2,1)} %param.6), channel_id=1, source_target_pairs={{0,3},{1,2},{2,1},{3,0},{4,7},{5,6},{6,5},{7,4},{8,11},{9,10},{10,... | collective-permute-start | bytes 393224 | tf_op jit(solution)/shard_map/ppermute | solution.py:66
  6.3 0.7 %fusion.6 = s32[1,32]{1,0:T(1,128)S(1)} fusion(s32[1,32]{1,0:T(1,128)} %param.7, s32[1,32]{1,0:T(1,128)} %param.8, s32[]{:T(128)} %bitcast.5, s32[]{:T(128)S(6)} %select_n.27), kind=kLoop, calls=%fused_computation.23 | loop fusion | flops 1728 | bytes 392 | tf_op jit(solution)/shard_map/add | solution.py:50
  7.1 1.1 %collective-permute-done.3.theirs = s32[1,33]{1,0:T(1,128)S(1)} collective-permute-done((s32[1,33]{1,0:T(1,128)S(1)}, s32[1,33]{1,0:T(1,128)S(1)}, u32[]{:S(2)}, u32[]{:S(2)}) %collective-permute-start.3) | collective-permute-done | bytes 164 | tf_op jit(solution)/shard_map/ppermute | solution.py:79
  8.3 3.4 %collective-permute-start.7 = (bf16[256,256]{1,0:T(8,128)(2,1)}, bf16[256,256]{1,0:T(8,128)(2,1)S(1)}, u32[]{:S(2)}, u32[]{:S(2)}) collective-permute-start(bf16[256,256]{1,0:T(8,128)(2,1)} %param.6), channel_id=1, source_target_pairs={{0,25},{1,24},{2,27},{3,26},{4,29},{5,28},{6,31},{7,30},{8,1},{9,0... | collective-permute-start | bytes 393224 | tf_op jit(solution)/shard_map/ppermute | solution.py:66
  11.6 1.5 %collective-permute-start.5 = (bf16[256,256]{1,0:T(8,128)(2,1)}, bf16[256,256]{1,0:T(8,128)(2,1)S(1)}, u32[]{:S(2)}, u32[]{:S(2)}) collective-permute-start(bf16[256,256]{1,0:T(8,128)(2,1)} %param.6), channel_id=1, source_target_pairs={{0,5},{1,4},{2,7},{3,6},{4,1},{5,0},{6,3},{7,2},{8,13},{9,12},{10,... | collective-permute-start | bytes 393224 | tf_op jit(solution)/shard_map/ppermute | solution.py:66
  13.6 1.9 %collective-permute-done.7.refs_3_ = bf16[256,256]{1,0:T(8,128)(2,1)S(1)} collective-permute-done((bf16[256,256]{1,0:T(8,128)(2,1)}, bf16[256,256]{1,0:T(8,128)(2,1)S(1)}, u32[]{:S(2)}, u32[]{:S(2)}) %collective-permute-start.7) | collective-permute-done | bytes 131104 | tf_op jit(solution)/shard_map/ppermute | solution.py:66
  15.5 1.8 %collective-permute-start.9 = (bf16[256,256]{1,0:T(8,128)(2,1)S(1)}, bf16[256,256]{1,0:T(8,128)(2,1)S(1)}, u32[]{:S(2)}, u32[]{:S(2)}) collective-permute-start(bf16[256,256]{1,0:T(8,128)(2,1)S(1)} %collective-permute-done.7.refs_3_), channel_id=1, source_target_pairs={{0,5},{1,4},{2,7},{3,6},{4,1},{5,0},{6,3},{7,2},{8,13},{9,12},{10,... | collective-permute-start | bytes 393224 | tf_op jit(solution)/shard_map/ppermute | solution.py:66
  17.3 1.4 %collective-permute-start.10 = (bf16[256,256]{1,0:T(8,128)(2,1)S(1)}, bf16[256,256]{1,0:T(8,128)(2,1)S(1)}, u32[]{:S(2)}, u32[]{:S(2)}) collective-permute-start(bf16[256,256]{1,0:T(8,128)(2,1)S(1)} %collective-permute-done.7.refs_3_), channel_id=1, source_target_pairs={{0,6},{1,7},{2,4},{3,5},{4,2},{5,3},{6,0},{7,1},{8,14},{9,15},{10,... | collective-permute-start | bytes 393224 | tf_op jit(solution)/shard_map/ppermute | solution.py:66
  18.7 1.5 %prepare.1 = (bf16[8,256,256]{2,1,0:T(8,128)(2,1)S(1)}, bf16[256,256]{1,0:T(8,128)(2,1)S(1)}, s32[42]{0:T(128)S(1)}, s32[26]{0:T(128)S(1)}) custom-call(bf16[1024,256]{1,0:T(8,128)(2,1)S(1)} %collective-permute-done.own, bf16[256,256]{1,0:T(8,128)(2,1)S(1)} %collective-permute-done.1.target, bf16[1024,256]{1,0:T(8,128)(2,1)S(1)} %collective-permute-done.2.other, ...), custom_call_target="tpu_custom_call" | custom-call | flops 268435456 | bytes 1048576 | tf_op jit(solution)/shard_map/prepare/pallas_call | solution.py:289
  20.3 2.0 %first.1 = (bf16[40,256,256]{2,1,0:T(8,128)(2,1)S(1)}, f32[9,256,128]{2,1,0:T(8,128)S(1)}) custom-call(bf16[8,256,256]{2,1,0:T(8,128)(2,1)S(1)} %get-tuple-element.12.units, s32[42]{0:T(128)S(1)} %get-tuple-element.13.table.lists_first, bf16[256,256]{1,0:T(8,128)(2,1)S(1)} %get-tuple-element.14.home, bf16[256,256]{1,0:T(8,128)(2,1)S(1)} %collective-permute-done.4.refs_0_, ...), custom_call_target="tpu_custom_call" | custom-call | flops 1342177280 | bytes 5242880 | tf_op jit(solution)/shard_map/first/pallas_call | solution.py:305
  22.3 2.8 %collective-permute-done.9.refs_1_ = bf16[256,256]{1,0:T(8,128)(2,1)S(1)} collective-permute-done((bf16[256,256]{1,0:T(8,128)(2,1)S(1)}, bf16[256,256]{1,0:T(8,128)(2,1)S(1)}, u32[]{:S(2)}, u32[]{:S(2)}) %collective-permute-start.9) | collective-permute-done | bytes 131104 | tf_op jit(solution)/shard_map/ppermute | solution.py:66
  25.5 1.6 %second.1 = (bf16[24,256,256]{2,1,0:T(8,128)(2,1)S(1)}, f32[8,256]{1,0:T(8,128)S(1)}) custom-call(bf16[8,256,256]{2,1,0:T(8,128)(2,1)S(1)} %get-tuple-element.12.units, s32[26]{0:T(128)S(1)} %get-tuple-element.16.table.lists_second, f32[9,256,128]{2,1,0:T(8,128)S(1)} %get-tuple-element.17.before, bf16[256,256]{1,0:T(8,128)(2,1)S(1)} %collective-permute-done.8.refs_0_, ...), custom_call_target="tpu_custom_call" | custom-call | flops 805306368 | bytes 3145728 | tf_op jit(solution)/shard_map/second/pallas_call | solution.py:306
  27.1 0.8 %collective-permute-start.11 = (f32[8,256]{1,0:T(8,128)S(1)}, f32[8,256]{1,0:T(8,128)S(1)}, u32[]{:S(2)}, u32[]{:S(2)}) collective-permute-start(f32[8,256]{1,0:T(8,128)S(1)} %get-tuple-element.19.rows), channel_id=1, source_target_pairs={{0,1},{1,0},{2,3},{3,2},{4,5},{5,4},{6,7},{7,6},{8,9},{9,8},{10,11... | collective-permute-start | bytes 24584 | tf_op jit(solution)/shard_map/ppermute | solution.py:79
  27.9 0.8 %collective-permute-done.11.arrived = f32[8,256]{1,0:T(8,128)S(1)} collective-permute-done((f32[8,256]{1,0:T(8,128)S(1)}, f32[8,256]{1,0:T(8,128)S(1)}, u32[]{:S(2)}, u32[]{:S(2)}) %collective-permute-start.11) | collective-permute-done | bytes 8224 | tf_op jit(solution)/shard_map/ppermute | solution.py:79
  28.7 1.4 %columns.2 = f32[8,256]{1,0:T(8,128)S(1)} custom-call(bf16[40,256,256]{2,1,0:T(8,128)(2,1)S(1)} %get-tuple-element.15.first, bf16[24,256,256]{2,1,0:T(8,128)(2,1)S(1)} %get-tuple-element.18.second, s32[42]{0:T(128)S(1)} %get-tuple-element.13.table.lists_first, s32[26]{0:T(128)S(1)} %get-tuple-element.16.table.lists_second, ...), custom_call_target="tpu_custom_call" | custom-call | tf_op jit(solution)/shard_map/columns/pallas_call | solution.py:334
  30.4 2.9 %collective-permute-done.12 = f32[8,256]{1,0:T(8,128)S(1)} collective-permute-done((f32[8,256]{1,0:T(8,128)S(1)}, f32[8,256]{1,0:T(8,128)S(1)}, u32[]{:S(2)}, u32[]{:S(2)}) %collective-permute-start.12) | collective-permute-done | bytes 8224 | tf_op jit(solution)/shard_map/ppermute | solution.py:66
  33.3 2.2 %collective-permute-start.13 = (f32[8,256]{1,0:T(8,128)S(1)}, f32[8,256]{1,0:T(8,128)S(1)}, u32[]{:S(2)}, u32[]{:S(2)}) collective-permute-start(f32[8,256]{1,0:T(8,128)S(1)} %add.59), channel_id=1, source_target_pairs={{0,5},{1,4},{2,7},{3,6},{4,1},{5,0},{6,3},{7,2},{8,13},{9,12},{10,... | collective-permute-start | bytes 24584 | tf_op jit(solution)/shard_map/ppermute | solution.py:66
  35.5 1.4 %collective-permute-done.13 = f32[8,256]{1,0:T(8,128)S(1)} collective-permute-done((f32[8,256]{1,0:T(8,128)S(1)}, f32[8,256]{1,0:T(8,128)S(1)}, u32[]{:S(2)}, u32[]{:S(2)}) %collective-permute-start.13) | collective-permute-done | bytes 8224 | tf_op jit(solution)/shard_map/ppermute | solution.py:66
  36.9 3.5 %collective-permute-start.15 = (f32[4,256]{1,0:T(4,128)S(1)}, f32[4,256]{1,0:T(4,128)S(1)}, u32[]{:S(2)}, u32[]{:S(2)}) collective-permute-start(f32[4,256]{1,0:T(4,128)S(1)} %get-tuple-element.25), channel_id=1, source_target_pairs={{0,25},{1,24},{2,27},{3,26},{4,29},{5,28},{6,31},{7,30},{8,1},{9,0... | collective-permute-start | bytes 12296 | tf_op jit(solution)/shard_map/ppermute | solution.py:66
  40.5 1.3 %collective-permute-done.14.before = f32[4,256]{1,0:T(4,128)S(1)} collective-permute-done((f32[4,256]{1,0:T(4,128)S(1)}, f32[4,256]{1,0:T(4,128)S(1)}, u32[]{:S(2)}, u32[]{:S(2)}) %collective-permute-start.14) | collective-permute-done | bytes 4128 | tf_op jit(solution)/shard_map/ppermute | solution.py:66
  41.8 1.5 %rows.1 = f32[8,256]{1,0:T(8,128)S(1)} custom-call(bf16[40,256,256]{2,1,0:T(8,128)(2,1)S(1)} %get-tuple-element.15.first, bf16[24,256,256]{2,1,0:T(8,128)(2,1)S(1)} %get-tuple-element.18.second, s32[42]{0:T(128)S(1)} %get-tuple-element.13.table.lists_first, s32[26]{0:T(128)S(1)} %get-tuple-element.16.table.lists_second, f32[8,256]{1,0:T(8,128)S(1)} %add.60.columns, ...), custom_call_target="tpu_custom_call" | custom-call | tf_op jit(solution)/shard_map/rows/pallas_call | solution.py:325
  43.5 1.0 %collective-permute-done.16.arrived = f32[8,256]{1,0:T(8,128)S(1)} collective-permute-done((f32[8,256]{1,0:T(8,128)S(1)}, f32[8,256]{1,0:T(8,128)S(1)}, u32[]{:S(2)}, u32[]{:S(2)}) %collective-permute-start.16) | collective-permute-done | bytes 8224 | tf_op jit(solution)/shard_map/ppermute | solution.py:79
  44.5 1.4 %columns.3 = (f32[8,256]{1,0:T(8,128)S(1)}, f32[4,256]{1,0:T(4,128)S(1)}) custom-call(bf16[40,256,256]{2,1,0:T(8,128)(2,1)S(1)} %get-tuple-element.15.first, bf16[24,256,256]{2,1,0:T(8,128)(2,1)S(1)} %get-tuple-element.18.second, s32[42]{0:T(128)S(1)} %get-tuple-element.13.table.lists_first, s32[26]{0:T(128)S(1)} %get-tuple-element.16.table.lists_second, ...), custom_call_target="tpu_custom_call" | custom-call | tf_op jit(solution)/shard_map/columns/pallas_call | solution.py:334
  46.0 3.0 %collective-permute-done.17 = f32[8,256]{1,0:T(8,128)S(1)} collective-permute-done((f32[8,256]{1,0:T(8,128)S(1)}, f32[8,256]{1,0:T(8,128)S(1)}, u32[]{:S(2)}, u32[]{:S(2)}) %collective-permute-start.17) | collective-permute-done | bytes 8224 | tf_op jit(solution)/shard_map/ppermute | solution.py:66
  49.1 0.7 %collective-permute-start.20 = (f32[1,256]{1,0:T(1,128)S(1)}, f32[1,256]{1,0:T(1,128)S(1)}, u32[]{:S(2)}, u32[]{:S(2)}) collective-permute-start(f32[1,256]{1,0:T(1,128)S(1)} %get-tuple-element.23), channel_id=1, source_target_pairs={{0,12},{1,13},{2,14},{3,15},{4,8},{5,9},{6,10},{7,11},{8,20},{9,21... | collective-permute-start | bytes 3080 | tf_op jit(solution)/shard_map/ppermute | solution.py:66
  49.8 1.3 %collective-permute-start.19 = (f32[1,256]{1,0:T(1,128)S(1)}, f32[1,256]{1,0:T(1,128)S(1)}, u32[]{:S(2)}, u32[]{:S(2)}) collective-permute-start(f32[1,256]{1,0:T(1,128)S(1)} %get-tuple-element.24), channel_id=1, source_target_pairs={{0,9},{1,8},{2,11},{3,10},{4,13},{5,12},{6,15},{7,14},{8,17},{9,16... | collective-permute-start | bytes 3080 | tf_op jit(solution)/shard_map/ppermute | solution.py:66
  51.1 1.1 %collective-permute-start.18 = (f32[1,256]{1,0:T(1,128)S(1)}, f32[1,256]{1,0:T(1,128)S(1)}, u32[]{:S(2)}, u32[]{:S(2)}) collective-permute-start(f32[1,256]{1,0:T(1,128)S(1)} %get-tuple-element.22), channel_id=1, source_target_pairs={{0,5},{1,4},{2,7},{3,6},{4,1},{5,0},{6,3},{7,2},{8,13},{9,12},{10,... | collective-permute-start | bytes 3080 | tf_op jit(solution)/shard_map/ppermute | solution.py:66
  52.2 0.6 %copy.7 = f32[1,2,4,128]{3,1,2,0:T(2,128)} copy(f32[1,2,4,128]{3,2,1,0:T(4,128)S(1)} %bitcast.7) | data formatting | bytes 8192
  52.8 2.6 %collective-permute-done.20 = f32[1,256]{1,0:T(1,128)S(1)} collective-permute-done((f32[1,256]{1,0:T(1,128)S(1)}, f32[1,256]{1,0:T(1,128)S(1)}, u32[]{:S(2)}, u32[]{:S(2)}) %collective-permute-start.20) | collective-permute-done | bytes 1056 | tf_op jit(solution)/shard_map/ppermute | solution.py:66
  55.9 0.6 %divide_log_fusion = f32[1,256]{1,0:T(1,128)} fusion(f32[1,256]{1,0:T(1,128)S(1)} %collective-permute-done.20, f32[1,256]{1,0:T(1,128)S(1)} %collective-permute-done.19, f32[1,256]{1,0:T(1,128)S(1)} %collective-permute-done.18, f32[8,256]{1,0:T(8,128)S(1)} %add.61, s32[]{:T(128)S(6)} %select_n.29), kind=kLoop, calls=%fused_computation.12 | loop fusion | flops 1024 | bytes 5124 | tf_op jit(solution)/shard_map/log | solution.py:368
  (25 shorter events, 2.6 us)
Async XLA Ops:
  0.6 14.9 %collective-permute-start = (bf16[1024,256]{1,0:T(8,128)(2,1)}, bf16[1024,256]{1,0:T(8,128)(2,1)S(1)}, u32[]{:S(2)}, u32[]{:S(2)}) collective-permute-start(bf16[1024,256]{1,0:T(8,128)(2,1)} %param.5), channel_id=1, source_target_pairs={{0,0},{1,1},{2,2},{3,3},{4,4},{5,5},{6,6},{7,7},{8,8},{9,9},{10,10... | collective-permute-start | bytes 1572872 | tf_op jit(solution)/shard_map/ppermute | solution.py:256
  1.7 15.6 %collective-permute-start.2 = (bf16[1024,256]{1,0:T(8,128)(2,1)}, bf16[1024,256]{1,0:T(8,128)(2,1)S(1)}, u32[]{:S(2)}, u32[]{:S(2)}) collective-permute-start(bf16[1024,256]{1,0:T(8,128)(2,1)} %param.5), channel_id=1, source_target_pairs={{0,1},{1,0},{2,3},{3,2},{4,5},{5,4},{6,7},{7,6},{8,9},{9,8},{10,11... | collective-permute-start | bytes 1572872 | tf_op jit(solution)/shard_map/ppermute | solution.py:79
  2.2 9.5 %collective-permute-start.1 = (bf16[256,256]{1,0:T(8,128)(2,1)}, bf16[256,256]{1,0:T(8,128)(2,1)S(1)}, u32[]{:S(2)}, u32[]{:S(2)}) collective-permute-start(bf16[256,256]{1,0:T(8,128)(2,1)} %param.6), channel_id=1, source_target_pairs={{0,0},{1,1},{2,2},{3,3},{4,4},{5,5},{6,6},{7,7},{8,8},{9,9},{10,10... | collective-permute-start | bytes 393224 | tf_op jit(solution)/shard_map/ppermute | solution.py:257
  3.1 10.0 %collective-permute-start.4 = (bf16[256,256]{1,0:T(8,128)(2,1)}, bf16[256,256]{1,0:T(8,128)(2,1)S(1)}, u32[]{:S(2)}, u32[]{:S(2)}) collective-permute-start(bf16[256,256]{1,0:T(8,128)(2,1)} %param.6), channel_id=1, source_target_pairs={{0,3},{1,2},{2,1},{3,0},{4,7},{5,6},{6,5},{7,4},{8,11},{9,10},{10,... | collective-permute-start | bytes 393224 | tf_op jit(solution)/shard_map/ppermute | solution.py:66
  7.1 1.2 %collective-permute-start.3 = (s32[1,33]{1,0:T(1,128)S(1)}, s32[1,33]{1,0:T(1,128)S(1)}, u32[]{:S(2)}, u32[]{:S(2)}) collective-permute-start(s32[1,33]{1,0:T(1,128)S(1)} %pad_add_fusion.mine), channel_id=1, source_target_pairs={{0,1},{1,0},{2,3},{3,2},{4,5},{5,4},{6,7},{7,6},{8,9},{9,8},{10,11... | collective-permute-start | bytes 404 | tf_op jit(solution)/shard_map/ppermute | solution.py:79
  8.3 7.2 %collective-permute-start.7 = (bf16[256,256]{1,0:T(8,128)(2,1)}, bf16[256,256]{1,0:T(8,128)(2,1)S(1)}, u32[]{:S(2)}, u32[]{:S(2)}) collective-permute-start(bf16[256,256]{1,0:T(8,128)(2,1)} %param.6), channel_id=1, source_target_pairs={{0,25},{1,24},{2,27},{3,26},{4,29},{5,28},{6,31},{7,30},{8,1},{9,0... | collective-permute-start | bytes 393224 | tf_op jit(solution)/shard_map/ppermute | solution.py:66
  11.6 8.6 %collective-permute-start.5 = (bf16[256,256]{1,0:T(8,128)(2,1)}, bf16[256,256]{1,0:T(8,128)(2,1)S(1)}, u32[]{:S(2)}, u32[]{:S(2)}) collective-permute-start(bf16[256,256]{1,0:T(8,128)(2,1)} %param.6), channel_id=1, source_target_pairs={{0,5},{1,4},{2,7},{3,6},{4,1},{5,0},{6,3},{7,2},{8,13},{9,12},{10,... | collective-permute-start | bytes 393224 | tf_op jit(solution)/shard_map/ppermute | solution.py:66
  13.1 7.2 %collective-permute-start.6 = (bf16[256,256]{1,0:T(8,128)(2,1)}, bf16[256,256]{1,0:T(8,128)(2,1)S(1)}, u32[]{:S(2)}, u32[]{:S(2)}) collective-permute-start(bf16[256,256]{1,0:T(8,128)(2,1)} %param.6), channel_id=1, source_target_pairs={{0,6},{1,7},{2,4},{3,5},{4,2},{5,3},{6,0},{7,1},{8,14},{9,15},{10,... | collective-permute-start | bytes 393224 | tf_op jit(solution)/shard_map/ppermute | solution.py:66
  15.5 6.8 %collective-permute-start.8 = (bf16[256,256]{1,0:T(8,128)(2,1)S(1)}, bf16[256,256]{1,0:T(8,128)(2,1)S(1)}, u32[]{:S(2)}, u32[]{:S(2)}) collective-permute-start(bf16[256,256]{1,0:T(8,128)(2,1)S(1)} %collective-permute-done.7.refs_3_), channel_id=1, source_target_pairs={{0,3},{1,2},{2,1},{3,0},{4,7},{5,6},{6,5},{7,4},{8,11},{9,10},{10,... | collective-permute-start | bytes 393224 | tf_op jit(solution)/shard_map/ppermute | solution.py:66
  15.5 9.6 %collective-permute-start.9 = (bf16[256,256]{1,0:T(8,128)(2,1)S(1)}, bf16[256,256]{1,0:T(8,128)(2,1)S(1)}, u32[]{:S(2)}, u32[]{:S(2)}) collective-permute-start(bf16[256,256]{1,0:T(8,128)(2,1)S(1)} %collective-permute-done.7.refs_3_), channel_id=1, source_target_pairs={{0,5},{1,4},{2,7},{3,6},{4,1},{5,0},{6,3},{7,2},{8,13},{9,12},{10,... | collective-permute-start | bytes 393224 | tf_op jit(solution)/shard_map/ppermute | solution.py:66
  17.3 8.3 %collective-permute-start.10 = (bf16[256,256]{1,0:T(8,128)(2,1)S(1)}, bf16[256,256]{1,0:T(8,128)(2,1)S(1)}, u32[]{:S(2)}, u32[]{:S(2)}) collective-permute-start(bf16[256,256]{1,0:T(8,128)(2,1)S(1)} %collective-permute-done.7.refs_3_), channel_id=1, source_target_pairs={{0,6},{1,7},{2,4},{3,5},{4,2},{5,3},{6,0},{7,1},{8,14},{9,15},{10,... | collective-permute-start | bytes 393224 | tf_op jit(solution)/shard_map/ppermute | solution.py:66
  27.1 1.6 %collective-permute-start.11 = (f32[8,256]{1,0:T(8,128)S(1)}, f32[8,256]{1,0:T(8,128)S(1)}, u32[]{:S(2)}, u32[]{:S(2)}) collective-permute-start(f32[8,256]{1,0:T(8,128)S(1)} %get-tuple-element.19.rows), channel_id=1, source_target_pairs={{0,1},{1,0},{2,3},{3,2},{4,5},{5,4},{6,7},{7,6},{8,9},{9,8},{10,11... | collective-permute-start | bytes 24584 | tf_op jit(solution)/shard_map/ppermute | solution.py:79
  30.2 3.1 %collective-permute-start.12 = (f32[8,256]{1,0:T(8,128)S(1)}, f32[8,256]{1,0:T(8,128)S(1)}, u32[]{:S(2)}, u32[]{:S(2)}) collective-permute-start(f32[8,256]{1,0:T(8,128)S(1)} %columns.2), channel_id=1, source_target_pairs={{0,3},{1,2},{2,1},{3,0},{4,7},{5,6},{6,5},{7,4},{8,11},{9,10},{10,... | collective-permute-start | bytes 24584 | tf_op jit(solution)/shard_map/ppermute | solution.py:66
  33.3 3.6 %collective-permute-start.13 = (f32[8,256]{1,0:T(8,128)S(1)}, f32[8,256]{1,0:T(8,128)S(1)}, u32[]{:S(2)}, u32[]{:S(2)}) collective-permute-start(f32[8,256]{1,0:T(8,128)S(1)} %add.59), channel_id=1, source_target_pairs={{0,5},{1,4},{2,7},{3,6},{4,1},{5,0},{6,3},{7,2},{8,13},{9,12},{10,... | collective-permute-start | bytes 24584 | tf_op jit(solution)/shard_map/ppermute | solution.py:66
  36.9 4.8 %collective-permute-start.14 = (f32[4,256]{1,0:T(4,128)S(1)}, f32[4,256]{1,0:T(4,128)S(1)}, u32[]{:S(2)}, u32[]{:S(2)}) collective-permute-start(f32[4,256]{1,0:T(4,128)S(1)} %get-tuple-element.26), channel_id=1, source_target_pairs={{0,9},{1,8},{2,11},{3,10},{4,13},{5,12},{6,15},{7,14},{8,17},{9,16... | collective-permute-start | bytes 12296 | tf_op jit(solution)/shard_map/ppermute | solution.py:66
  36.9 4.9 %collective-permute-start.15 = (f32[4,256]{1,0:T(4,128)S(1)}, f32[4,256]{1,0:T(4,128)S(1)}, u32[]{:S(2)}, u32[]{:S(2)}) collective-permute-start(f32[4,256]{1,0:T(4,128)S(1)} %get-tuple-element.25), channel_id=1, source_target_pairs={{0,25},{1,24},{2,27},{3,26},{4,29},{5,28},{6,31},{7,30},{8,1},{9,0... | collective-permute-start | bytes 12296 | tf_op jit(solution)/shard_map/ppermute | solution.py:66
  43.3 1.2 %collective-permute-start.16 = (f32[8,256]{1,0:T(8,128)S(1)}, f32[8,256]{1,0:T(8,128)S(1)}, u32[]{:S(2)}, u32[]{:S(2)}) collective-permute-start(f32[8,256]{1,0:T(8,128)S(1)} %rows.1), channel_id=1, source_target_pairs={{0,1},{1,0},{2,3},{3,2},{4,5},{5,4},{6,7},{7,6},{8,9},{9,8},{10,11... | collective-permute-start | bytes 24584 | tf_op jit(solution)/shard_map/ppermute | solution.py:79
  45.9 3.1 %collective-permute-start.17 = (f32[8,256]{1,0:T(8,128)S(1)}, f32[8,256]{1,0:T(8,128)S(1)}, u32[]{:S(2)}, u32[]{:S(2)}) collective-permute-start(f32[8,256]{1,0:T(8,128)S(1)} %get-tuple-element.21), channel_id=1, source_target_pairs={{0,3},{1,2},{2,1},{3,0},{4,7},{5,6},{6,5},{7,4},{8,11},{9,10},{10,... | collective-permute-start | bytes 24584 | tf_op jit(solution)/shard_map/ppermute | solution.py:66
  49.1 6.3 %collective-permute-start.20 = (f32[1,256]{1,0:T(1,128)S(1)}, f32[1,256]{1,0:T(1,128)S(1)}, u32[]{:S(2)}, u32[]{:S(2)}) collective-permute-start(f32[1,256]{1,0:T(1,128)S(1)} %get-tuple-element.23), channel_id=1, source_target_pairs={{0,12},{1,13},{2,14},{3,15},{4,8},{5,9},{6,10},{7,11},{8,20},{9,21... | collective-permute-start | bytes 3080 | tf_op jit(solution)/shard_map/ppermute | solution.py:66
  49.8 6.1 %collective-permute-start.19 = (f32[1,256]{1,0:T(1,128)S(1)}, f32[1,256]{1,0:T(1,128)S(1)}, u32[]{:S(2)}, u32[]{:S(2)}) collective-permute-start(f32[1,256]{1,0:T(1,128)S(1)} %get-tuple-element.24), channel_id=1, source_target_pairs={{0,9},{1,8},{2,11},{3,10},{4,13},{5,12},{6,15},{7,14},{8,17},{9,16... | collective-permute-start | bytes 3080 | tf_op jit(solution)/shard_map/ppermute | solution.py:66
  51.1 4.7 %collective-permute-start.18 = (f32[1,256]{1,0:T(1,128)S(1)}, f32[1,256]{1,0:T(1,128)S(1)}, u32[]{:S(2)}, u32[]{:S(2)}) collective-permute-start(f32[1,256]{1,0:T(1,128)S(1)} %get-tuple-element.22), channel_id=1, source_target_pairs={{0,5},{1,4},{2,7},{3,6},{4,1},{5,0},{6,3},{7,2},{8,13},{9,12},{10,... | collective-permute-start | bytes 3080 | tf_op jit(solution)/shard_map/ppermute | solution.py:66

commit v3 on v2

--- a/solution.py
+++ b/solution.py
@@ -17,6 +17,7 @@
 MIB = 2**20
 GROUP = 4
 FIELD = 256
+STRAIGHT = {3: 8}
 
 
 BOTH = ("group", "member")
@@ -74,16 +75,45 @@
     )
 
 
+def pair_groups(x, odd_first):
+    groups, members = lax.axis_size("group"), lax.axis_size("member")
+    pairs = []
+    for g in range(groups):
+        other = (g + (1 if (g % 2 == 1) == odd_first else -1)) % groups
+        pairs += [(g * members + m, other * members + (m ^ 1)) for m in range(members)]
+    return lax.ppermute(x, BOTH, pairs)
+
+
 def partner(x):
     size = lax.axis_size("member")
     return lax.ppermute(x, "member", [(i, i ^ 1) for i in range(size)])
 
 
-def spread_tiles(start, chips):
-    tiles = [start]
+def plan_of(chips):
+    return {k: STRAIGHT.get(k, 0) for k in range(1, chips)}
+
+
+def gathered(target, beyond, chips):
+    own = []
     for k in range(1, chips):
-        tiles.append(hop(start, 0, k))
-    return tiles
+        own.append(hop(target, 0, k))
+    blocks = {}
+    for k, eighths in plan_of(chips).items():
+        cut = target.shape[0] * eighths // 8
+        blocks[k] = []
+        if cut > 0:
+            blocks[k].append(hop(target[:cut], 1, k))
+        if cut < target.shape[0]:
+            blocks[k].append(hop(beyond[cut:], 0, k))
+    return own, [blocks[k] for k in range(1, chips)]
+
+
+def place(window, at, blocks):
+    row = 0
+    for block in blocks:
+        rows = block.shape[0]
+        window[at, row : row + rows] = unit(block[...])
+        row += rows
 
 
 def unit(values):
@@ -172,22 +202,29 @@
     build_pairs(units, window, table, factors, acc, lambda w: jnp.minimum(w, chips))
 
 
-def second_kernel(chips, units, table, before, *refs):
-    tiles = refs[: chips - 1]
-    factors, rows, acc, window = refs[chips - 1 :]
+def second_kernel(shape, units, table, before, *refs):
+    chips = len(shape) + 1
+    tiles = list(refs[: sum(shape)])
+    factors, rows, acc, window = refs[sum(shape) :]
     chip = lax.axis_index("member") // CORES
-    for k in range(1, chips):
-        window[chip ^ k] = unit(tiles[k - 1][...])
+    for k, count in enumerate(shape):
+        place(window, chip ^ (k + 1), [tiles.pop(0) for _ in range(count)])
     acc[...] = before[...]
     build_pairs(units, window, table, factors, acc, lambda w: w - chips)
     rows_out(acc, rows)
 
 
-def row_kernel(first, second, lists_first, lists_second, columns, before, after, rows, scale, acc):
-    chips = before.shape[0]
+def row_kernel(
+    paired, first, second, lists_first, lists_second, columns, wide, near, rows, scale, acc
+):
+    chips = columns.shape[0] // 2
     tiles = acc.shape[0] // CORES
-    scale[:chips] = float(tiles) / (columns[:chips] + before[...])
-    scale[chips:] = float(tiles) / (columns[chips:] + after[...])
+    below, above = wide[...], near[...]
+    if paired:
+        swapped = (lax.axis_index("group") & 1) == 1
+        below, above = jnp.where(swapped, above, below), jnp.where(swapped, below, above)
+    scale[:chips] = float(tiles) / (columns[:chips] + below[chips:])
+    scale[chips:] = float(tiles) / (columns[chips:] + above[:chips])
     acc[...] = jnp.zeros_like(acc)
     for factors, table in ((first, lists_first), (second, lists_second)):
 
@@ -248,8 +285,7 @@
     most_second = up_to_group(min(CORES * slots, both * (chips - 1)))
 
     beyond = hop(target, 1, 0)
-    own_tiles = spread_tiles(target, chips)
-    next_tiles = spread_tiles(beyond, chips)
+    own_tiles, next_tiles = gathered(target, beyond, chips)
     info = coded(pair_source, pair_target, pair_count, members, even)
     partner_source = partner(source)
     stay = [(i, i) for i in range(members)]
@@ -290,8 +326,8 @@
         own_source, own_target, partner_source, info, partner_info
     )
 
-    early = own_tiles[1:] + [next_tiles[0]]
-    late = next_tiles[1:]
+    early = own_tiles + [beyond]
+    late = [block for blocks in next_tiles for block in blocks]
     first_call = pl.pallas_call(
         functools.partial(first_kernel, chips),
         out_shape=(shaped(most_first, cells, cells, kind=BF16), shaped(both + 1, cells, LANES)),
@@ -304,7 +340,7 @@
     )
     first, acc = first_call(units, lists_first, home, *early)
     second, rows = pl.pallas_call(
-        functools.partial(second_kernel, chips),
+        functools.partial(second_kernel, [len(blocks) for blocks in next_tiles]),
         out_shape=(shaped(most_second, cells, cells, kind=BF16), shaped(both, cells)),
         in_specs=[VM, SM, VM] + [VM] * len(late),
         out_specs=(VM, VM),
@@ -323,14 +359,14 @@
         last = sweep + 1 == ITERS
         if sweep > 0:
             rows = pl.pallas_call(
-                row_kernel,
+                functools.partial(row_kernel, even == 1),
                 out_shape=shaped(both, cells),
                 in_specs=[VM, VM, SM, SM, VM, VM, VM],
                 out_specs=VM,
                 scratch_shapes=[pltpu.VMEM((2 * chips, cells), F32), pltpu.VMEM(lanes_acc, F32)],
                 compiler_params=held_limit,
                 name="rows",
-            )(*held, columns, before, after)
+            )(*held, columns, wide, near)
         found = pl.pallas_call(
             functools.partial(column_kernel, last),
             out_shape=(shaped(2 * chips, cells),) + ((shaped(tiles, cells),) if last else ()),
@@ -348,8 +384,8 @@
         if not last:
             for bit in bits:
                 columns = columns + hop(columns, 0, bit)
-            before = hop(columns[chips:], -1, 0)
-            after = hop(columns[:chips], 1, 0)
+            wide = pair_groups(columns, True) if even else hop(columns, -1, 0)
+            near = pair_groups(columns, False) if even else hop(columns, 1, 0)
         else:
             chip = lax.axis_index("member") // CORES
             for bit in bits[:-1]:

time: 56.6 us -> 57.1 us (level)
    ppermute x0 -> x2, waiting for transfers between devices: none -> 3.53 us  [pair_groups(): return lax.ppermute(x, BOTH, pairs)]
    ppermute x15 -> x13, waiting for transfers between devices: 16.8 us -> 13.7 us  [hop(): lax.ppermute(x, BOTH, [(g * members + m, (g - up) % groups * members + (m...]
    ppermute x0 -> x2, starting transfers between devices: none -> 1.34 us  [pair_groups(): return lax.ppermute(x, BOTH, pairs)]
    ppermute x15 -> x13, starting transfers between devices: 20.3 us -> 19 us  [hop(): lax.ppermute(x, BOTH, [(g * members + m, (g - up) % groups * members + (m...]
  transfers between devices with their start and end apart: 21 -> 21, of which waited for: 12 -> 11; matrix products, arithmetic and copies ran while one was open for 2% -> 2% of each run, Pallas kernels for 6% -> 6%
where the time goes in v3:
time: 57.1 us; the launch traced here: 56.9 us
  starting transfers between devices  23.9 us (42%)
  waiting for transfers between devices  20.1 us (35%)
  Pallas kernels  9.53 us (17%)
  between operations  1.37 us (2%)
  other arithmetic  1.36 us (2%)
  local copies, waits for them, and re-layouts  0.61 us (1%)
    ppermute x13, starting transfers between devices, hop(): lax.ppermute(x, BOTH, [(g * members + m, (g - up) % groups * members + (m...  19 us
    ppermute x13, waiting for transfers between devices, hop(): lax.ppermute(x, BOTH, [(g * members + m, (g - up) % groups * members + (m...  13.7 us
    ppermute x2, waiting for transfers between devices, pair_groups(): return lax.ppermute(x, BOTH, pairs)  3.53 us
    pallas_call x2, Pallas kernels, step(): pl.pallas_call(functools.partial(column_kernel, last), out_shape=(shaped(...  2.89 us
    ppermute x4, waiting for transfers between devices, partner(): return lax.ppermute(x, 'member', [(i, i ^ 1) for i in range(size)])  2.81 us
    pallas_call x1, Pallas kernels, step(): first, acc = first_call(units, lists_first, home, *early)  2.03 us
    ppermute x4, starting transfers between devices, partner(): return lax.ppermute(x, 'member', [(i, i ^ 1) for i in range(size)])  1.68 us
    pallas_call x1, Pallas kernels, step(): pl.pallas_call(functools.partial(second_kernel, [len(blocks) for blocks i...  1.57 us
  transfers between devices with their start and end apart: 21, of which 11 were waited for; matrix products, arithmetic and copies ran while one was open for 2% of the time, Pallas kernels for 6%

profile of v3, /device:TPU:0, one launch (start us, length us, event | category | flops | bytes accessed | tf_op | source)
XLA Modules:
  0.0 56.9 jit_solution(2127276594753055502)
XLA Ops:
  0.6 1.0 %collective-permute-start = (bf16[1024,256]{1,0:T(8,128)(2,1)}, bf16[1024,256]{1,0:T(8,128)(2,1)S(1)}, u32[]{:S(2)}, u32[]{:S(2)}) collective-permute-start(bf16[1024,256]{1,0:T(8,128)(2,1)} %param.5), channel_id=1, source_target_pairs={{0,0},{1,1},{2,2},{3,3},{4,4},{5,5},{6,6},{7,7},{8,8},{9,9},{10,10... | collective-permute-start | bytes 1572872 | tf_op jit(solution)/shard_map/ppermute | solution.py:292
  2.2 0.9 %collective-permute-start.1 = (bf16[256,256]{1,0:T(8,128)(2,1)}, bf16[256,256]{1,0:T(8,128)(2,1)S(1)}, u32[]{:S(2)}, u32[]{:S(2)}) collective-permute-start(bf16[256,256]{1,0:T(8,128)(2,1)} %param.6), channel_id=1, source_target_pairs={{0,0},{1,1},{2,2},{3,3},{4,4},{5,5},{6,6},{7,7},{8,8},{9,9},{10,10... | collective-permute-start | bytes 393224 | tf_op jit(solution)/shard_map/ppermute | solution.py:293
  3.1 2.6 %collective-permute-start.4 = (bf16[256,256]{1,0:T(8,128)(2,1)}, bf16[256,256]{1,0:T(8,128)(2,1)S(1)}, u32[]{:S(2)}, u32[]{:S(2)}) collective-permute-start(bf16[256,256]{1,0:T(8,128)(2,1)} %param.6), channel_id=1, source_target_pairs={{0,3},{1,2},{2,1},{3,0},{4,7},{5,6},{6,5},{7,4},{8,11},{9,10},{10,... | collective-permute-start | bytes 393224 | tf_op jit(solution)/shard_map/ppermute | solution.py:67
  6.3 0.7 %fusion.6 = s32[1,32]{1,0:T(1,128)S(1)} fusion(s32[1,32]{1,0:T(1,128)} %param.7, s32[1,32]{1,0:T(1,128)} %param.8, s32[]{:T(128)} %bitcast.5, s32[]{:T(128)S(6)} %select_n.27), kind=kLoop, calls=%fused_computation.23 | loop fusion | flops 1728 | bytes 392 | tf_op jit(solution)/shard_map/add | solution.py:51
  7.1 1.1 %collective-permute-done.3.theirs = s32[1,33]{1,0:T(1,128)S(1)} collective-permute-done((s32[1,33]{1,0:T(1,128)S(1)}, s32[1,33]{1,0:T(1,128)S(1)}, u32[]{:S(2)}, u32[]{:S(2)}) %collective-permute-start.3) | collective-permute-done | bytes 164 | tf_op jit(solution)/shard_map/ppermute | solution.py:89
  8.3 3.4 %collective-permute-start.7 = (bf16[256,256]{1,0:T(8,128)(2,1)}, bf16[256,256]{1,0:T(8,128)(2,1)S(1)}, u32[]{:S(2)}, u32[]{:S(2)}) collective-permute-start(bf16[256,256]{1,0:T(8,128)(2,1)} %param.6), channel_id=1, source_target_pairs={{0,25},{1,24},{2,27},{3,26},{4,29},{5,28},{6,31},{7,30},{8,1},{9,0... | collective-permute-start | bytes 393224 | tf_op jit(solution)/shard_map/ppermute | solution.py:67
  11.6 1.5 %collective-permute-start.5 = (bf16[256,256]{1,0:T(8,128)(2,1)}, bf16[256,256]{1,0:T(8,128)(2,1)S(1)}, u32[]{:S(2)}, u32[]{:S(2)}) collective-permute-start(bf16[256,256]{1,0:T(8,128)(2,1)} %param.6), channel_id=1, source_target_pairs={{0,5},{1,4},{2,7},{3,6},{4,1},{5,0},{6,3},{7,2},{8,13},{9,12},{10,... | collective-permute-start | bytes 393224 | tf_op jit(solution)/shard_map/ppermute | solution.py:67
  13.6 1.9 %collective-permute-done.7.refs_3_ = bf16[256,256]{1,0:T(8,128)(2,1)S(1)} collective-permute-done((bf16[256,256]{1,0:T(8,128)(2,1)}, bf16[256,256]{1,0:T(8,128)(2,1)S(1)}, u32[]{:S(2)}, u32[]{:S(2)}) %collective-permute-start.7) | collective-permute-done | bytes 131104 | tf_op jit(solution)/shard_map/ppermute | solution.py:67
  15.5 4.5 %collective-permute-start.10 = (bf16[256,256]{1,0:T(8,128)(2,1)}, bf16[256,256]{1,0:T(8,128)(2,1)S(1)}, u32[]{:S(2)}, u32[]{:S(2)}) collective-permute-start(bf16[256,256]{1,0:T(8,128)(2,1)} %param.6), channel_id=1, source_target_pairs={{0,31},{1,30},{2,29},{3,28},{4,27},{5,26},{6,25},{7,24},{8,7},{9,6... | collective-permute-start | bytes 393224 | tf_op jit(solution)/shard_map/ppermute | solution.py:67
  20.0 1.4 %collective-permute-start.8 = (bf16[256,256]{1,0:T(8,128)(2,1)S(1)}, bf16[256,256]{1,0:T(8,128)(2,1)S(1)}, u32[]{:S(2)}, u32[]{:S(2)}) collective-permute-start(bf16[256,256]{1,0:T(8,128)(2,1)S(1)} %collective-permute-done.7.refs_3_), channel_id=1, source_target_pairs={{0,3},{1,2},{2,1},{3,0},{4,7},{5,6},{6,5},{7,4},{8,11},{9,10},{10,... | collective-permute-start | bytes 393224 | tf_op jit(solution)/shard_map/ppermute | solution.py:67
  21.7 1.5 %prepare.1 = (bf16[8,256,256]{2,1,0:T(8,128)(2,1)S(1)}, bf16[256,256]{1,0:T(8,128)(2,1)S(1)}, s32[42]{0:T(128)S(1)}, s32[26]{0:T(128)S(1)}) custom-call(bf16[1024,256]{1,0:T(8,128)(2,1)S(1)} %collective-permute-done.own, bf16[256,256]{1,0:T(8,128)(2,1)S(1)} %collective-permute-done.1.target, bf16[1024,256]{1,0:T(8,128)(2,1)S(1)} %collective-permute-done.2.other, ...), custom_call_target="tpu_custom_call" | custom-call | flops 268435456 | bytes 1048576 | tf_op jit(solution)/shard_map/prepare/pallas_call | solution.py:325
  23.3 2.0 %first.1 = (bf16[40,256,256]{2,1,0:T(8,128)(2,1)S(1)}, f32[9,256,128]{2,1,0:T(8,128)S(1)}) custom-call(bf16[8,256,256]{2,1,0:T(8,128)(2,1)S(1)} %get-tuple-element.12.units, s32[42]{0:T(128)S(1)} %get-tuple-element.13.table.lists_first, bf16[256,256]{1,0:T(8,128)(2,1)S(1)} %get-tuple-element.14.home, bf16[256,256]{1,0:T(8,128)(2,1)S(1)} %collective-permute-done.4.refs_0_, ...), custom_call_target="tpu_custom_call" | custom-call | flops 1342177280 | bytes 5242880 | tf_op jit(solution)/shard_map/first/pallas_call | solution.py:341
  25.9 1.0 %collective-permute-done.9.refs_1_ = bf16[256,256]{1,0:T(8,128)(2,1)S(1)} collective-permute-done((bf16[256,256]{1,0:T(8,128)(2,1)S(1)}, bf16[256,256]{1,0:T(8,128)(2,1)S(1)}, u32[]{:S(2)}, u32[]{:S(2)}) %collective-permute-start.9) | collective-permute-done | bytes 131104 | tf_op jit(solution)/shard_map/ppermute | solution.py:67
  26.9 1.6 %second.1 = (bf16[24,256,256]{2,1,0:T(8,128)(2,1)S(1)}, f32[8,256]{1,0:T(8,128)S(1)}) custom-call(bf16[8,256,256]{2,1,0:T(8,128)(2,1)S(1)} %get-tuple-element.12.units, s32[26]{0:T(128)S(1)} %get-tuple-element.16.table.lists_second, f32[9,256,128]{2,1,0:T(8,128)S(1)} %get-tuple-element.17.before, bf16[256,256]{1,0:T(8,128)(2,1)S(1)} %collective-permute-done.8.refs_0_, ...), custom_call_target="tpu_custom_call" | custom-call | flops 805306368 | bytes 3145728 | tf_op jit(solution)/shard_map/second/pallas_call | solution.py:342
  29.1 0.8 %collective-permute-done.11.arrived = f32[8,256]{1,0:T(8,128)S(1)} collective-permute-done((f32[8,256]{1,0:T(8,128)S(1)}, f32[8,256]{1,0:T(8,128)S(1)}, u32[]{:S(2)}, u32[]{:S(2)}) %collective-permute-start.11) | collective-permute-done | bytes 8224 | tf_op jit(solution)/shard_map/ppermute | solution.py:89
  29.9 1.4 %columns.2 = f32[8,256]{1,0:T(8,128)S(1)} custom-call(bf16[40,256,256]{2,1,0:T(8,128)(2,1)S(1)} %get-tuple-element.15.first, bf16[24,256,256]{2,1,0:T(8,128)(2,1)S(1)} %get-tuple-element.18.second, s32[42]{0:T(128)S(1)} %get-tuple-element.13.table.lists_first, s32[26]{0:T(128)S(1)} %get-tuple-element.16.table.lists_second, ...), custom_call_target="tpu_custom_call" | custom-call | tf_op jit(solution)/shard_map/columns/pallas_call | solution.py:370
  31.8 2.7 %collective-permute-done.12 = f32[8,256]{1,0:T(8,128)S(1)} collective-permute-done((f32[8,256]{1,0:T(8,128)S(1)}, f32[8,256]{1,0:T(8,128)S(1)}, u32[]{:S(2)}, u32[]{:S(2)}) %collective-permute-start.12) | collective-permute-done | bytes 8224 | tf_op jit(solution)/shard_map/ppermute | solution.py:67
  34.5 1.4 %collective-permute-start.13 = (f32[8,256]{1,0:T(8,128)S(1)}, f32[8,256]{1,0:T(8,128)S(1)}, u32[]{:S(2)}, u32[]{:S(2)}) collective-permute-start(f32[8,256]{1,0:T(8,128)S(1)} %add.59), channel_id=1, source_target_pairs={{0,5},{1,4},{2,7},{3,6},{4,1},{5,0},{6,3},{7,2},{8,13},{9,12},{10,... | collective-permute-start | bytes 24584 | tf_op jit(solution)/shard_map/ppermute | solution.py:67
  35.9 1.7 %collective-permute-done.13 = f32[8,256]{1,0:T(8,128)S(1)} collective-permute-done((f32[8,256]{1,0:T(8,128)S(1)}, f32[8,256]{1,0:T(8,128)S(1)}, u32[]{:S(2)}, u32[]{:S(2)}) %collective-permute-start.13) | collective-permute-done | bytes 8224 | tf_op jit(solution)/shard_map/ppermute | solution.py:67
  37.6 1.1 %collective-permute-start.14 = (f32[8,256]{1,0:T(8,128)S(1)}, f32[8,256]{1,0:T(8,128)S(1)}, u32[]{:S(2)}, u32[]{:S(2)}) collective-permute-start(f32[8,256]{1,0:T(8,128)S(1)} %add.60.columns), channel_id=1, source_target_pairs={{0,25},{1,24},{2,27},{3,26},{4,29},{5,28},{6,31},{7,30},{8,17},{9,... | collective-permute-start | bytes 24584 | tf_op jit(solution)/shard_map/ppermute | solution.py:84
  38.9 3.5 %collective-permute-done.14.wide = f32[8,256]{1,0:T(8,128)S(1)} collective-permute-done((f32[8,256]{1,0:T(8,128)S(1)}, f32[8,256]{1,0:T(8,128)S(1)}, u32[]{:S(2)}, u32[]{:S(2)}) %collective-permute-start.14) | collective-permute-done | bytes 8224 | tf_op jit(solution)/shard_map/ppermute | solution.py:84
  42.4 1.5 %rows.1 = f32[8,256]{1,0:T(8,128)S(1)} custom-call(bf16[40,256,256]{2,1,0:T(8,128)(2,1)S(1)} %get-tuple-element.15.first, bf16[24,256,256]{2,1,0:T(8,128)(2,1)S(1)} %get-tuple-element.18.second, s32[42]{0:T(128)S(1)} %get-tuple-element.13.table.lists_first, s32[26]{0:T(128)S(1)} %get-tuple-element.16.table.lists_second, f32[8,256]{1,0:T(8,128)S(1)} %add.60.columns, ...), custom_call_target="tpu_custom_call" | custom-call | tf_op jit(solution)/shard_map/rows/pallas_call | solution.py:361
  43.9 0.6 %collective-permute-start.16 = (f32[8,256]{1,0:T(8,128)S(1)}, f32[8,256]{1,0:T(8,128)S(1)}, u32[]{:S(2)}, u32[]{:S(2)}) collective-permute-start(f32[8,256]{1,0:T(8,128)S(1)} %rows.1), channel_id=1, source_target_pairs={{0,1},{1,0},{2,3},{3,2},{4,5},{5,4},{6,7},{7,6},{8,9},{9,8},{10,11... | collective-permute-start | bytes 24584 | tf_op jit(solution)/shard_map/ppermute | solution.py:89
  44.5 0.8 %collective-permute-done.16.arrived = f32[8,256]{1,0:T(8,128)S(1)} collective-permute-done((f32[8,256]{1,0:T(8,128)S(1)}, f32[8,256]{1,0:T(8,128)S(1)}, u32[]{:S(2)}, u32[]{:S(2)}) %collective-permute-start.16) | collective-permute-done | bytes 8224 | tf_op jit(solution)/shard_map/ppermute | solution.py:89
  45.3 1.4 %columns.3 = (f32[8,256]{1,0:T(8,128)S(1)}, f32[4,256]{1,0:T(4,128)S(1)}) custom-call(bf16[40,256,256]{2,1,0:T(8,128)(2,1)S(1)} %get-tuple-element.15.first, bf16[24,256,256]{2,1,0:T(8,128)(2,1)S(1)} %get-tuple-element.18.second, s32[42]{0:T(128)S(1)} %get-tuple-element.13.table.lists_first, s32[26]{0:T(128)S(1)} %get-tuple-element.16.table.lists_second, ...), custom_call_target="tpu_custom_call" | custom-call | tf_op jit(solution)/shard_map/columns/pallas_call | solution.py:370
  47.0 2.9 %collective-permute-done.17 = f32[8,256]{1,0:T(8,128)S(1)} collective-permute-done((f32[8,256]{1,0:T(8,128)S(1)}, f32[8,256]{1,0:T(8,128)S(1)}, u32[]{:S(2)}, u32[]{:S(2)}) %collective-permute-start.17) | collective-permute-done | bytes 8224 | tf_op jit(solution)/shard_map/ppermute | solution.py:67
  50.0 0.8 %collective-permute-start.20 = (f32[1,256]{1,0:T(1,128)S(1)}, f32[1,256]{1,0:T(1,128)S(1)}, u32[]{:S(2)}, u32[]{:S(2)}) collective-permute-start(f32[1,256]{1,0:T(1,128)S(1)} %get-tuple-element.23), channel_id=1, source_target_pairs={{0,12},{1,13},{2,14},{3,15},{4,8},{5,9},{6,10},{7,11},{8,20},{9,21... | collective-permute-start | bytes 3080 | tf_op jit(solution)/shard_map/ppermute | solution.py:67
  50.8 0.8 %collective-permute-start.19 = (f32[1,256]{1,0:T(1,128)S(1)}, f32[1,256]{1,0:T(1,128)S(1)}, u32[]{:S(2)}, u32[]{:S(2)}) collective-permute-start(f32[1,256]{1,0:T(1,128)S(1)} %get-tuple-element.24), channel_id=1, source_target_pairs={{0,9},{1,8},{2,11},{3,10},{4,13},{5,12},{6,15},{7,14},{8,17},{9,16... | collective-permute-start | bytes 3080 | tf_op jit(solution)/shard_map/ppermute | solution.py:67
  51.5 1.2 %collective-permute-start.18 = (f32[1,256]{1,0:T(1,128)S(1)}, f32[1,256]{1,0:T(1,128)S(1)}, u32[]{:S(2)}, u32[]{:S(2)}) collective-permute-start(f32[1,256]{1,0:T(1,128)S(1)} %get-tuple-element.22), channel_id=1, source_target_pairs={{0,5},{1,4},{2,7},{3,6},{4,1},{5,0},{6,3},{7,2},{8,13},{9,12},{10,... | collective-permute-start | bytes 3080 | tf_op jit(solution)/shard_map/ppermute | solution.py:67
  52.8 0.6 %copy.7 = f32[1,2,4,128]{3,1,2,0:T(2,128)} copy(f32[1,2,4,128]{3,2,1,0:T(4,128)S(1)} %bitcast.7) | data formatting | bytes 8192
  53.4 2.9 %collective-permute-done.20 = f32[1,256]{1,0:T(1,128)S(1)} collective-permute-done((f32[1,256]{1,0:T(1,128)S(1)}, f32[1,256]{1,0:T(1,128)S(1)}, u32[]{:S(2)}, u32[]{:S(2)}) %collective-permute-start.20) | collective-permute-done | bytes 1056 | tf_op jit(solution)/shard_map/ppermute | solution.py:67
  56.3 0.6 %divide_log_fusion = f32[1,256]{1,0:T(1,128)} fusion(f32[1,256]{1,0:T(1,128)S(1)} %collective-permute-done.20, f32[1,256]{1,0:T(1,128)S(1)} %collective-permute-done.19, f32[1,256]{1,0:T(1,128)S(1)} %collective-permute-done.18, f32[8,256]{1,0:T(8,128)S(1)} %add.61, s32[]{:T(128)S(6)} %select_n.29), kind=kLoop, calls=%fused_computation.12 | loop fusion | flops 1024 | bytes 5124 | tf_op jit(solution)/shard_map/log | solution.py:404
  (24 shorter events, 3.4 us)
Async XLA Ops:
  0.6 19.4 %collective-permute-start = (bf16[1024,256]{1,0:T(8,128)(2,1)}, bf16[1024,256]{1,0:T(8,128)(2,1)S(1)}, u32[]{:S(2)}, u32[]{:S(2)}) collective-permute-start(bf16[1024,256]{1,0:T(8,128)(2,1)} %param.5), channel_id=1, source_target_pairs={{0,0},{1,1},{2,2},{3,3},{4,4},{5,5},{6,6},{7,7},{8,8},{9,9},{10,10... | collective-permute-start | bytes 1572872 | tf_op jit(solution)/shard_map/ppermute | solution.py:292
  1.7 19.8 %collective-permute-start.2 = (bf16[1024,256]{1,0:T(8,128)(2,1)}, bf16[1024,256]{1,0:T(8,128)(2,1)S(1)}, u32[]{:S(2)}, u32[]{:S(2)}) collective-permute-start(bf16[1024,256]{1,0:T(8,128)(2,1)} %param.5), channel_id=1, source_target_pairs={{0,1},{1,0},{2,3},{3,2},{4,5},{5,4},{6,7},{7,6},{8,9},{9,8},{10,11... | collective-permute-start | bytes 1572872 | tf_op jit(solution)/shard_map/ppermute | solution.py:89
  2.2 9.5 %collective-permute-start.1 = (bf16[256,256]{1,0:T(8,128)(2,1)}, bf16[256,256]{1,0:T(8,128)(2,1)S(1)}, u32[]{:S(2)}, u32[]{:S(2)}) collective-permute-start(bf16[256,256]{1,0:T(8,128)(2,1)} %param.6), channel_id=1, source_target_pairs={{0,0},{1,1},{2,2},{3,3},{4,4},{5,5},{6,6},{7,7},{8,8},{9,9},{10,10... | collective-permute-start | bytes 393224 | tf_op jit(solution)/shard_map/ppermute | solution.py:293
  3.1 10.0 %collective-permute-start.4 = (bf16[256,256]{1,0:T(8,128)(2,1)}, bf16[256,256]{1,0:T(8,128)(2,1)S(1)}, u32[]{:S(2)}, u32[]{:S(2)}) collective-permute-start(bf16[256,256]{1,0:T(8,128)(2,1)} %param.6), channel_id=1, source_target_pairs={{0,3},{1,2},{2,1},{3,0},{4,7},{5,6},{6,5},{7,4},{8,11},{9,10},{10,... | collective-permute-start | bytes 393224 | tf_op jit(solution)/shard_map/ppermute | solution.py:67
  7.1 1.2 %collective-permute-start.3 = (s32[1,33]{1,0:T(1,128)S(1)}, s32[1,33]{1,0:T(1,128)S(1)}, u32[]{:S(2)}, u32[]{:S(2)}) collective-permute-start(s32[1,33]{1,0:T(1,128)S(1)} %pad_add_fusion.mine), channel_id=1, source_target_pairs={{0,1},{1,0},{2,3},{3,2},{4,5},{5,4},{6,7},{7,6},{8,9},{9,8},{10,11... | collective-permute-start | bytes 404 | tf_op jit(solution)/shard_map/ppermute | solution.py:89
  8.3 7.2 %collective-permute-start.7 = (bf16[256,256]{1,0:T(8,128)(2,1)}, bf16[256,256]{1,0:T(8,128)(2,1)S(1)}, u32[]{:S(2)}, u32[]{:S(2)}) collective-permute-start(bf16[256,256]{1,0:T(8,128)(2,1)} %param.6), channel_id=1, source_target_pairs={{0,25},{1,24},{2,27},{3,26},{4,29},{5,28},{6,31},{7,30},{8,1},{9,0... | collective-permute-start | bytes 393224 | tf_op jit(solution)/shard_map/ppermute | solution.py:67
  11.6 11.7 %collective-permute-start.5 = (bf16[256,256]{1,0:T(8,128)(2,1)}, bf16[256,256]{1,0:T(8,128)(2,1)S(1)}, u32[]{:S(2)}, u32[]{:S(2)}) collective-permute-start(bf16[256,256]{1,0:T(8,128)(2,1)} %param.6), channel_id=1, source_target_pairs={{0,5},{1,4},{2,7},{3,6},{4,1},{5,0},{6,3},{7,2},{8,13},{9,12},{10,... | collective-permute-start | bytes 393224 | tf_op jit(solution)/shard_map/ppermute | solution.py:67
  13.1 10.2 %collective-permute-start.6 = (bf16[256,256]{1,0:T(8,128)(2,1)}, bf16[256,256]{1,0:T(8,128)(2,1)S(1)}, u32[]{:S(2)}, u32[]{:S(2)}) collective-permute-start(bf16[256,256]{1,0:T(8,128)(2,1)} %param.6), channel_id=1, source_target_pairs={{0,6},{1,7},{2,4},{3,5},{4,2},{5,3},{6,0},{7,1},{8,14},{9,15},{10,... | collective-permute-start | bytes 393224 | tf_op jit(solution)/shard_map/ppermute | solution.py:67
  15.5 9.9 %collective-permute-start.10 = (bf16[256,256]{1,0:T(8,128)(2,1)}, bf16[256,256]{1,0:T(8,128)(2,1)S(1)}, u32[]{:S(2)}, u32[]{:S(2)}) collective-permute-start(bf16[256,256]{1,0:T(8,128)(2,1)} %param.6), channel_id=1, source_target_pairs={{0,31},{1,30},{2,29},{3,28},{4,27},{5,26},{6,25},{7,24},{8,7},{9,6... | collective-permute-start | bytes 393224 | tf_op jit(solution)/shard_map/ppermute | solution.py:67
  20.0 5.9 %collective-permute-start.8 = (bf16[256,256]{1,0:T(8,128)(2,1)S(1)}, bf16[256,256]{1,0:T(8,128)(2,1)S(1)}, u32[]{:S(2)}, u32[]{:S(2)}) collective-permute-start(bf16[256,256]{1,0:T(8,128)(2,1)S(1)} %collective-permute-done.7.refs_3_), channel_id=1, source_target_pairs={{0,3},{1,2},{2,1},{3,0},{4,7},{5,6},{6,5},{7,4},{8,11},{9,10},{10,... | collective-permute-start | bytes 393224 | tf_op jit(solution)/shard_map/ppermute | solution.py:67
  21.5 5.4 %collective-permute-start.9 = (bf16[256,256]{1,0:T(8,128)(2,1)S(1)}, bf16[256,256]{1,0:T(8,128)(2,1)S(1)}, u32[]{:S(2)}, u32[]{:S(2)}) collective-permute-start(bf16[256,256]{1,0:T(8,128)(2,1)S(1)} %collective-permute-done.7.refs_3_), channel_id=1, source_target_pairs={{0,5},{1,4},{2,7},{3,6},{4,1},{5,0},{6,3},{7,2},{8,13},{9,12},{10,... | collective-permute-start | bytes 393224 | tf_op jit(solution)/shard_map/ppermute | solution.py:67
  28.5 1.4 %collective-permute-start.11 = (f32[8,256]{1,0:T(8,128)S(1)}, f32[8,256]{1,0:T(8,128)S(1)}, u32[]{:S(2)}, u32[]{:S(2)}) collective-permute-start(f32[8,256]{1,0:T(8,128)S(1)} %get-tuple-element.19.rows), channel_id=1, source_target_pairs={{0,1},{1,0},{2,3},{3,2},{4,5},{5,4},{6,7},{7,6},{8,9},{9,8},{10,11... | collective-permute-start | bytes 24584 | tf_op jit(solution)/shard_map/ppermute | solution.py:89
  31.3 3.1 %collective-permute-start.12 = (f32[8,256]{1,0:T(8,128)S(1)}, f32[8,256]{1,0:T(8,128)S(1)}, u32[]{:S(2)}, u32[]{:S(2)}) collective-permute-start(f32[8,256]{1,0:T(8,128)S(1)} %columns.2), channel_id=1, source_target_pairs={{0,3},{1,2},{2,1},{3,0},{4,7},{5,6},{6,5},{7,4},{8,11},{9,10},{10,... | collective-permute-start | bytes 24584 | tf_op jit(solution)/shard_map/ppermute | solution.py:67
  34.5 3.1 %collective-permute-start.13 = (f32[8,256]{1,0:T(8,128)S(1)}, f32[8,256]{1,0:T(8,128)S(1)}, u32[]{:S(2)}, u32[]{:S(2)}) collective-permute-start(f32[8,256]{1,0:T(8,128)S(1)} %add.59), channel_id=1, source_target_pairs={{0,5},{1,4},{2,7},{3,6},{4,1},{5,0},{6,3},{7,2},{8,13},{9,12},{10,... | collective-permute-start | bytes 24584 | tf_op jit(solution)/shard_map/ppermute | solution.py:67
  37.6 4.9 %collective-permute-start.14 = (f32[8,256]{1,0:T(8,128)S(1)}, f32[8,256]{1,0:T(8,128)S(1)}, u32[]{:S(2)}, u32[]{:S(2)}) collective-permute-start(f32[8,256]{1,0:T(8,128)S(1)} %add.60.columns), channel_id=1, source_target_pairs={{0,25},{1,24},{2,27},{3,26},{4,29},{5,28},{6,31},{7,30},{8,17},{9,... | collective-permute-start | bytes 24584 | tf_op jit(solution)/shard_map/ppermute | solution.py:84
  38.6 3.8 %collective-permute-start.15 = (f32[8,256]{1,0:T(8,128)S(1)}, f32[8,256]{1,0:T(8,128)S(1)}, u32[]{:S(2)}, u32[]{:S(2)}) collective-permute-start(f32[8,256]{1,0:T(8,128)S(1)} %add.60.columns), channel_id=1, source_target_pairs={{0,9},{1,8},{2,11},{3,10},{4,13},{5,12},{6,15},{7,14},{8,1},{9,0},... | collective-permute-start | bytes 24584 | tf_op jit(solution)/shard_map/ppermute | solution.py:84
  43.9 1.4 %collective-permute-start.16 = (f32[8,256]{1,0:T(8,128)S(1)}, f32[8,256]{1,0:T(8,128)S(1)}, u32[]{:S(2)}, u32[]{:S(2)}) collective-permute-start(f32[8,256]{1,0:T(8,128)S(1)} %rows.1), channel_id=1, source_target_pairs={{0,1},{1,0},{2,3},{3,2},{4,5},{5,4},{6,7},{7,6},{8,9},{9,8},{10,11... | collective-permute-start | bytes 24584 | tf_op jit(solution)/shard_map/ppermute | solution.py:89
  46.8 3.1 %collective-permute-start.17 = (f32[8,256]{1,0:T(8,128)S(1)}, f32[8,256]{1,0:T(8,128)S(1)}, u32[]{:S(2)}, u32[]{:S(2)}) collective-permute-start(f32[8,256]{1,0:T(8,128)S(1)} %get-tuple-element.21), channel_id=1, source_target_pairs={{0,3},{1,2},{2,1},{3,0},{4,7},{5,6},{6,5},{7,4},{8,11},{9,10},{10,... | collective-permute-start | bytes 24584 | tf_op jit(solution)/shard_map/ppermute | solution.py:67
  50.0 6.3 %collective-permute-start.20 = (f32[1,256]{1,0:T(1,128)S(1)}, f32[1,256]{1,0:T(1,128)S(1)}, u32[]{:S(2)}, u32[]{:S(2)}) collective-permute-start(f32[1,256]{1,0:T(1,128)S(1)} %get-tuple-element.23), channel_id=1, source_target_pairs={{0,12},{1,13},{2,14},{3,15},{4,8},{5,9},{6,10},{7,11},{8,20},{9,21... | collective-permute-start | bytes 3080 | tf_op jit(solution)/shard_map/ppermute | solution.py:67
  50.8 5.5 %collective-permute-start.19 = (f32[1,256]{1,0:T(1,128)S(1)}, f32[1,256]{1,0:T(1,128)S(1)}, u32[]{:S(2)}, u32[]{:S(2)}) collective-permute-start(f32[1,256]{1,0:T(1,128)S(1)} %get-tuple-element.24), channel_id=1, source_target_pairs={{0,9},{1,8},{2,11},{3,10},{4,13},{5,12},{6,15},{7,14},{8,17},{9,16... | collective-permute-start | bytes 3080 | tf_op jit(solution)/shard_map/ppermute | solution.py:67
  51.5 4.7 %collective-permute-start.18 = (f32[1,256]{1,0:T(1,128)S(1)}, f32[1,256]{1,0:T(1,128)S(1)}, u32[]{:S(2)}, u32[]{:S(2)}) collective-permute-start(f32[1,256]{1,0:T(1,128)S(1)} %get-tuple-element.22), channel_id=1, source_target_pairs={{0,5},{1,4},{2,7},{3,6},{4,1},{5,0},{6,3},{7,2},{8,13},{9,12},{10,... | collective-permute-start | bytes 3080 | tf_op jit(solution)/shard_map/ppermute | solution.py:67

commit v4 on v3

--- a/solution.py
+++ b/solution.py
@@ -382,8 +382,14 @@
         columns = found[0]
         bits = [1 << b for b in range(chips.bit_length() - 1)]
         if not last:
-            for bit in bits:
-                columns = columns + hop(columns, 0, bit)
+            if chips == 4:
+                shares = []
+                for k in (3, 1, 2):
+                    shares.append(hop(columns, 0, k))
+                columns = columns + shares[0] + shares[1] + shares[2]
+            else:
+                for bit in bits:
+                    columns = columns + hop(columns, 0, bit)
             wide = pair_groups(columns, True) if even else hop(columns, -1, 0)
             near = pair_groups(columns, False) if even else hop(columns, 1, 0)
         else:

time: 57.1 us -> 57.7 us (1.011)
  starting transfers between devices: 23.9 us -> 25.7 us
  waiting for transfers between devices: 20.1 us -> 18.9 us
    ppermute x13 -> x14, waiting for transfers between devices: 13.7 us -> 12.6 us  [hop(): lax.ppermute(x, BOTH, [(g * members + m, (g - up) % groups * members + (m...]
    ppermute x13 -> x14, starting transfers between devices: 19 us -> 19.8 us  [hop(): lax.ppermute(x, BOTH, [(g * members + m, (g - up) % groups * members + (m...]
    ppermute x4, starting transfers between devices: 1.68 us -> 2.49 us  [partner(): return lax.ppermute(x, 'member', [(i, i ^ 1) for i in range(size)])]
  transfers between devices with their start and end apart: 21 -> 22, of which waited for: 11 -> 11; matrix products, arithmetic and copies ran while one was open for 2% -> 2% of each run, Pallas kernels for 6% -> 6%
where the time goes in v4:
time: 57.7 us; the launch traced here: 57.5 us
  starting transfers between devices  25.7 us (45%)
  waiting for transfers between devices  18.9 us (33%)
  Pallas kernels  9.53 us (17%)
  between operations  1.38 us (2%)
  other arithmetic  1.36 us (2%)
  local copies, waits for them, and re-layouts  0.61 us (1%)
    ppermute x14, starting transfers between devices, hop(): lax.ppermute(x, BOTH, [(g * members + m, (g - up) % groups * members + (m...  19.8 us
    ppermute x14, waiting for transfers between devices, hop(): lax.ppermute(x, BOTH, [(g * members + m, (g - up) % groups * members + (m...  12.6 us
    ppermute x2, waiting for transfers between devices, pair_groups(): return lax.ppermute(x, BOTH, pairs)  3.41 us
    pallas_call x2, Pallas kernels, step(): pl.pallas_call(functools.partial(column_kernel, last), out_shape=(shaped(...  2.89 us
    ppermute x4, waiting for transfers between devices, partner(): return lax.ppermute(x, 'member', [(i, i ^ 1) for i in range(size)])  2.81 us
    ppermute x4, starting transfers between devices, partner(): return lax.ppermute(x, 'member', [(i, i ^ 1) for i in range(size)])  2.49 us
    pallas_call x1, Pallas kernels, step(): first, acc = first_call(units, lists_first, home, *early)  2.03 us
    pallas_call x1, Pallas kernels, step(): pl.pallas_call(functools.partial(second_kernel, [len(blocks) for blocks i...  1.57 us
  transfers between devices with their start and end apart: 22, of which 11 were waited for; matrix products, arithmetic and copies ran while one was open for 2% of the time, Pallas kernels for 6%

profile of v4, /device:TPU:0, one launch (start us, length us, event | category | flops | bytes accessed | tf_op | source)
XLA Modules:
  0.0 57.5 jit_solution(1523615876396451213)
XLA Ops:
  0.6 1.0 %collective-permute-start = (bf16[1024,256]{1,0:T(8,128)(2,1)}, bf16[1024,256]{1,0:T(8,128)(2,1)S(1)}, u32[]{:S(2)}, u32[]{:S(2)}) collective-permute-start(bf16[1024,256]{1,0:T(8,128)(2,1)} %param.5), channel_id=1, source_target_pairs={{0,0},{1,1},{2,2},{3,3},{4,4},{5,5},{6,6},{7,7},{8,8},{9,9},{10,10... | collective-permute-start | bytes 1572872 | tf_op jit(solution)/shard_map/ppermute | solution.py:292
  2.2 0.9 %collective-permute-start.1 = (bf16[256,256]{1,0:T(8,128)(2,1)}, bf16[256,256]{1,0:T(8,128)(2,1)S(1)}, u32[]{:S(2)}, u32[]{:S(2)}) collective-permute-start(bf16[256,256]{1,0:T(8,128)(2,1)} %param.6), channel_id=1, source_target_pairs={{0,0},{1,1},{2,2},{3,3},{4,4},{5,5},{6,6},{7,7},{8,8},{9,9},{10,10... | collective-permute-start | bytes 393224 | tf_op jit(solution)/shard_map/ppermute | solution.py:293
  3.1 2.6 %collective-permute-start.4 = (bf16[256,256]{1,0:T(8,128)(2,1)}, bf16[256,256]{1,0:T(8,128)(2,1)S(1)}, u32[]{:S(2)}, u32[]{:S(2)}) collective-permute-start(bf16[256,256]{1,0:T(8,128)(2,1)} %param.6), channel_id=1, source_target_pairs={{0,3},{1,2},{2,1},{3,0},{4,7},{5,6},{6,5},{7,4},{8,11},{9,10},{10,... | collective-permute-start | bytes 393224 | tf_op jit(solution)/shard_map/ppermute | solution.py:67
  6.3 0.7 %fusion.6 = s32[1,32]{1,0:T(1,128)S(1)} fusion(s32[1,32]{1,0:T(1,128)} %param.7, s32[1,32]{1,0:T(1,128)} %param.8, s32[]{:T(128)} %bitcast.5, s32[]{:T(128)S(6)} %select_n.27), kind=kLoop, calls=%fused_computation.24 | loop fusion | flops 1728 | bytes 392 | tf_op jit(solution)/shard_map/add | solution.py:51
  7.1 1.1 %collective-permute-done.3.theirs = s32[1,33]{1,0:T(1,128)S(1)} collective-permute-done((s32[1,33]{1,0:T(1,128)S(1)}, s32[1,33]{1,0:T(1,128)S(1)}, u32[]{:S(2)}, u32[]{:S(2)}) %collective-permute-start.3) | collective-permute-done | bytes 164 | tf_op jit(solution)/shard_map/ppermute | solution.py:89
  8.3 3.4 %collective-permute-start.7 = (bf16[256,256]{1,0:T(8,128)(2,1)}, bf16[256,256]{1,0:T(8,128)(2,1)S(1)}, u32[]{:S(2)}, u32[]{:S(2)}) collective-permute-start(bf16[256,256]{1,0:T(8,128)(2,1)} %param.6), channel_id=1, source_target_pairs={{0,25},{1,24},{2,27},{3,26},{4,29},{5,28},{6,31},{7,30},{8,1},{9,0... | collective-permute-start | bytes 393224 | tf_op jit(solution)/shard_map/ppermute | solution.py:67
  11.6 1.5 %collective-permute-start.5 = (bf16[256,256]{1,0:T(8,128)(2,1)}, bf16[256,256]{1,0:T(8,128)(2,1)S(1)}, u32[]{:S(2)}, u32[]{:S(2)}) collective-permute-start(bf16[256,256]{1,0:T(8,128)(2,1)} %param.6), channel_id=1, source_target_pairs={{0,5},{1,4},{2,7},{3,6},{4,1},{5,0},{6,3},{7,2},{8,13},{9,12},{10,... | collective-permute-start | bytes 393224 | tf_op jit(solution)/shard_map/ppermute | solution.py:67
  13.6 1.9 %collective-permute-done.7.refs_3_ = bf16[256,256]{1,0:T(8,128)(2,1)S(1)} collective-permute-done((bf16[256,256]{1,0:T(8,128)(2,1)}, bf16[256,256]{1,0:T(8,128)(2,1)S(1)}, u32[]{:S(2)}, u32[]{:S(2)}) %collective-permute-start.7) | collective-permute-done | bytes 131104 | tf_op jit(solution)/shard_map/ppermute | solution.py:67
  15.5 4.5 %collective-permute-start.10 = (bf16[256,256]{1,0:T(8,128)(2,1)}, bf16[256,256]{1,0:T(8,128)(2,1)S(1)}, u32[]{:S(2)}, u32[]{:S(2)}) collective-permute-start(bf16[256,256]{1,0:T(8,128)(2,1)} %param.6), channel_id=1, source_target_pairs={{0,31},{1,30},{2,29},{3,28},{4,27},{5,26},{6,25},{7,24},{8,7},{9,6... | collective-permute-start | bytes 393224 | tf_op jit(solution)/shard_map/ppermute | solution.py:67
  20.0 1.4 %collective-permute-start.8 = (bf16[256,256]{1,0:T(8,128)(2,1)S(1)}, bf16[256,256]{1,0:T(8,128)(2,1)S(1)}, u32[]{:S(2)}, u32[]{:S(2)}) collective-permute-start(bf16[256,256]{1,0:T(8,128)(2,1)S(1)} %collective-permute-done.7.refs_3_), channel_id=1, source_target_pairs={{0,3},{1,2},{2,1},{3,0},{4,7},{5,6},{6,5},{7,4},{8,11},{9,10},{10,... | collective-permute-start | bytes 393224 | tf_op jit(solution)/shard_map/ppermute | solution.py:67
  21.7 1.5 %prepare.1 = (bf16[8,256,256]{2,1,0:T(8,128)(2,1)S(1)}, bf16[256,256]{1,0:T(8,128)(2,1)S(1)}, s32[42]{0:T(128)S(1)}, s32[26]{0:T(128)S(1)}) custom-call(bf16[1024,256]{1,0:T(8,128)(2,1)S(1)} %collective-permute-done.own, bf16[256,256]{1,0:T(8,128)(2,1)S(1)} %collective-permute-done.1.target, bf16[1024,256]{1,0:T(8,128)(2,1)S(1)} %collective-permute-done.2.other, ...), custom_call_target="tpu_custom_call" | custom-call | flops 268435456 | bytes 1048576 | tf_op jit(solution)/shard_map/prepare/pallas_call | solution.py:325
  23.3 2.0 %first.1 = (bf16[40,256,256]{2,1,0:T(8,128)(2,1)S(1)}, f32[9,256,128]{2,1,0:T(8,128)S(1)}) custom-call(bf16[8,256,256]{2,1,0:T(8,128)(2,1)S(1)} %get-tuple-element.12.units, s32[42]{0:T(128)S(1)} %get-tuple-element.13.table.lists_first, bf16[256,256]{1,0:T(8,128)(2,1)S(1)} %get-tuple-element.14.home, bf16[256,256]{1,0:T(8,128)(2,1)S(1)} %collective-permute-done.4.refs_0_, ...), custom_call_target="tpu_custom_call" | custom-call | flops 1342177280 | bytes 5242880 | tf_op jit(solution)/shard_map/first/pallas_call | solution.py:341
  25.9 1.0 %collective-permute-done.9.refs_1_ = bf16[256,256]{1,0:T(8,128)(2,1)S(1)} collective-permute-done((bf16[256,256]{1,0:T(8,128)(2,1)S(1)}, bf16[256,256]{1,0:T(8,128)(2,1)S(1)}, u32[]{:S(2)}, u32[]{:S(2)}) %collective-permute-start.9) | collective-permute-done | bytes 131104 | tf_op jit(solution)/shard_map/ppermute | solution.py:67
  26.9 1.6 %second.1 = (bf16[24,256,256]{2,1,0:T(8,128)(2,1)S(1)}, f32[8,256]{1,0:T(8,128)S(1)}) custom-call(bf16[8,256,256]{2,1,0:T(8,128)(2,1)S(1)} %get-tuple-element.12.units, s32[26]{0:T(128)S(1)} %get-tuple-element.16.table.lists_second, f32[9,256,128]{2,1,0:T(8,128)S(1)} %get-tuple-element.17.before, bf16[256,256]{1,0:T(8,128)(2,1)S(1)} %collective-permute-done.8.refs_0_, ...), custom_call_target="tpu_custom_call" | custom-call | flops 805306368 | bytes 3145728 | tf_op jit(solution)/shard_map/second/pallas_call | solution.py:342
  28.5 0.6 %collective-permute-start.11 = (f32[8,256]{1,0:T(8,128)S(1)}, f32[8,256]{1,0:T(8,128)S(1)}, u32[]{:S(2)}, u32[]{:S(2)}) collective-permute-start(f32[8,256]{1,0:T(8,128)S(1)} %get-tuple-element.19.rows), channel_id=1, source_target_pairs={{0,1},{1,0},{2,3},{3,2},{4,5},{5,4},{6,7},{7,6},{8,9},{9,8},{10,11... | collective-permute-start | bytes 24584 | tf_op jit(solution)/shard_map/ppermute | solution.py:89
  29.1 0.8 %collective-permute-done.11.arrived = f32[8,256]{1,0:T(8,128)S(1)} collective-permute-done((f32[8,256]{1,0:T(8,128)S(1)}, f32[8,256]{1,0:T(8,128)S(1)}, u32[]{:S(2)}, u32[]{:S(2)}) %collective-permute-start.11) | collective-permute-done | bytes 8224 | tf_op jit(solution)/shard_map/ppermute | solution.py:89
  29.9 1.4 %columns.2 = f32[8,256]{1,0:T(8,128)S(1)} custom-call(bf16[40,256,256]{2,1,0:T(8,128)(2,1)S(1)} %get-tuple-element.15.first, bf16[24,256,256]{2,1,0:T(8,128)(2,1)S(1)} %get-tuple-element.18.second, s32[42]{0:T(128)S(1)} %get-tuple-element.13.table.lists_first, s32[26]{0:T(128)S(1)} %get-tuple-element.16.table.lists_second, ...), custom_call_target="tpu_custom_call" | custom-call | tf_op jit(solution)/shard_map/columns/pallas_call | solution.py:370
  31.3 1.4 %collective-permute-start.14 = (f32[8,256]{1,0:T(8,128)S(1)}, f32[8,256]{1,0:T(8,128)S(1)}, u32[]{:S(2)}, u32[]{:S(2)}) collective-permute-start(f32[8,256]{1,0:T(8,128)S(1)} %columns.2), channel_id=1, source_target_pairs={{0,5},{1,4},{2,7},{3,6},{4,1},{5,0},{6,3},{7,2},{8,13},{9,12},{10,... | collective-permute-start | bytes 24584 | tf_op jit(solution)/shard_map/ppermute | solution.py:67
  32.8 1.8 %collective-permute-start.12 = (f32[8,256]{1,0:T(8,128)S(1)}, f32[8,256]{1,0:T(8,128)S(1)}, u32[]{:S(2)}, u32[]{:S(2)}) collective-permute-start(f32[8,256]{1,0:T(8,128)S(1)} %columns.2), channel_id=1, source_target_pairs={{0,6},{1,7},{2,4},{3,5},{4,2},{5,3},{6,0},{7,1},{8,14},{9,15},{10,... | collective-permute-start | bytes 24584 | tf_op jit(solution)/shard_map/ppermute | solution.py:67
  34.6 1.2 %collective-permute-done.13 = f32[8,256]{1,0:T(8,128)S(1)} collective-permute-done((f32[8,256]{1,0:T(8,128)S(1)}, f32[8,256]{1,0:T(8,128)S(1)}, u32[]{:S(2)}, u32[]{:S(2)}) %collective-permute-start.13) | collective-permute-done | bytes 8224 | tf_op jit(solution)/shard_map/ppermute | solution.py:67
  35.9 1.5 %collective-permute-done.12 = f32[8,256]{1,0:T(8,128)S(1)} collective-permute-done((f32[8,256]{1,0:T(8,128)S(1)}, f32[8,256]{1,0:T(8,128)S(1)}, u32[]{:S(2)}, u32[]{:S(2)}) %collective-permute-start.12) | collective-permute-done | bytes 8224 | tf_op jit(solution)/shard_map/ppermute | solution.py:67
  37.3 1.5 %collective-permute-start.15 = (f32[8,256]{1,0:T(8,128)S(1)}, f32[8,256]{1,0:T(8,128)S(1)}, u32[]{:S(2)}, u32[]{:S(2)}) collective-permute-start(f32[8,256]{1,0:T(8,128)S(1)} %add_add_fusion.columns), channel_id=1, source_target_pairs={{0,25},{1,24},{2,27},{3,26},{4,29},{5,28},{6,31},{7,30},{8,17},{9,... | collective-permute-start | bytes 24584 | tf_op jit(solution)/shard_map/ppermute | solution.py:84
  38.8 3.4 %collective-permute-done.15.wide = f32[8,256]{1,0:T(8,128)S(1)} collective-permute-done((f32[8,256]{1,0:T(8,128)S(1)}, f32[8,256]{1,0:T(8,128)S(1)}, u32[]{:S(2)}, u32[]{:S(2)}) %collective-permute-start.15) | collective-permute-done | bytes 8224 | tf_op jit(solution)/shard_map/ppermute | solution.py:84
  42.2 1.5 %rows.1 = f32[8,256]{1,0:T(8,128)S(1)} custom-call(bf16[40,256,256]{2,1,0:T(8,128)(2,1)S(1)} %get-tuple-element.15.first, bf16[24,256,256]{2,1,0:T(8,128)(2,1)S(1)} %get-tuple-element.18.second, s32[42]{0:T(128)S(1)} %get-tuple-element.13.table.lists_first, s32[26]{0:T(128)S(1)} %get-tuple-element.16.table.lists_second, f32[8,256]{1,0:T(8,128)S(1)} %add_add_fusion.columns, ...), custom_call_target="tpu_custom_call" | custom-call | tf_op jit(solution)/shard_map/rows/pallas_call | solution.py:361
  43.7 1.4 %collective-permute-start.17 = (f32[8,256]{1,0:T(8,128)S(1)}, f32[8,256]{1,0:T(8,128)S(1)}, u32[]{:S(2)}, u32[]{:S(2)}) collective-permute-start(f32[8,256]{1,0:T(8,128)S(1)} %rows.1), channel_id=1, source_target_pairs={{0,1},{1,0},{2,3},{3,2},{4,5},{5,4},{6,7},{7,6},{8,9},{9,8},{10,11... | collective-permute-start | bytes 24584 | tf_op jit(solution)/shard_map/ppermute | solution.py:89
  45.1 0.8 %collective-permute-done.17.arrived = f32[8,256]{1,0:T(8,128)S(1)} collective-permute-done((f32[8,256]{1,0:T(8,128)S(1)}, f32[8,256]{1,0:T(8,128)S(1)}, u32[]{:S(2)}, u32[]{:S(2)}) %collective-permute-start.17) | collective-permute-done | bytes 8224 | tf_op jit(solution)/shard_map/ppermute | solution.py:89
  45.9 1.4 %columns.3 = (f32[8,256]{1,0:T(8,128)S(1)}, f32[4,256]{1,0:T(4,128)S(1)}) custom-call(bf16[40,256,256]{2,1,0:T(8,128)(2,1)S(1)} %get-tuple-element.15.first, bf16[24,256,256]{2,1,0:T(8,128)(2,1)S(1)} %get-tuple-element.18.second, s32[42]{0:T(128)S(1)} %get-tuple-element.13.table.lists_first, s32[26]{0:T(128)S(1)} %get-tuple-element.16.table.lists_second, ...), custom_call_target="tpu_custom_call" | custom-call | tf_op jit(solution)/shard_map/columns/pallas_call | solution.py:370
  47.8 2.7 %collective-permute-done.18 = f32[8,256]{1,0:T(8,128)S(1)} collective-permute-done((f32[8,256]{1,0:T(8,128)S(1)}, f32[8,256]{1,0:T(8,128)S(1)}, u32[]{:S(2)}, u32[]{:S(2)}) %collective-permute-start.18) | collective-permute-done | bytes 8224 | tf_op jit(solution)/shard_map/ppermute | solution.py:67
  50.7 1.9 %collective-permute-start.19 = (f32[1,256]{1,0:T(1,128)S(1)}, f32[1,256]{1,0:T(1,128)S(1)}, u32[]{:S(2)}, u32[]{:S(2)}) collective-permute-start(f32[1,256]{1,0:T(1,128)S(1)} %get-tuple-element.22), channel_id=1, source_target_pairs={{0,5},{1,4},{2,7},{3,6},{4,1},{5,0},{6,3},{7,2},{8,13},{9,12},{10,... | collective-permute-start | bytes 3080 | tf_op jit(solution)/shard_map/ppermute | solution.py:67
  52.5 0.6 %copy.7 = f32[1,2,4,128]{3,1,2,0:T(2,128)} copy(f32[1,2,4,128]{3,2,1,0:T(4,128)S(1)} %bitcast.7) | data formatting | bytes 8192
  53.1 3.7 %collective-permute-done.21 = f32[1,256]{1,0:T(1,128)S(1)} collective-permute-done((f32[1,256]{1,0:T(1,128)S(1)}, f32[1,256]{1,0:T(1,128)S(1)}, u32[]{:S(2)}, u32[]{:S(2)}) %collective-permute-start.21) | collective-permute-done | bytes 1056 | tf_op jit(solution)/shard_map/ppermute | solution.py:67
  56.9 0.6 %divide_log_fusion = f32[1,256]{1,0:T(1,128)} fusion(f32[1,256]{1,0:T(1,128)S(1)} %collective-permute-done.21, f32[1,256]{1,0:T(1,128)S(1)} %collective-permute-done.20, f32[1,256]{1,0:T(1,128)S(1)} %collective-permute-done.19, f32[8,256]{1,0:T(8,128)S(1)} %add.65, s32[]{:T(128)S(6)} %select_n.29), kind=kLoop, calls=%fused_computation.13 | loop fusion | flops 1024 | bytes 5124 | tf_op jit(solution)/shard_map/log | solution.py:410
  (25 shorter events, 2.4 us)
Async XLA Ops:
  0.6 19.4 %collective-permute-start = (bf16[1024,256]{1,0:T(8,128)(2,1)}, bf16[1024,256]{1,0:T(8,128)(2,1)S(1)}, u32[]{:S(2)}, u32[]{:S(2)}) collective-permute-start(bf16[1024,256]{1,0:T(8,128)(2,1)} %param.5), channel_id=1, source_target_pairs={{0,0},{1,1},{2,2},{3,3},{4,4},{5,5},{6,6},{7,7},{8,8},{9,9},{10,10... | collective-permute-start | bytes 1572872 | tf_op jit(solution)/shard_map/ppermute | solution.py:292
  1.7 19.8 %collective-permute-start.2 = (bf16[1024,256]{1,0:T(8,128)(2,1)}, bf16[1024,256]{1,0:T(8,128)(2,1)S(1)}, u32[]{:S(2)}, u32[]{:S(2)}) collective-permute-start(bf16[1024,256]{1,0:T(8,128)(2,1)} %param.5), channel_id=1, source_target_pairs={{0,1},{1,0},{2,3},{3,2},{4,5},{5,4},{6,7},{7,6},{8,9},{9,8},{10,11... | collective-permute-start | bytes 1572872 | tf_op jit(solution)/shard_map/ppermute | solution.py:89
  2.2 9.5 %collective-permute-start.1 = (bf16[256,256]{1,0:T(8,128)(2,1)}, bf16[256,256]{1,0:T(8,128)(2,1)S(1)}, u32[]{:S(2)}, u32[]{:S(2)}) collective-permute-start(bf16[256,256]{1,0:T(8,128)(2,1)} %param.6), channel_id=1, source_target_pairs={{0,0},{1,1},{2,2},{3,3},{4,4},{5,5},{6,6},{7,7},{8,8},{9,9},{10,10... | collective-permute-start | bytes 393224 | tf_op jit(solution)/shard_map/ppermute | solution.py:293
  3.1 10.0 %collective-permute-start.4 = (bf16[256,256]{1,0:T(8,128)(2,1)}, bf16[256,256]{1,0:T(8,128)(2,1)S(1)}, u32[]{:S(2)}, u32[]{:S(2)}) collective-permute-start(bf16[256,256]{1,0:T(8,128)(2,1)} %param.6), channel_id=1, source_target_pairs={{0,3},{1,2},{2,1},{3,0},{4,7},{5,6},{6,5},{7,4},{8,11},{9,10},{10,... | collective-permute-start | bytes 393224 | tf_op jit(solution)/shard_map/ppermute | solution.py:67
  7.1 1.2 %collective-permute-start.3 = (s32[1,33]{1,0:T(1,128)S(1)}, s32[1,33]{1,0:T(1,128)S(1)}, u32[]{:S(2)}, u32[]{:S(2)}) collective-permute-start(s32[1,33]{1,0:T(1,128)S(1)} %pad_add_fusion.mine), channel_id=1, source_target_pairs={{0,1},{1,0},{2,3},{3,2},{4,5},{5,4},{6,7},{7,6},{8,9},{9,8},{10,11... | collective-permute-start | bytes 404 | tf_op jit(solution)/shard_map/ppermute | solution.py:89
  8.3 7.2 %collective-permute-start.7 = (bf16[256,256]{1,0:T(8,128)(2,1)}, bf16[256,256]{1,0:T(8,128)(2,1)S(1)}, u32[]{:S(2)}, u32[]{:S(2)}) collective-permute-start(bf16[256,256]{1,0:T(8,128)(2,1)} %param.6), channel_id=1, source_target_pairs={{0,25},{1,24},{2,27},{3,26},{4,29},{5,28},{6,31},{7,30},{8,1},{9,0... | collective-permute-start | bytes 393224 | tf_op jit(solution)/shard_map/ppermute | solution.py:67
  11.6 11.7 %collective-permute-start.5 = (bf16[256,256]{1,0:T(8,128)(2,1)}, bf16[256,256]{1,0:T(8,128)(2,1)S(1)}, u32[]{:S(2)}, u32[]{:S(2)}) collective-permute-start(bf16[256,256]{1,0:T(8,128)(2,1)} %param.6), channel_id=1, source_target_pairs={{0,5},{1,4},{2,7},{3,6},{4,1},{5,0},{6,3},{7,2},{8,13},{9,12},{10,... | collective-permute-start | bytes 393224 | tf_op jit(solution)/shard_map/ppermute | solution.py:67
  13.1 10.2 %collective-permute-start.6 = (bf16[256,256]{1,0:T(8,128)(2,1)}, bf16[256,256]{1,0:T(8,128)(2,1)S(1)}, u32[]{:S(2)}, u32[]{:S(2)}) collective-permute-start(bf16[256,256]{1,0:T(8,128)(2,1)} %param.6), channel_id=1, source_target_pairs={{0,6},{1,7},{2,4},{3,5},{4,2},{5,3},{6,0},{7,1},{8,14},{9,15},{10,... | collective-permute-start | bytes 393224 | tf_op jit(solution)/shard_map/ppermute | solution.py:67
  15.5 9.9 %collective-permute-start.10 = (bf16[256,256]{1,0:T(8,128)(2,1)}, bf16[256,256]{1,0:T(8,128)(2,1)S(1)}, u32[]{:S(2)}, u32[]{:S(2)}) collective-permute-start(bf16[256,256]{1,0:T(8,128)(2,1)} %param.6), channel_id=1, source_target_pairs={{0,31},{1,30},{2,29},{3,28},{4,27},{5,26},{6,25},{7,24},{8,7},{9,6... | collective-permute-start | bytes 393224 | tf_op jit(solution)/shard_map/ppermute | solution.py:67
  20.0 5.9 %collective-permute-start.8 = (bf16[256,256]{1,0:T(8,128)(2,1)S(1)}, bf16[256,256]{1,0:T(8,128)(2,1)S(1)}, u32[]{:S(2)}, u32[]{:S(2)}) collective-permute-start(bf16[256,256]{1,0:T(8,128)(2,1)S(1)} %collective-permute-done.7.refs_3_), channel_id=1, source_target_pairs={{0,3},{1,2},{2,1},{3,0},{4,7},{5,6},{6,5},{7,4},{8,11},{9,10},{10,... | collective-permute-start | bytes 393224 | tf_op jit(solution)/shard_map/ppermute | solution.py:67
  21.5 5.4 %collective-permute-start.9 = (bf16[256,256]{1,0:T(8,128)(2,1)S(1)}, bf16[256,256]{1,0:T(8,128)(2,1)S(1)}, u32[]{:S(2)}, u32[]{:S(2)}) collective-permute-start(bf16[256,256]{1,0:T(8,128)(2,1)S(1)} %collective-permute-done.7.refs_3_), channel_id=1, source_target_pairs={{0,5},{1,4},{2,7},{3,6},{4,1},{5,0},{6,3},{7,2},{8,13},{9,12},{10,... | collective-permute-start | bytes 393224 | tf_op jit(solution)/shard_map/ppermute | solution.py:67
  28.5 1.4 %collective-permute-start.11 = (f32[8,256]{1,0:T(8,128)S(1)}, f32[8,256]{1,0:T(8,128)S(1)}, u32[]{:S(2)}, u32[]{:S(2)}) collective-permute-start(f32[8,256]{1,0:T(8,128)S(1)} %get-tuple-element.19.rows), channel_id=1, source_target_pairs={{0,1},{1,0},{2,3},{3,2},{4,5},{5,4},{6,7},{7,6},{8,9},{9,8},{10,11... | collective-permute-start | bytes 24584 | tf_op jit(solution)/shard_map/ppermute | solution.py:89
  31.3 3.3 %collective-permute-start.14 = (f32[8,256]{1,0:T(8,128)S(1)}, f32[8,256]{1,0:T(8,128)S(1)}, u32[]{:S(2)}, u32[]{:S(2)}) collective-permute-start(f32[8,256]{1,0:T(8,128)S(1)} %columns.2), channel_id=1, source_target_pairs={{0,5},{1,4},{2,7},{3,6},{4,1},{5,0},{6,3},{7,2},{8,13},{9,12},{10,... | collective-permute-start | bytes 24584 | tf_op jit(solution)/shard_map/ppermute | solution.py:67
  32.8 3.1 %collective-permute-start.13 = (f32[8,256]{1,0:T(8,128)S(1)}, f32[8,256]{1,0:T(8,128)S(1)}, u32[]{:S(2)}, u32[]{:S(2)}) collective-permute-start(f32[8,256]{1,0:T(8,128)S(1)} %columns.2), channel_id=1, source_target_pairs={{0,3},{1,2},{2,1},{3,0},{4,7},{5,6},{6,5},{7,4},{8,11},{9,10},{10,... | collective-permute-start | bytes 24584 | tf_op jit(solution)/shard_map/ppermute | solution.py:67
  32.8 4.5 %collective-permute-start.12 = (f32[8,256]{1,0:T(8,128)S(1)}, f32[8,256]{1,0:T(8,128)S(1)}, u32[]{:S(2)}, u32[]{:S(2)}) collective-permute-start(f32[8,256]{1,0:T(8,128)S(1)} %columns.2), channel_id=1, source_target_pairs={{0,6},{1,7},{2,4},{3,5},{4,2},{5,3},{6,0},{7,1},{8,14},{9,15},{10,... | collective-permute-start | bytes 24584 | tf_op jit(solution)/shard_map/ppermute | solution.py:67
  37.3 4.9 %collective-permute-start.15 = (f32[8,256]{1,0:T(8,128)S(1)}, f32[8,256]{1,0:T(8,128)S(1)}, u32[]{:S(2)}, u32[]{:S(2)}) collective-permute-start(f32[8,256]{1,0:T(8,128)S(1)} %add_add_fusion.columns), channel_id=1, source_target_pairs={{0,25},{1,24},{2,27},{3,26},{4,29},{5,28},{6,31},{7,30},{8,17},{9,... | collective-permute-start | bytes 24584 | tf_op jit(solution)/shard_map/ppermute | solution.py:84
  38.8 3.4 %collective-permute-start.16 = (f32[8,256]{1,0:T(8,128)S(1)}, f32[8,256]{1,0:T(8,128)S(1)}, u32[]{:S(2)}, u32[]{:S(2)}) collective-permute-start(f32[8,256]{1,0:T(8,128)S(1)} %add_add_fusion.columns), channel_id=1, source_target_pairs={{0,9},{1,8},{2,11},{3,10},{4,13},{5,12},{6,15},{7,14},{8,1},{9,0},... | collective-permute-start | bytes 24584 | tf_op jit(solution)/shard_map/ppermute | solution.py:84
  43.7 2.2 %collective-permute-start.17 = (f32[8,256]{1,0:T(8,128)S(1)}, f32[8,256]{1,0:T(8,128)S(1)}, u32[]{:S(2)}, u32[]{:S(2)}) collective-permute-start(f32[8,256]{1,0:T(8,128)S(1)} %rows.1), channel_id=1, source_target_pairs={{0,1},{1,0},{2,3},{3,2},{4,5},{5,4},{6,7},{7,6},{8,9},{9,8},{10,11... | collective-permute-start | bytes 24584 | tf_op jit(solution)/shard_map/ppermute | solution.py:89
  47.4 3.1 %collective-permute-start.18 = (f32[8,256]{1,0:T(8,128)S(1)}, f32[8,256]{1,0:T(8,128)S(1)}, u32[]{:S(2)}, u32[]{:S(2)}) collective-permute-start(f32[8,256]{1,0:T(8,128)S(1)} %get-tuple-element.21), channel_id=1, source_target_pairs={{0,3},{1,2},{2,1},{3,0},{4,7},{5,6},{6,5},{7,4},{8,11},{9,10},{10,... | collective-permute-start | bytes 24584 | tf_op jit(solution)/shard_map/ppermute | solution.py:67
  50.5 6.3 %collective-permute-start.21 = (f32[1,256]{1,0:T(1,128)S(1)}, f32[1,256]{1,0:T(1,128)S(1)}, u32[]{:S(2)}, u32[]{:S(2)}) collective-permute-start(f32[1,256]{1,0:T(1,128)S(1)} %get-tuple-element.23), channel_id=1, source_target_pairs={{0,12},{1,13},{2,14},{3,15},{4,8},{5,9},{6,10},{7,11},{8,20},{9,21... | collective-permute-start | bytes 3080 | tf_op jit(solution)/shard_map/ppermute | solution.py:67
  50.6 6.3 %collective-permute-start.20 = (f32[1,256]{1,0:T(1,128)S(1)}, f32[1,256]{1,0:T(1,128)S(1)}, u32[]{:S(2)}, u32[]{:S(2)}) collective-permute-start(f32[1,256]{1,0:T(1,128)S(1)} %get-tuple-element.24), channel_id=1, source_target_pairs={{0,9},{1,8},{2,11},{3,10},{4,13},{5,12},{6,15},{7,14},{8,17},{9,16... | collective-permute-start | bytes 3080 | tf_op jit(solution)/shard_map/ppermute | solution.py:67
  50.7 6.2 %collective-permute-start.19 = (f32[1,256]{1,0:T(1,128)S(1)}, f32[1,256]{1,0:T(1,128)S(1)}, u32[]{:S(2)}, u32[]{:S(2)}) collective-permute-start(f32[1,256]{1,0:T(1,128)S(1)} %get-tuple-element.22), channel_id=1, source_target_pairs={{0,5},{1,4},{2,7},{3,6},{4,1},{5,0},{6,3},{7,2},{8,13},{9,12},{10,... | collective-permute-start | bytes 3080 | tf_op jit(solution)/shard_map/ppermute | solution.py:67

commit v5 on v4

--- a/solution.py
+++ b/solution.py
@@ -123,13 +123,8 @@
 
 
 def rows_out(acc, out):
-    tiles = out.shape[0]
-    cells, lanes = acc.shape[1:]
-    lane = lax.broadcasted_iota(jnp.int32, (cells, lanes), 1)
-    table = jnp.zeros((cells, lanes), F32)
-    for s in range(tiles):
-        table = jnp.where(lane == s, jnp.sum(acc[s], axis=1, keepdims=True), table)
-    out[...] = jnp.transpose(table)[:tiles]
+    for s in range(out.shape[0]):
+        out[s : s + 1] = jnp.sum(jnp.transpose(acc[s]), axis=0, keepdims=True)
 
 
 def add_halves(acc, s, values):
@@ -394,9 +389,9 @@
             near = pair_groups(columns, False) if even else hop(columns, 1, 0)
         else:
             chip = lax.axis_index("member") // CORES
-            for bit in bits[:-1]:
+            for bit in bits[1:]:
                 columns = columns + hop(columns, 0, bit)
-            far = bits[-1]
+            far = bits[0]
 
             def row(index):
                 return lax.dynamic_slice_in_dim(columns, index, 1, 0)

time: 57.7 us -> 57.7 us (level)
  no operation moved by 1% of the time
where the time goes in v5:
time: 57.7 us; the launch traced here: 57.5 us
  starting transfers between devices  26.1 us (45%)
  waiting for transfers between devices  18.5 us (32%)
  Pallas kernels  9.47 us (16%)
  between operations  1.38 us (2%)
  other arithmetic  1.36 us (2%)
  local copies, waits for them, and re-layouts  0.61 us (1%)
    ppermute x14, starting transfers between devices, hop(): lax.ppermute(x, BOTH, [(g * members + m, (g - up) % groups * members + (m...  20.2 us
    ppermute x14, waiting for transfers between devices, hop(): lax.ppermute(x, BOTH, [(g * members + m, (g - up) % groups * members + (m...  12.3 us
    ppermute x2, waiting for transfers between devices, pair_groups(): return lax.ppermute(x, BOTH, pairs)  3.41 us
    pallas_call x2, Pallas kernels, step(): pl.pallas_call(functools.partial(column_kernel, last), out_shape=(shaped(...  2.89 us
    ppermute x4, waiting for transfers between devices, partner(): return lax.ppermute(x, 'member', [(i, i ^ 1) for i in range(size)])  2.81 us
    ppermute x4, starting transfers between devices, partner(): return lax.ppermute(x, 'member', [(i, i ^ 1) for i in range(size)])  2.54 us
    pallas_call x1, Pallas kernels, step(): first, acc = first_call(units, lists_first, home, *early)  2.03 us
    pallas_call x1, Pallas kernels, step(): prepare(own_source, own_target, partner_source, info, partner_info)  1.55 us
  transfers between devices with their start and end apart: 22, of which 11 were waited for; matrix products, arithmetic and copies ran while one was open for 2% of the time, Pallas kernels for 6%

profile of v5, /device:TPU:0, one launch (start us, length us, event | category | flops | bytes accessed | tf_op | source)
XLA Modules:
  0.0 57.5 jit_solution(7567760506095017685)
XLA Ops:
  0.6 1.0 %collective-permute-start = (bf16[1024,256]{1,0:T(8,128)(2,1)}, bf16[1024,256]{1,0:T(8,128)(2,1)S(1)}, u32[]{:S(2)}, u32[]{:S(2)}) collective-permute-start(bf16[1024,256]{1,0:T(8,128)(2,1)} %param.5), channel_id=1, source_target_pairs={{0,0},{1,1},{2,2},{3,3},{4,4},{5,5},{6,6},{7,7},{8,8},{9,9},{10,10... | collective-permute-start | bytes 1572872 | tf_op jit(solution)/shard_map/ppermute | solution.py:287
  2.2 0.9 %collective-permute-start.1 = (bf16[256,256]{1,0:T(8,128)(2,1)}, bf16[256,256]{1,0:T(8,128)(2,1)S(1)}, u32[]{:S(2)}, u32[]{:S(2)}) collective-permute-start(bf16[256,256]{1,0:T(8,128)(2,1)} %param.6), channel_id=1, source_target_pairs={{0,0},{1,1},{2,2},{3,3},{4,4},{5,5},{6,6},{7,7},{8,8},{9,9},{10,10... | collective-permute-start | bytes 393224 | tf_op jit(solution)/shard_map/ppermute | solution.py:288
  3.1 2.6 %collective-permute-start.4 = (bf16[256,256]{1,0:T(8,128)(2,1)}, bf16[256,256]{1,0:T(8,128)(2,1)S(1)}, u32[]{:S(2)}, u32[]{:S(2)}) collective-permute-start(bf16[256,256]{1,0:T(8,128)(2,1)} %param.6), channel_id=1, source_target_pairs={{0,3},{1,2},{2,1},{3,0},{4,7},{5,6},{6,5},{7,4},{8,11},{9,10},{10,... | collective-permute-start | bytes 393224 | tf_op jit(solution)/shard_map/ppermute | solution.py:67
  6.3 0.7 %fusion.6 = s32[1,32]{1,0:T(1,128)S(1)} fusion(s32[1,32]{1,0:T(1,128)} %param.7, s32[1,32]{1,0:T(1,128)} %param.8, s32[]{:T(128)} %bitcast.5, s32[]{:T(128)S(6)} %select_n.27), kind=kLoop, calls=%fused_computation.24 | loop fusion | flops 1728 | bytes 392 | tf_op jit(solution)/shard_map/add | solution.py:51
  7.1 1.1 %collective-permute-done.3.theirs = s32[1,33]{1,0:T(1,128)S(1)} collective-permute-done((s32[1,33]{1,0:T(1,128)S(1)}, s32[1,33]{1,0:T(1,128)S(1)}, u32[]{:S(2)}, u32[]{:S(2)}) %collective-permute-start.3) | collective-permute-done | bytes 164 | tf_op jit(solution)/shard_map/ppermute | solution.py:89
  8.3 3.4 %collective-permute-start.7 = (bf16[256,256]{1,0:T(8,128)(2,1)}, bf16[256,256]{1,0:T(8,128)(2,1)S(1)}, u32[]{:S(2)}, u32[]{:S(2)}) collective-permute-start(bf16[256,256]{1,0:T(8,128)(2,1)} %param.6), channel_id=1, source_target_pairs={{0,25},{1,24},{2,27},{3,26},{4,29},{5,28},{6,31},{7,30},{8,1},{9,0... | collective-permute-start | bytes 393224 | tf_op jit(solution)/shard_map/ppermute | solution.py:67
  11.6 1.5 %collective-permute-start.5 = (bf16[256,256]{1,0:T(8,128)(2,1)}, bf16[256,256]{1,0:T(8,128)(2,1)S(1)}, u32[]{:S(2)}, u32[]{:S(2)}) collective-permute-start(bf16[256,256]{1,0:T(8,128)(2,1)} %param.6), channel_id=1, source_target_pairs={{0,5},{1,4},{2,7},{3,6},{4,1},{5,0},{6,3},{7,2},{8,13},{9,12},{10,... | collective-permute-start | bytes 393224 | tf_op jit(solution)/shard_map/ppermute | solution.py:67
  13.6 1.9 %collective-permute-done.7.refs_3_ = bf16[256,256]{1,0:T(8,128)(2,1)S(1)} collective-permute-done((bf16[256,256]{1,0:T(8,128)(2,1)}, bf16[256,256]{1,0:T(8,128)(2,1)S(1)}, u32[]{:S(2)}, u32[]{:S(2)}) %collective-permute-start.7) | collective-permute-done | bytes 131104 | tf_op jit(solution)/shard_map/ppermute | solution.py:67
  15.5 4.5 %collective-permute-start.10 = (bf16[256,256]{1,0:T(8,128)(2,1)}, bf16[256,256]{1,0:T(8,128)(2,1)S(1)}, u32[]{:S(2)}, u32[]{:S(2)}) collective-permute-start(bf16[256,256]{1,0:T(8,128)(2,1)} %param.6), channel_id=1, source_target_pairs={{0,31},{1,30},{2,29},{3,28},{4,27},{5,26},{6,25},{7,24},{8,7},{9,6... | collective-permute-start | bytes 393224 | tf_op jit(solution)/shard_map/ppermute | solution.py:67
  20.0 1.4 %collective-permute-start.8 = (bf16[256,256]{1,0:T(8,128)(2,1)S(1)}, bf16[256,256]{1,0:T(8,128)(2,1)S(1)}, u32[]{:S(2)}, u32[]{:S(2)}) collective-permute-start(bf16[256,256]{1,0:T(8,128)(2,1)S(1)} %collective-permute-done.7.refs_3_), channel_id=1, source_target_pairs={{0,3},{1,2},{2,1},{3,0},{4,7},{5,6},{6,5},{7,4},{8,11},{9,10},{10,... | collective-permute-start | bytes 393224 | tf_op jit(solution)/shard_map/ppermute | solution.py:67
  21.7 1.5 %prepare.1 = (bf16[8,256,256]{2,1,0:T(8,128)(2,1)S(1)}, bf16[256,256]{1,0:T(8,128)(2,1)S(1)}, s32[42]{0:T(128)S(1)}, s32[26]{0:T(128)S(1)}) custom-call(bf16[1024,256]{1,0:T(8,128)(2,1)S(1)} %collective-permute-done.own, bf16[256,256]{1,0:T(8,128)(2,1)S(1)} %collective-permute-done.1.target, bf16[1024,256]{1,0:T(8,128)(2,1)S(1)} %collective-permute-done.2.other, ...), custom_call_target="tpu_custom_call" | custom-call | flops 268435456 | bytes 1048576 | tf_op jit(solution)/shard_map/prepare/pallas_call | solution.py:320
  23.3 2.0 %first.1 = (bf16[40,256,256]{2,1,0:T(8,128)(2,1)S(1)}, f32[9,256,128]{2,1,0:T(8,128)S(1)}) custom-call(bf16[8,256,256]{2,1,0:T(8,128)(2,1)S(1)} %get-tuple-element.12.units, s32[42]{0:T(128)S(1)} %get-tuple-element.13.table.lists_first, bf16[256,256]{1,0:T(8,128)(2,1)S(1)} %get-tuple-element.14.home, bf16[256,256]{1,0:T(8,128)(2,1)S(1)} %collective-permute-done.4.refs_0_, ...), custom_call_target="tpu_custom_call" | custom-call | flops 1342177280 | bytes 5242880 | tf_op jit(solution)/shard_map/first/pallas_call | solution.py:336
  25.9 1.0 %collective-permute-done.9.refs_1_ = bf16[256,256]{1,0:T(8,128)(2,1)S(1)} collective-permute-done((bf16[256,256]{1,0:T(8,128)(2,1)S(1)}, bf16[256,256]{1,0:T(8,128)(2,1)S(1)}, u32[]{:S(2)}, u32[]{:S(2)}) %collective-permute-start.9) | collective-permute-done | bytes 131104 | tf_op jit(solution)/shard_map/ppermute | solution.py:67
  26.9 1.5 %second.1 = (bf16[24,256,256]{2,1,0:T(8,128)(2,1)S(1)}, f32[8,256]{1,0:T(8,128)S(1)}) custom-call(bf16[8,256,256]{2,1,0:T(8,128)(2,1)S(1)} %get-tuple-element.12.units, s32[26]{0:T(128)S(1)} %get-tuple-element.16.table.lists_second, f32[9,256,128]{2,1,0:T(8,128)S(1)} %get-tuple-element.17.before, bf16[256,256]{1,0:T(8,128)(2,1)S(1)} %collective-permute-done.8.refs_0_, ...), custom_call_target="tpu_custom_call" | custom-call | flops 805306368 | bytes 3145728 | tf_op jit(solution)/shard_map/second/pallas_call | solution.py:337
  28.5 0.6 %collective-permute-start.11 = (f32[8,256]{1,0:T(8,128)S(1)}, f32[8,256]{1,0:T(8,128)S(1)}, u32[]{:S(2)}, u32[]{:S(2)}) collective-permute-start(f32[8,256]{1,0:T(8,128)S(1)} %get-tuple-element.19.rows), channel_id=1, source_target_pairs={{0,1},{1,0},{2,3},{3,2},{4,5},{5,4},{6,7},{7,6},{8,9},{9,8},{10,11... | collective-permute-start | bytes 24584 | tf_op jit(solution)/shard_map/ppermute | solution.py:89
  29.1 0.8 %collective-permute-done.11.arrived = f32[8,256]{1,0:T(8,128)S(1)} collective-permute-done((f32[8,256]{1,0:T(8,128)S(1)}, f32[8,256]{1,0:T(8,128)S(1)}, u32[]{:S(2)}, u32[]{:S(2)}) %collective-permute-start.11) | collective-permute-done | bytes 8224 | tf_op jit(solution)/shard_map/ppermute | solution.py:89
  29.9 1.4 %columns.2 = f32[8,256]{1,0:T(8,128)S(1)} custom-call(bf16[40,256,256]{2,1,0:T(8,128)(2,1)S(1)} %get-tuple-element.15.first, bf16[24,256,256]{2,1,0:T(8,128)(2,1)S(1)} %get-tuple-element.18.second, s32[42]{0:T(128)S(1)} %get-tuple-element.13.table.lists_first, s32[26]{0:T(128)S(1)} %get-tuple-element.16.table.lists_second, ...), custom_call_target="tpu_custom_call" | custom-call | tf_op jit(solution)/shard_map/columns/pallas_call | solution.py:365
  31.3 1.4 %collective-permute-start.14 = (f32[8,256]{1,0:T(8,128)S(1)}, f32[8,256]{1,0:T(8,128)S(1)}, u32[]{:S(2)}, u32[]{:S(2)}) collective-permute-start(f32[8,256]{1,0:T(8,128)S(1)} %columns.2), channel_id=1, source_target_pairs={{0,5},{1,4},{2,7},{3,6},{4,1},{5,0},{6,3},{7,2},{8,13},{9,12},{10,... | collective-permute-start | bytes 24584 | tf_op jit(solution)/shard_map/ppermute | solution.py:67
  32.8 1.8 %collective-permute-start.12 = (f32[8,256]{1,0:T(8,128)S(1)}, f32[8,256]{1,0:T(8,128)S(1)}, u32[]{:S(2)}, u32[]{:S(2)}) collective-permute-start(f32[8,256]{1,0:T(8,128)S(1)} %columns.2), channel_id=1, source_target_pairs={{0,6},{1,7},{2,4},{3,5},{4,2},{5,3},{6,0},{7,1},{8,14},{9,15},{10,... | collective-permute-start | bytes 24584 | tf_op jit(solution)/shard_map/ppermute | solution.py:67
  34.6 1.2 %collective-permute-done.13 = f32[8,256]{1,0:T(8,128)S(1)} collective-permute-done((f32[8,256]{1,0:T(8,128)S(1)}, f32[8,256]{1,0:T(8,128)S(1)}, u32[]{:S(2)}, u32[]{:S(2)}) %collective-permute-start.13) | collective-permute-done | bytes 8224 | tf_op jit(solution)/shard_map/ppermute | solution.py:67
  35.9 1.5 %collective-permute-done.12 = f32[8,256]{1,0:T(8,128)S(1)} collective-permute-done((f32[8,256]{1,0:T(8,128)S(1)}, f32[8,256]{1,0:T(8,128)S(1)}, u32[]{:S(2)}, u32[]{:S(2)}) %collective-permute-start.12) | collective-permute-done | bytes 8224 | tf_op jit(solution)/shard_map/ppermute | solution.py:67
  37.3 1.5 %collective-permute-start.15 = (f32[8,256]{1,0:T(8,128)S(1)}, f32[8,256]{1,0:T(8,128)S(1)}, u32[]{:S(2)}, u32[]{:S(2)}) collective-permute-start(f32[8,256]{1,0:T(8,128)S(1)} %add_add_fusion.columns), channel_id=1, source_target_pairs={{0,25},{1,24},{2,27},{3,26},{4,29},{5,28},{6,31},{7,30},{8,17},{9,... | collective-permute-start | bytes 24584 | tf_op jit(solution)/shard_map/ppermute | solution.py:84
  38.8 3.4 %collective-permute-done.15.wide = f32[8,256]{1,0:T(8,128)S(1)} collective-permute-done((f32[8,256]{1,0:T(8,128)S(1)}, f32[8,256]{1,0:T(8,128)S(1)}, u32[]{:S(2)}, u32[]{:S(2)}) %collective-permute-start.15) | collective-permute-done | bytes 8224 | tf_op jit(solution)/shard_map/ppermute | solution.py:84
  42.2 1.5 %rows.1 = f32[8,256]{1,0:T(8,128)S(1)} custom-call(bf16[40,256,256]{2,1,0:T(8,128)(2,1)S(1)} %get-tuple-element.15.first, bf16[24,256,256]{2,1,0:T(8,128)(2,1)S(1)} %get-tuple-element.18.second, s32[42]{0:T(128)S(1)} %get-tuple-element.13.table.lists_first, s32[26]{0:T(128)S(1)} %get-tuple-element.16.table.lists_second, f32[8,256]{1,0:T(8,128)S(1)} %add_add_fusion.columns, ...), custom_call_target="tpu_custom_call" | custom-call | tf_op jit(solution)/shard_map/rows/pallas_call | solution.py:356
  43.7 1.4 %collective-permute-start.17 = (f32[8,256]{1,0:T(8,128)S(1)}, f32[8,256]{1,0:T(8,128)S(1)}, u32[]{:S(2)}, u32[]{:S(2)}) collective-permute-start(f32[8,256]{1,0:T(8,128)S(1)} %rows.1), channel_id=1, source_target_pairs={{0,1},{1,0},{2,3},{3,2},{4,5},{5,4},{6,7},{7,6},{8,9},{9,8},{10,11... | collective-permute-start | bytes 24584 | tf_op jit(solution)/shard_map/ppermute | solution.py:89
  45.1 0.8 %collective-permute-done.17.arrived = f32[8,256]{1,0:T(8,128)S(1)} collective-permute-done((f32[8,256]{1,0:T(8,128)S(1)}, f32[8,256]{1,0:T(8,128)S(1)}, u32[]{:S(2)}, u32[]{:S(2)}) %collective-permute-start.17) | collective-permute-done | bytes 8224 | tf_op jit(solution)/shard_map/ppermute | solution.py:89
  45.9 1.4 %columns.3 = (f32[8,256]{1,0:T(8,128)S(1)}, f32[4,256]{1,0:T(4,128)S(1)}) custom-call(bf16[40,256,256]{2,1,0:T(8,128)(2,1)S(1)} %get-tuple-element.15.first, bf16[24,256,256]{2,1,0:T(8,128)(2,1)S(1)} %get-tuple-element.18.second, s32[42]{0:T(128)S(1)} %get-tuple-element.13.table.lists_first, s32[26]{0:T(128)S(1)} %get-tuple-element.16.table.lists_second, ...), custom_call_target="tpu_custom_call" | custom-call | tf_op jit(solution)/shard_map/columns/pallas_call | solution.py:365
  47.4 0.7 %collective-permute-start.18 = (f32[8,256]{1,0:T(8,128)S(1)}, f32[8,256]{1,0:T(8,128)S(1)}, u32[]{:S(2)}, u32[]{:S(2)}) collective-permute-start(f32[8,256]{1,0:T(8,128)S(1)} %get-tuple-element.21), channel_id=1, source_target_pairs={{0,5},{1,4},{2,7},{3,6},{4,1},{5,0},{6,3},{7,2},{8,13},{9,12},{10,... | collective-permute-start | bytes 24584 | tf_op jit(solution)/shard_map/ppermute | solution.py:67
  48.1 2.4 %collective-permute-done.18 = f32[8,256]{1,0:T(8,128)S(1)} collective-permute-done((f32[8,256]{1,0:T(8,128)S(1)}, f32[8,256]{1,0:T(8,128)S(1)}, u32[]{:S(2)}, u32[]{:S(2)}) %collective-permute-start.18) | collective-permute-done | bytes 8224 | tf_op jit(solution)/shard_map/ppermute | solution.py:67
  51.3 1.3 %collective-permute-start.19 = (f32[1,256]{1,0:T(1,128)S(1)}, f32[1,256]{1,0:T(1,128)S(1)}, u32[]{:S(2)}, u32[]{:S(2)}) collective-permute-start(f32[1,256]{1,0:T(1,128)S(1)} %get-tuple-element.22), channel_id=1, source_target_pairs={{0,3},{1,2},{2,1},{3,0},{4,7},{5,6},{6,5},{7,4},{8,11},{9,10},{10,... | collective-permute-start | bytes 3080 | tf_op jit(solution)/shard_map/ppermute | solution.py:67
  52.5 0.6 %copy.7 = f32[1,2,4,128]{3,1,2,0:T(2,128)} copy(f32[1,2,4,128]{3,2,1,0:T(4,128)S(1)} %bitcast.7) | data formatting | bytes 8192
  53.1 3.7 %collective-permute-done.21 = f32[1,256]{1,0:T(1,128)S(1)} collective-permute-done((f32[1,256]{1,0:T(1,128)S(1)}, f32[1,256]{1,0:T(1,128)S(1)}, u32[]{:S(2)}, u32[]{:S(2)}) %collective-permute-start.21) | collective-permute-done | bytes 1056 | tf_op jit(solution)/shard_map/ppermute | solution.py:67
  (25 shorter events, 3.2 us)
Async XLA Ops:
  0.6 19.4 %collective-permute-start = (bf16[1024,256]{1,0:T(8,128)(2,1)}, bf16[1024,256]{1,0:T(8,128)(2,1)S(1)}, u32[]{:S(2)}, u32[]{:S(2)}) collective-permute-start(bf16[1024,256]{1,0:T(8,128)(2,1)} %param.5), channel_id=1, source_target_pairs={{0,0},{1,1},{2,2},{3,3},{4,4},{5,5},{6,6},{7,7},{8,8},{9,9},{10,10... | collective-permute-start | bytes 1572872 | tf_op jit(solution)/shard_map/ppermute | solution.py:287
  1.7 19.8 %collective-permute-start.2 = (bf16[1024,256]{1,0:T(8,128)(2,1)}, bf16[1024,256]{1,0:T(8,128)(2,1)S(1)}, u32[]{:S(2)}, u32[]{:S(2)}) collective-permute-start(bf16[1024,256]{1,0:T(8,128)(2,1)} %param.5), channel_id=1, source_target_pairs={{0,1},{1,0},{2,3},{3,2},{4,5},{5,4},{6,7},{7,6},{8,9},{9,8},{10,11... | collective-permute-start | bytes 1572872 | tf_op jit(solution)/shard_map/ppermute | solution.py:89
  2.2 9.5 %collective-permute-start.1 = (bf16[256,256]{1,0:T(8,128)(2,1)}, bf16[256,256]{1,0:T(8,128)(2,1)S(1)}, u32[]{:S(2)}, u32[]{:S(2)}) collective-permute-start(bf16[256,256]{1,0:T(8,128)(2,1)} %param.6), channel_id=1, source_target_pairs={{0,0},{1,1},{2,2},{3,3},{4,4},{5,5},{6,6},{7,7},{8,8},{9,9},{10,10... | collective-permute-start | bytes 393224 | tf_op jit(solution)/shard_map/ppermute | solution.py:288
  3.1 10.0 %collective-permute-start.4 = (bf16[256,256]{1,0:T(8,128)(2,1)}, bf16[256,256]{1,0:T(8,128)(2,1)S(1)}, u32[]{:S(2)}, u32[]{:S(2)}) collective-permute-start(bf16[256,256]{1,0:T(8,128)(2,1)} %param.6), channel_id=1, source_target_pairs={{0,3},{1,2},{2,1},{3,0},{4,7},{5,6},{6,5},{7,4},{8,11},{9,10},{10,... | collective-permute-start | bytes 393224 | tf_op jit(solution)/shard_map/ppermute | solution.py:67
  7.1 1.2 %collective-permute-start.3 = (s32[1,33]{1,0:T(1,128)S(1)}, s32[1,33]{1,0:T(1,128)S(1)}, u32[]{:S(2)}, u32[]{:S(2)}) collective-permute-start(s32[1,33]{1,0:T(1,128)S(1)} %pad_add_fusion.mine), channel_id=1, source_target_pairs={{0,1},{1,0},{2,3},{3,2},{4,5},{5,4},{6,7},{7,6},{8,9},{9,8},{10,11... | collective-permute-start | bytes 404 | tf_op jit(solution)/shard_map/ppermute | solution.py:89
  8.3 7.2 %collective-permute-start.7 = (bf16[256,256]{1,0:T(8,128)(2,1)}, bf16[256,256]{1,0:T(8,128)(2,1)S(1)}, u32[]{:S(2)}, u32[]{:S(2)}) collective-permute-start(bf16[256,256]{1,0:T(8,128)(2,1)} %param.6), channel_id=1, source_target_pairs={{0,25},{1,24},{2,27},{3,26},{4,29},{5,28},{6,31},{7,30},{8,1},{9,0... | collective-permute-start | bytes 393224 | tf_op jit(solution)/shard_map/ppermute | solution.py:67
  11.6 11.7 %collective-permute-start.5 = (bf16[256,256]{1,0:T(8,128)(2,1)}, bf16[256,256]{1,0:T(8,128)(2,1)S(1)}, u32[]{:S(2)}, u32[]{:S(2)}) collective-permute-start(bf16[256,256]{1,0:T(8,128)(2,1)} %param.6), channel_id=1, source_target_pairs={{0,5},{1,4},{2,7},{3,6},{4,1},{5,0},{6,3},{7,2},{8,13},{9,12},{10,... | collective-permute-start | bytes 393224 | tf_op jit(solution)/shard_map/ppermute | solution.py:67
  13.1 10.2 %collective-permute-start.6 = (bf16[256,256]{1,0:T(8,128)(2,1)}, bf16[256,256]{1,0:T(8,128)(2,1)S(1)}, u32[]{:S(2)}, u32[]{:S(2)}) collective-permute-start(bf16[256,256]{1,0:T(8,128)(2,1)} %param.6), channel_id=1, source_target_pairs={{0,6},{1,7},{2,4},{3,5},{4,2},{5,3},{6,0},{7,1},{8,14},{9,15},{10,... | collective-permute-start | bytes 393224 | tf_op jit(solution)/shard_map/ppermute | solution.py:67
  15.5 9.9 %collective-permute-start.10 = (bf16[256,256]{1,0:T(8,128)(2,1)}, bf16[256,256]{1,0:T(8,128)(2,1)S(1)}, u32[]{:S(2)}, u32[]{:S(2)}) collective-permute-start(bf16[256,256]{1,0:T(8,128)(2,1)} %param.6), channel_id=1, source_target_pairs={{0,31},{1,30},{2,29},{3,28},{4,27},{5,26},{6,25},{7,24},{8,7},{9,6... | collective-permute-start | bytes 393224 | tf_op jit(solution)/shard_map/ppermute | solution.py:67
  20.0 5.9 %collective-permute-start.8 = (bf16[256,256]{1,0:T(8,128)(2,1)S(1)}, bf16[256,256]{1,0:T(8,128)(2,1)S(1)}, u32[]{:S(2)}, u32[]{:S(2)}) collective-permute-start(bf16[256,256]{1,0:T(8,128)(2,1)S(1)} %collective-permute-done.7.refs_3_), channel_id=1, source_target_pairs={{0,3},{1,2},{2,1},{3,0},{4,7},{5,6},{6,5},{7,4},{8,11},{9,10},{10,... | collective-permute-start | bytes 393224 | tf_op jit(solution)/shard_map/ppermute | solution.py:67
  21.5 5.4 %collective-permute-start.9 = (bf16[256,256]{1,0:T(8,128)(2,1)S(1)}, bf16[256,256]{1,0:T(8,128)(2,1)S(1)}, u32[]{:S(2)}, u32[]{:S(2)}) collective-permute-start(bf16[256,256]{1,0:T(8,128)(2,1)S(1)} %collective-permute-done.7.refs_3_), channel_id=1, source_target_pairs={{0,5},{1,4},{2,7},{3,6},{4,1},{5,0},{6,3},{7,2},{8,13},{9,12},{10,... | collective-permute-start | bytes 393224 | tf_op jit(solution)/shard_map/ppermute | solution.py:67
  28.5 1.4 %collective-permute-start.11 = (f32[8,256]{1,0:T(8,128)S(1)}, f32[8,256]{1,0:T(8,128)S(1)}, u32[]{:S(2)}, u32[]{:S(2)}) collective-permute-start(f32[8,256]{1,0:T(8,128)S(1)} %get-tuple-element.19.rows), channel_id=1, source_target_pairs={{0,1},{1,0},{2,3},{3,2},{4,5},{5,4},{6,7},{7,6},{8,9},{9,8},{10,11... | collective-permute-start | bytes 24584 | tf_op jit(solution)/shard_map/ppermute | solution.py:89
  31.3 3.3 %collective-permute-start.14 = (f32[8,256]{1,0:T(8,128)S(1)}, f32[8,256]{1,0:T(8,128)S(1)}, u32[]{:S(2)}, u32[]{:S(2)}) collective-permute-start(f32[8,256]{1,0:T(8,128)S(1)} %columns.2), channel_id=1, source_target_pairs={{0,5},{1,4},{2,7},{3,6},{4,1},{5,0},{6,3},{7,2},{8,13},{9,12},{10,... | collective-permute-start | bytes 24584 | tf_op jit(solution)/shard_map/ppermute | solution.py:67
  32.8 3.1 %collective-permute-start.13 = (f32[8,256]{1,0:T(8,128)S(1)}, f32[8,256]{1,0:T(8,128)S(1)}, u32[]{:S(2)}, u32[]{:S(2)}) collective-permute-start(f32[8,256]{1,0:T(8,128)S(1)} %columns.2), channel_id=1, source_target_pairs={{0,3},{1,2},{2,1},{3,0},{4,7},{5,6},{6,5},{7,4},{8,11},{9,10},{10,... | collective-permute-start | bytes 24584 | tf_op jit(solution)/shard_map/ppermute | solution.py:67
  32.8 4.5 %collective-permute-start.12 = (f32[8,256]{1,0:T(8,128)S(1)}, f32[8,256]{1,0:T(8,128)S(1)}, u32[]{:S(2)}, u32[]{:S(2)}) collective-permute-start(f32[8,256]{1,0:T(8,128)S(1)} %columns.2), channel_id=1, source_target_pairs={{0,6},{1,7},{2,4},{3,5},{4,2},{5,3},{6,0},{7,1},{8,14},{9,15},{10,... | collective-permute-start | bytes 24584 | tf_op jit(solution)/shard_map/ppermute | solution.py:67
  37.3 4.9 %collective-permute-start.15 = (f32[8,256]{1,0:T(8,128)S(1)}, f32[8,256]{1,0:T(8,128)S(1)}, u32[]{:S(2)}, u32[]{:S(2)}) collective-permute-start(f32[8,256]{1,0:T(8,128)S(1)} %add_add_fusion.columns), channel_id=1, source_target_pairs={{0,25},{1,24},{2,27},{3,26},{4,29},{5,28},{6,31},{7,30},{8,17},{9,... | collective-permute-start | bytes 24584 | tf_op jit(solution)/shard_map/ppermute | solution.py:84
  38.8 3.4 %collective-permute-start.16 = (f32[8,256]{1,0:T(8,128)S(1)}, f32[8,256]{1,0:T(8,128)S(1)}, u32[]{:S(2)}, u32[]{:S(2)}) collective-permute-start(f32[8,256]{1,0:T(8,128)S(1)} %add_add_fusion.columns), channel_id=1, source_target_pairs={{0,9},{1,8},{2,11},{3,10},{4,13},{5,12},{6,15},{7,14},{8,1},{9,0},... | collective-permute-start | bytes 24584 | tf_op jit(solution)/shard_map/ppermute | solution.py:84
  43.7 2.3 %collective-permute-start.17 = (f32[8,256]{1,0:T(8,128)S(1)}, f32[8,256]{1,0:T(8,128)S(1)}, u32[]{:S(2)}, u32[]{:S(2)}) collective-permute-start(f32[8,256]{1,0:T(8,128)S(1)} %rows.1), channel_id=1, source_target_pairs={{0,1},{1,0},{2,3},{3,2},{4,5},{5,4},{6,7},{7,6},{8,9},{9,8},{10,11... | collective-permute-start | bytes 24584 | tf_op jit(solution)/shard_map/ppermute | solution.py:89
  47.4 3.1 %collective-permute-start.18 = (f32[8,256]{1,0:T(8,128)S(1)}, f32[8,256]{1,0:T(8,128)S(1)}, u32[]{:S(2)}, u32[]{:S(2)}) collective-permute-start(f32[8,256]{1,0:T(8,128)S(1)} %get-tuple-element.21), channel_id=1, source_target_pairs={{0,5},{1,4},{2,7},{3,6},{4,1},{5,0},{6,3},{7,2},{8,13},{9,12},{10,... | collective-permute-start | bytes 24584 | tf_op jit(solution)/shard_map/ppermute | solution.py:67
  50.5 6.3 %collective-permute-start.21 = (f32[1,256]{1,0:T(1,128)S(1)}, f32[1,256]{1,0:T(1,128)S(1)}, u32[]{:S(2)}, u32[]{:S(2)}) collective-permute-start(f32[1,256]{1,0:T(1,128)S(1)} %get-tuple-element.23), channel_id=1, source_target_pairs={{0,10},{1,11},{2,8},{3,9},{4,14},{5,15},{6,12},{7,13},{8,18},{9,19... | collective-permute-start | bytes 3080 | tf_op jit(solution)/shard_map/ppermute | solution.py:67
  50.7 6.2 %collective-permute-start.20 = (f32[1,256]{1,0:T(1,128)S(1)}, f32[1,256]{1,0:T(1,128)S(1)}, u32[]{:S(2)}, u32[]{:S(2)}) collective-permute-start(f32[1,256]{1,0:T(1,128)S(1)} %get-tuple-element.24), channel_id=1, source_target_pairs={{0,9},{1,8},{2,11},{3,10},{4,13},{5,12},{6,15},{7,14},{8,17},{9,16... | collective-permute-start | bytes 3080 | tf_op jit(solution)/shard_map/ppermute | solution.py:67
  51.3 5.6 %collective-permute-start.19 = (f32[1,256]{1,0:T(1,128)S(1)}, f32[1,256]{1,0:T(1,128)S(1)}, u32[]{:S(2)}, u32[]{:S(2)}) collective-permute-start(f32[1,256]{1,0:T(1,128)S(1)} %get-tuple-element.22), channel_id=1, source_target_pairs={{0,3},{1,2},{2,1},{3,0},{4,7},{5,6},{6,5},{7,4},{8,11},{9,10},{10,... | collective-permute-start | bytes 3080 | tf_op jit(solution)/shard_map/ppermute | solution.py:67
